TPU v7x, 32 devices: a whole 2x2x4 slice. The times are simulated.
32 devices in a mesh: src: 4 (over y, x), rec: 4 (over z), freq: 2 (over core).
Axes of the slice: x: 2, y: 2, z: 4, core: 2. Of those that a mesh axis runs over, the one named last changes fastest.
Arguments:
- wave: bfloat16 [2, 4, 256, 2048], P(None, 'freq', 'src', 'rec'), may hold values from -6 to 6
- tap_table: float32 [2, 64, 4, 33], P(None, None, 'freq'), may hold values from -0.75 to 0.75
- src_index: int32 [3, 256], P(None, 'src'), may hold values from 0 to 63
- rec_index: int32 [3, 2048], P(None, 'rec'), may hold values from 0 to 63
- offset_bin: int32 [256, 2048], P('src', 'rec'), may hold values from 0 to 63
- bin_weight: float32 [3, 64], replicated, may hold values from 0.5 to 2
Outputs:
- final_wave: bfloat16 [2, 4, 256, 2048], P(None, 'freq', 'src', 'rec')
- image: float32 [256, 2048], P(('src', 'freq'), 'rec')
All inputs are finite; a program needn't handle non-finite values.
Results may differ from a plain program's by a relative error of at most 0.012.
Values may be sent and summed in bfloat16 or wider, within the bound.
No kernel may reach another device: no remote copies, remote signals or barrier semaphores. Data moves between devices by JAX's collectives and lax.ppermute only.
A program may use at most 64 MiB of HBM per device.

v0:
```python
import math

import jax
import jax.numpy as jnp
from jax import lax
from jax.sharding import PartitionSpec as P

TAPS = 33
DEPTHS = 3


def padded_2(cells, sides, width):
    for axis, dim in sides:
        count = lax.axis_size(axis)
        ends = count - 1
        head = lax.slice_in_dim(cells, 0, width, axis=dim)
        tail = lax.slice_in_dim(cells, cells.shape[dim] - width, cells.shape[dim], axis=dim)
        cells = jnp.concatenate(
            [
                lax.ppermute(tail, axis, [(i, (i + 1) % count) for i in range(ends)]),
                cells,
                lax.ppermute(head, axis, [((i + 1) % count, i) for i in range(ends)]),
            ],
            axis=dim,
        )
    return cells


def banded(tap_rows, block_size):
    leading = tap_rows.shape[:-2]
    tap_count = tap_rows.shape[-1]
    block_count = tap_rows.shape[-2] // block_size
    grouped = tap_rows.reshape(leading + (block_count, block_size, tap_count))
    padded = jnp.pad(grouped, [(0, 0)] * (len(leading) + 2) + [(0, block_size)])
    flattened = padded.reshape(leading + (block_count, block_size * (tap_count + block_size)))
    flattened = flattened[..., : block_size * (block_size + tap_count - 1)]
    return flattened.reshape(leading + (block_count, block_size, block_size + tap_count - 1))


def operator_pair(tap_rows, block_size):
    matrices = banded(tap_rows, block_size)
    real_part = jnp.concatenate([matrices[0], -matrices[1]], axis=-1)
    imag_part = jnp.concatenate([matrices[1], matrices[0]], axis=-1)
    return (real_part, imag_part)


def position_taps(table_bf, index_row):
    onehot = (index_row[:, None] == jnp.arange(table_bf.shape[1], dtype=jnp.int32)).astype(
        jnp.bfloat16
    )
    gathered = jnp.einsum("ln,cnfk->cflk", onehot, table_bf, preferred_element_type=jnp.float32)
    return gathered.astype(jnp.bfloat16)


def pair_weights(offset_bin, bin_weight):
    row_count, col_count = offset_bin.shape
    bin_count = bin_weight.shape[1]
    grouped = offset_bin.reshape(row_count // 8, 8, col_count)

    def one_block(bins_block):
        onehot = (bins_block[:, :, None] == jnp.arange(bin_count, dtype=jnp.int32)).astype(
            jnp.float32
        )
        return jnp.einsum("srh,zh->zsr", onehot, bin_weight, precision=lax.Precision.HIGHEST)

    blocks = lax.map(one_block, grouped)
    return jnp.moveaxis(blocks, 1, 0).reshape(bin_weight.shape[0], row_count, col_count)


def receiver_pass(padded, operators, block_size):
    block_count = operators[0].shape[1]
    extra = (block_count + 1) * block_size - padded.shape[3]
    widened = jnp.pad(padded, ((0, 0), (0, 0), (0, 0), (0, extra)))
    grouped = widened.reshape(padded.shape[:3] + (block_count + 1, block_size))
    windows = jnp.concatenate(
        [grouped[..., :block_count, :], grouped[..., 1:, : TAPS - 1]], axis=-1
    )
    stacked = jnp.concatenate([windows[0], windows[1]], axis=-1)
    real_out = jnp.einsum(
        "fsnj,fncj->fsnc", stacked, operators[0], preferred_element_type=jnp.float32
    )
    imag_out = jnp.einsum(
        "fsnj,fncj->fsnc", stacked, operators[1], preferred_element_type=jnp.float32
    )
    result = jnp.stack([real_out, imag_out]).reshape(padded.shape[:3] + (block_count * block_size,))
    return result.astype(jnp.bfloat16)


def source_pass(padded, operators, block_size):
    block_count = operators[0].shape[1]
    extra = (block_count + 1) * block_size - padded.shape[2]
    widened = jnp.pad(padded, ((0, 0), (0, 0), (0, extra), (0, 0)))
    grouped = widened.reshape(padded.shape[:2] + (block_count + 1, block_size, padded.shape[3]))
    windows = jnp.concatenate([grouped[:, :, :block_count], grouped[:, :, 1:, : TAPS - 1]], axis=3)
    stacked = jnp.concatenate([windows[0], windows[1]], axis=2)
    real_out = jnp.einsum(
        "fnjr,fncj->fncr", stacked, operators[0], preferred_element_type=jnp.float32
    )
    imag_out = jnp.einsum(
        "fnjr,fncj->fncr", stacked, operators[1], preferred_element_type=jnp.float32
    )
    result = jnp.stack([real_out, imag_out]).reshape(
        padded.shape[:2] + (block_count * block_size, padded.shape[3])
    )
    return result.astype(jnp.bfloat16)


def shards(wave, tap_table, src_index, rec_index, offset_bin, bin_weight):
    half_taps = TAPS // 2
    row_count = wave.shape[2]
    col_count = wave.shape[3]
    block_src = min(128, row_count)
    block_rec = min(128, col_count)
    table_bf = tap_table.astype(jnp.bfloat16)
    pair_weight = pair_weights(offset_bin, bin_weight)
    wavefield = wave
    image_part = jnp.zeros((row_count, col_count), jnp.float32)
    for depth_step in range(DEPTHS):
        rec_ops = operator_pair(position_taps(table_bf, rec_index[depth_step]), block_rec)
        src_ops = operator_pair(position_taps(table_bf, src_index[depth_step]), block_src)
        framed = padded_2(wavefield, (("rec", 3),), half_taps)
        swept = padded_2(receiver_pass(framed, rec_ops, block_rec), (("src", 2),), half_taps)
        wavefield = source_pass(swept, src_ops, block_src)
        image_part = image_part + pair_weight[depth_step] * jnp.sum(
            wavefield[0].astype(jnp.float32), axis=0
        )
    total = lax.psum_scatter(
        image_part.astype(jnp.bfloat16), "freq", scatter_dimension=0, tiled=True
    ).astype(jnp.float32)
    scale = 1.0 / math.sqrt(wave.shape[1] * lax.axis_size("freq") * DEPTHS)
    return (wavefield, total * scale)


def solution(mesh):
    placed = (
        P(None, "freq", "src", "rec"),
        P(None, None, "freq", None),
        P(None, "src"),
        P(None, "rec"),
        P("src", "rec"),
        P(),
    )
    return jax.shard_map(
        shards,
        mesh=mesh,
        in_specs=placed,
        out_specs=(P(None, "freq", "src", "rec"), P(("src", "freq"), "rec")),
        check_vma=False,
    )
```

profile of v0, /device:TPU:9, one launch (start us, length us, event | category | flops | bytes accessed | tf_op | source)
XLA Modules:
  0.0 117.0 jit_solution(4522201817802059259)
XLA Ops:
  7.2 1.6 %fusion.138 = (bf16[2,2,64,16]{3,2,1,0:T(8,128)(2,1)}, bf16[2,2,64,16]{3,2,1,0:T(8,128)(2,1)S(1)}) fusion(bf16[2,2,64,512]{3,2,1,0:T(8,128)(2,1)} %param.8), kind=kLoop, calls=%fused_computation.219 | loop fusion | bytes 32768 | tf_op jit(solution)/shard_map/slice | solution.py:17
  8.8 3.2 %collective-permute-start = (bf16[2,2,64,16]{3,2,1,0:T(8,128)(2,1)}, bf16[2,2,64,16]{3,2,1,0:T(8,128)(2,1)}, u32[]{:S(2)}, u32[]{:S(2)}) collective-permute-start(bf16[2,2,64,16]{3,2,1,0:T(8,128)(2,1)} %get-tuple-element.64), channel_id=1, source_target_pairs={{0,2},{2,4},{4,6},{1,3},{3,5},{5,7},{8,10},{10,12},{12,14},{9,11},... | collective-permute-start | bytes 24584 | tf_op jit(solution)/shard_map/ppermute | solution.py:20
  12.0 2.7 %collective-permute-start.1 = (bf16[2,2,64,16]{3,2,1,0:T(8,128)(2,1)S(1)}, bf16[2,2,64,16]{3,2,1,0:T(8,128)(2,1)}, u32[]{:S(2)}, u32[]{:S(2)}) collective-permute-start(bf16[2,2,64,16]{3,2,1,0:T(8,128)(2,1)S(1)} %get-tuple-element.65), channel_id=1, source_target_pairs={{2,0},{4,2},{6,4},{3,1},{5,3},{7,5},{10,8},{12,10},{14,12},{11,9},... | collective-permute-start | bytes 24584 | tf_op jit(solution)/shard_map/ppermute | solution.py:22
  17.1 1.6 %reshape.234 = bf16[2,2,4,20608]{3,2,1,0:T(4,128)(2,1)S(1)} reshape(bf16[2,2,4,128,161]{4,3,2,1,0:T(8,128)(2,1)S(1)} %pad.45.clone) | data formatting | bytes 1318912 | tf_op jit(solution)/shard_map/reshape | solution.py:35
  18.7 1.0 fusion.129
  21.0 1.6 %reshape.229 = bf16[2,2,4,20608]{3,2,1,0:T(4,128)(2,1)S(1)} reshape(bf16[2,2,4,128,161]{4,3,2,1,0:T(8,128)(2,1)S(1)} %pad.43.clone) | data formatting | bytes 1318912 | tf_op jit(solution)/shard_map/reshape | solution.py:35
  23.5 1.6 %reshape.224 = bf16[2,2,4,20608]{3,2,1,0:T(4,128)(2,1)S(1)} reshape(bf16[2,2,4,128,161]{4,3,2,1,0:T(8,128)(2,1)S(1)} %pad.41.clone) | data formatting | bytes 1318912 | tf_op jit(solution)/shard_map/reshape | solution.py:35
  25.8 14.2 %while.10 = (s32[]{:T(128)}, f32[8,3,8,512]{3,1,2,0:T(4,128)}, s32[8,8,512]{2,1,0:T(8,128)}, f32[3,64]{1,0:T(4,128)S(1)}, s32[]{:T(128)}) while((s32[]{:T(128)}, f32[8,3,8,512]{3,1,2,0:T(4,128)}, s32[8,8,512]{2,1,0:T(8,128)}, f32[3,64]{1,0:T(4,128)S(1)}, s32[]{:T(128)}) %tuple.55), condition=%wide.region_1.2_spmd, body=%wide.region_0.1_spmd.sunk | while | flops 9699330 | bytes 116033 | solution.py:66
  26.5 1.1 fusion.146
  28.3 1.1 fusion.146
  30.1 1.1 fusion.146
  31.8 1.0 fusion.146
  33.6 1.1 fusion.146
  35.4 1.1 fusion.146
  37.2 1.1 fusion.146
  38.9 1.1 fusion.146
  42.9 1.1 fusion.68
  46.5 3.1 %collective-permute-start.2 = (bf16[2,2,16,512]{3,2,1,0:T(8,128)(2,1)S(1)}, bf16[2,2,16,512]{3,2,1,0:T(8,128)(2,1)S(1)}, u32[]{:S(2)}, u32[]{:S(2)}) collective-permute-start(bf16[2,2,16,512]{3,2,1,0:T(8,128)(2,1)S(1)} %get-tuple-element.62), channel_id=1, source_target_pairs={{0,8},{8,16},{16,24},{1,9},{9,17},{17,25},{2,10},{10,18},{18,26},{... | collective-permute-start | bytes 196616 | tf_op jit(solution)/shard_map/ppermute | solution.py:20
  49.6 1.5 %collective-permute-start.3 = (bf16[2,2,16,512]{3,2,1,0:T(8,128)(2,1)S(1)}, bf16[2,2,16,512]{3,2,1,0:T(8,128)(2,1)S(1)}, u32[]{:S(2)}, u32[]{:S(2)}) collective-permute-start(bf16[2,2,16,512]{3,2,1,0:T(8,128)(2,1)S(1)} %get-tuple-element.63), channel_id=1, source_target_pairs={{8,0},{16,8},{24,16},{9,1},{17,9},{25,17},{10,2},{18,10},{26,18},{... | collective-permute-start | bytes 196616 | tf_op jit(solution)/shard_map/ppermute | solution.py:22
  51.7 3.2 %collective-permute-done.3 = bf16[2,2,16,512]{3,2,1,0:T(8,128)(2,1)S(1)} collective-permute-done((bf16[2,2,16,512]{3,2,1,0:T(8,128)(2,1)S(1)}, bf16[2,2,16,512]{3,2,1,0:T(8,128)(2,1)S(1)}, u32[]{:S(2)}, u32[]{:S(2)}) %collective-permute-start.3) | collective-permute-done | bytes 65568 | tf_op jit(solution)/shard_map/ppermute | solution.py:22
  55.6 2.6 %collective-permute-start.4 = (bf16[2,2,64,16]{3,2,1,0:T(8,128)(2,1)S(1)}, bf16[2,2,64,16]{3,2,1,0:T(8,128)(2,1)S(1)}, u32[]{:S(2)}, u32[]{:S(2)}) collective-permute-start(bf16[2,2,64,16]{3,2,1,0:T(8,128)(2,1)S(1)} %get-tuple-element.60), channel_id=1, source_target_pairs={{0,2},{2,4},{4,6},{1,3},{3,5},{5,7},{8,10},{10,12},{12,14},{9,11},... | collective-permute-start | bytes 24584 | tf_op jit(solution)/shard_map/ppermute | solution.py:20
  58.2 2.7 %collective-permute-start.5 = (bf16[2,2,64,16]{3,2,1,0:T(8,128)(2,1)S(1)}, bf16[2,2,64,16]{3,2,1,0:T(8,128)(2,1)S(1)}, u32[]{:S(2)}, u32[]{:S(2)}) collective-permute-start(bf16[2,2,64,16]{3,2,1,0:T(8,128)(2,1)S(1)} %get-tuple-element.61), channel_id=1, source_target_pairs={{2,0},{4,2},{6,4},{3,1},{5,3},{7,5},{10,8},{12,10},{14,12},{11,9},... | collective-permute-start | bytes 24584 | tf_op jit(solution)/shard_map/ppermute | solution.py:22
  65.9 3.9 %collective-permute-start.6 = (bf16[2,2,16,512]{3,2,1,0:T(8,128)(2,1)S(1)}, bf16[2,2,16,512]{3,2,1,0:T(8,128)(2,1)S(1)}, u32[]{:S(2)}, u32[]{:S(2)}) collective-permute-start(bf16[2,2,16,512]{3,2,1,0:T(8,128)(2,1)S(1)} %get-tuple-element.58), channel_id=1, source_target_pairs={{0,8},{8,16},{16,24},{1,9},{9,17},{17,25},{2,10},{10,18},{18,26},{... | collective-permute-start | bytes 196616 | tf_op jit(solution)/shard_map/ppermute | solution.py:20
  69.9 1.3 %collective-permute-start.7 = (bf16[2,2,16,512]{3,2,1,0:T(8,128)(2,1)S(1)}, bf16[2,2,16,512]{3,2,1,0:T(8,128)(2,1)S(1)}, u32[]{:S(2)}, u32[]{:S(2)}) collective-permute-start(bf16[2,2,16,512]{3,2,1,0:T(8,128)(2,1)S(1)} %get-tuple-element.59), channel_id=1, source_target_pairs={{8,0},{16,8},{24,16},{9,1},{17,9},{25,17},{10,2},{18,10},{26,18},{... | collective-permute-start | bytes 196616 | tf_op jit(solution)/shard_map/ppermute | solution.py:22
  71.8 3.1 %collective-permute-done.7 = bf16[2,2,16,512]{3,2,1,0:T(8,128)(2,1)S(1)} collective-permute-done((bf16[2,2,16,512]{3,2,1,0:T(8,128)(2,1)S(1)}, bf16[2,2,16,512]{3,2,1,0:T(8,128)(2,1)S(1)}, u32[]{:S(2)}, u32[]{:S(2)}) %collective-permute-start.7) | collective-permute-done | bytes 65568 | tf_op jit(solution)/shard_map/ppermute | solution.py:22
  75.6 3.1 %collective-permute-start.8 = (bf16[2,2,64,16]{3,2,1,0:T(8,128)(2,1)S(1)}, bf16[2,2,64,16]{3,2,1,0:T(8,128)(2,1)S(1)}, u32[]{:S(2)}, u32[]{:S(2)}) collective-permute-start(bf16[2,2,64,16]{3,2,1,0:T(8,128)(2,1)S(1)} %get-tuple-element.56), channel_id=1, source_target_pairs={{0,2},{2,4},{4,6},{1,3},{3,5},{5,7},{8,10},{10,12},{12,14},{9,11},... | collective-permute-start | bytes 24584 | tf_op jit(solution)/shard_map/ppermute | solution.py:20
  78.7 2.2 %collective-permute-start.9 = (bf16[2,2,64,16]{3,2,1,0:T(8,128)(2,1)S(1)}, bf16[2,2,64,16]{3,2,1,0:T(8,128)(2,1)S(1)}, u32[]{:S(2)}, u32[]{:S(2)}) collective-permute-start(bf16[2,2,64,16]{3,2,1,0:T(8,128)(2,1)S(1)} %get-tuple-element.57), channel_id=1, source_target_pairs={{2,0},{4,2},{6,4},{3,1},{5,3},{7,5},{10,8},{12,10},{14,12},{11,9},... | collective-permute-start | bytes 24584 | tf_op jit(solution)/shard_map/ppermute | solution.py:22
  85.8 3.8 %collective-permute-start.10 = (bf16[2,2,16,512]{3,2,1,0:T(8,128)(2,1)S(1)}, bf16[2,2,16,512]{3,2,1,0:T(8,128)(2,1)S(1)}, u32[]{:S(2)}, u32[]{:S(2)}) collective-permute-start(bf16[2,2,16,512]{3,2,1,0:T(8,128)(2,1)S(1)} %get-tuple-element.54), channel_id=1, source_target_pairs={{0,8},{8,16},{16,24},{1,9},{9,17},{17,25},{2,10},{10,18},{18,26},{... | collective-permute-start | bytes 196616 | tf_op jit(solution)/shard_map/ppermute | solution.py:20
  89.7 1.3 %collective-permute-start.11 = (bf16[2,2,16,512]{3,2,1,0:T(8,128)(2,1)S(1)}, bf16[2,2,16,512]{3,2,1,0:T(8,128)(2,1)S(1)}, u32[]{:S(2)}, u32[]{:S(2)}) collective-permute-start(bf16[2,2,16,512]{3,2,1,0:T(8,128)(2,1)S(1)} %get-tuple-element.55), channel_id=1, source_target_pairs={{8,0},{16,8},{24,16},{9,1},{17,9},{25,17},{10,2},{18,10},{26,18},{... | collective-permute-start | bytes 196616 | tf_op jit(solution)/shard_map/ppermute | solution.py:22
  91.6 3.1 %collective-permute-done.11 = bf16[2,2,16,512]{3,2,1,0:T(8,128)(2,1)S(1)} collective-permute-done((bf16[2,2,16,512]{3,2,1,0:T(8,128)(2,1)S(1)}, bf16[2,2,16,512]{3,2,1,0:T(8,128)(2,1)S(1)}, u32[]{:S(2)}, u32[]{:S(2)}) %collective-permute-start.11) | collective-permute-done | bytes 65568 | tf_op jit(solution)/shard_map/ppermute | solution.py:22
  96.7 12.0 %reduce-scatter.2.cloned.1.call-done = bf16[32,512]{1,0:T(8,128)(2,1)} async-done(((bf16[64,512]{1,0:T(8,128)(2,1)}), bf16[32,512]{1,0:T(8,128)(2,1)}) %reduce-scatter.2.cloned.1.call-update) | async-done | bytes 32784 | tf_op jit(solution)/shard_map/reduce_scatter | solution.py:127
  108.8 1.4 %convert_multiply_fusion = f32[32,512]{1,0:T(8,128)} fusion(bf16[32,512]{1,0:T(8,128)(2,1)} %reduce-scatter.2.cloned.1.call-done), kind=kLoop, calls=%fused_computation.170 | loop fusion | flops 32768 | bytes 98304 | tf_op jit(solution)/shard_map/mul | solution.py:131
  (157 shorter events, 30.9 us)
Async XLA Ops:
  7.2 101.6 %reduce-scatter.2.cloned.1.call-start = ((), (), s32[]{:S(2)}) async-start(), calls=%async_computation.1 | async-start | bytes 98304 | tf_op jit(solution)/shard_map/reduce_scatter | solution.py:127
  8.8 34.0 %collective-permute-start = (bf16[2,2,64,16]{3,2,1,0:T(8,128)(2,1)}, bf16[2,2,64,16]{3,2,1,0:T(8,128)(2,1)}, u32[]{:S(2)}, u32[]{:S(2)}) collective-permute-start(bf16[2,2,64,16]{3,2,1,0:T(8,128)(2,1)} %get-tuple-element.64), channel_id=1, source_target_pairs={{0,2},{2,4},{4,6},{1,3},{3,5},{5,7},{8,10},{10,12},{12,14},{9,11},... | collective-permute-start | bytes 24584 | tf_op jit(solution)/shard_map/ppermute | solution.py:20
  12.0 30.8 %collective-permute-start.1 = (bf16[2,2,64,16]{3,2,1,0:T(8,128)(2,1)S(1)}, bf16[2,2,64,16]{3,2,1,0:T(8,128)(2,1)}, u32[]{:S(2)}, u32[]{:S(2)}) collective-permute-start(bf16[2,2,64,16]{3,2,1,0:T(8,128)(2,1)S(1)} %get-tuple-element.65), channel_id=1, source_target_pairs={{2,0},{4,2},{6,4},{3,1},{5,3},{7,5},{10,8},{12,10},{14,12},{11,9},... | collective-permute-start | bytes 24584 | tf_op jit(solution)/shard_map/ppermute | solution.py:22
  18.7 1.0 copy-start.4
  25.1 0.7 copy-start.5
  25.4 14.7 %copy-start = (bf16[1,2,4,20480]{3,2,1,0:T(4,128)(2,1)S(1)}, bf16[1,2,4,20480]{3,2,1,0:T(4,128)(2,1)}, u32[]{:S(2)}) copy-start(bf16[1,2,4,20480]{3,2,1,0:T(4,128)(2,1)} %get-tuple-element.34) | copy-start | bytes 983044
  41.7 1.1 copy-start.1
  44.8 1.0 copy-start.2
  46.5 5.2 %collective-permute-start.2 = (bf16[2,2,16,512]{3,2,1,0:T(8,128)(2,1)S(1)}, bf16[2,2,16,512]{3,2,1,0:T(8,128)(2,1)S(1)}, u32[]{:S(2)}, u32[]{:S(2)}) collective-permute-start(bf16[2,2,16,512]{3,2,1,0:T(8,128)(2,1)S(1)} %get-tuple-element.62), channel_id=1, source_target_pairs={{0,8},{8,16},{16,24},{1,9},{9,17},{17,25},{2,10},{10,18},{18,26},{... | collective-permute-start | bytes 196616 | tf_op jit(solution)/shard_map/ppermute | solution.py:20
  49.6 5.2 %collective-permute-start.3 = (bf16[2,2,16,512]{3,2,1,0:T(8,128)(2,1)S(1)}, bf16[2,2,16,512]{3,2,1,0:T(8,128)(2,1)S(1)}, u32[]{:S(2)}, u32[]{:S(2)}) collective-permute-start(bf16[2,2,16,512]{3,2,1,0:T(8,128)(2,1)S(1)} %get-tuple-element.63), channel_id=1, source_target_pairs={{8,0},{16,8},{24,16},{9,1},{17,9},{25,17},{10,2},{18,10},{26,18},{... | collective-permute-start | bytes 196616 | tf_op jit(solution)/shard_map/ppermute | solution.py:22
  55.6 7.4 %collective-permute-start.4 = (bf16[2,2,64,16]{3,2,1,0:T(8,128)(2,1)S(1)}, bf16[2,2,64,16]{3,2,1,0:T(8,128)(2,1)S(1)}, u32[]{:S(2)}, u32[]{:S(2)}) collective-permute-start(bf16[2,2,64,16]{3,2,1,0:T(8,128)(2,1)S(1)} %get-tuple-element.60), channel_id=1, source_target_pairs={{0,2},{2,4},{4,6},{1,3},{3,5},{5,7},{8,10},{10,12},{12,14},{9,11},... | collective-permute-start | bytes 24584 | tf_op jit(solution)/shard_map/ppermute | solution.py:20
  58.2 5.6 %collective-permute-start.5 = (bf16[2,2,64,16]{3,2,1,0:T(8,128)(2,1)S(1)}, bf16[2,2,64,16]{3,2,1,0:T(8,128)(2,1)S(1)}, u32[]{:S(2)}, u32[]{:S(2)}) collective-permute-start(bf16[2,2,64,16]{3,2,1,0:T(8,128)(2,1)S(1)} %get-tuple-element.61), channel_id=1, source_target_pairs={{2,0},{4,2},{6,4},{3,1},{5,3},{7,5},{10,8},{12,10},{14,12},{11,9},... | collective-permute-start | bytes 24584 | tf_op jit(solution)/shard_map/ppermute | solution.py:22
  65.9 5.8 %collective-permute-start.6 = (bf16[2,2,16,512]{3,2,1,0:T(8,128)(2,1)S(1)}, bf16[2,2,16,512]{3,2,1,0:T(8,128)(2,1)S(1)}, u32[]{:S(2)}, u32[]{:S(2)}) collective-permute-start(bf16[2,2,16,512]{3,2,1,0:T(8,128)(2,1)S(1)} %get-tuple-element.58), channel_id=1, source_target_pairs={{0,8},{8,16},{16,24},{1,9},{9,17},{17,25},{2,10},{10,18},{18,26},{... | collective-permute-start | bytes 196616 | tf_op jit(solution)/shard_map/ppermute | solution.py:20
  69.9 5.0 %collective-permute-start.7 = (bf16[2,2,16,512]{3,2,1,0:T(8,128)(2,1)S(1)}, bf16[2,2,16,512]{3,2,1,0:T(8,128)(2,1)S(1)}, u32[]{:S(2)}, u32[]{:S(2)}) collective-permute-start(bf16[2,2,16,512]{3,2,1,0:T(8,128)(2,1)S(1)} %get-tuple-element.59), channel_id=1, source_target_pairs={{8,0},{16,8},{24,16},{9,1},{17,9},{25,17},{10,2},{18,10},{26,18},{... | collective-permute-start | bytes 196616 | tf_op jit(solution)/shard_map/ppermute | solution.py:22
  75.6 7.2 %collective-permute-start.8 = (bf16[2,2,64,16]{3,2,1,0:T(8,128)(2,1)S(1)}, bf16[2,2,64,16]{3,2,1,0:T(8,128)(2,1)S(1)}, u32[]{:S(2)}, u32[]{:S(2)}) collective-permute-start(bf16[2,2,64,16]{3,2,1,0:T(8,128)(2,1)S(1)} %get-tuple-element.56), channel_id=1, source_target_pairs={{0,2},{2,4},{4,6},{1,3},{3,5},{5,7},{8,10},{10,12},{12,14},{9,11},... | collective-permute-start | bytes 24584 | tf_op jit(solution)/shard_map/ppermute | solution.py:20
  78.7 5.0 %collective-permute-start.9 = (bf16[2,2,64,16]{3,2,1,0:T(8,128)(2,1)S(1)}, bf16[2,2,64,16]{3,2,1,0:T(8,128)(2,1)S(1)}, u32[]{:S(2)}, u32[]{:S(2)}) collective-permute-start(bf16[2,2,64,16]{3,2,1,0:T(8,128)(2,1)S(1)} %get-tuple-element.57), channel_id=1, source_target_pairs={{2,0},{4,2},{6,4},{3,1},{5,3},{7,5},{10,8},{12,10},{14,12},{11,9},... | collective-permute-start | bytes 24584 | tf_op jit(solution)/shard_map/ppermute | solution.py:22
  85.6 5.4 %copy-start.3 = (f32[8,3,8,512]{3,1,2,0:T(4,128)S(1)}, f32[8,3,8,512]{3,1,2,0:T(4,128)}, u32[]{:S(2)}) copy-start(f32[8,3,8,512]{3,1,2,0:T(4,128)} %get-tuple-element.24) | copy-start | bytes 1179652
  85.8 5.7 %collective-permute-start.10 = (bf16[2,2,16,512]{3,2,1,0:T(8,128)(2,1)S(1)}, bf16[2,2,16,512]{3,2,1,0:T(8,128)(2,1)S(1)}, u32[]{:S(2)}, u32[]{:S(2)}) collective-permute-start(bf16[2,2,16,512]{3,2,1,0:T(8,128)(2,1)S(1)} %get-tuple-element.54), channel_id=1, source_target_pairs={{0,8},{8,16},{16,24},{1,9},{9,17},{17,25},{2,10},{10,18},{18,26},{... | collective-permute-start | bytes 196616 | tf_op jit(solution)/shard_map/ppermute | solution.py:20
  89.7 5.0 %collective-permute-start.11 = (bf16[2,2,16,512]{3,2,1,0:T(8,128)(2,1)S(1)}, bf16[2,2,16,512]{3,2,1,0:T(8,128)(2,1)S(1)}, u32[]{:S(2)}, u32[]{:S(2)}) collective-permute-start(bf16[2,2,16,512]{3,2,1,0:T(8,128)(2,1)S(1)} %get-tuple-element.55), channel_id=1, source_target_pairs={{8,0},{16,8},{24,16},{9,1},{17,9},{25,17},{10,2},{18,10},{26,18},{... | collective-permute-start | bytes 196616 | tf_op jit(solution)/shard_map/ppermute | solution.py:22
Sparse Core Ops, SparseCore 0:
  95.9 12.8 reduce-scatter.1
where the time goes:
time: 119 us; the launch traced here: 117 us
  starting transfers between devices  31.4 us (26%)
  local copies, waits for them, and re-layouts  28 us (24%)
  waiting for transfers between devices  23.1 us (19%)
  between operations  15 us (13%)
  matrix products  13.1 us (11%)
  other arithmetic  6.36 us (5%)
    ppermute x6, starting transfers between devices, padded_2(): lax.ppermute(tail, axis, [(i, (i + 1) % count) for i in range(ends)])  19.7 us
    reduce_scatter x1, waiting for transfers between devices, shards(): lax.psum_scatter(image_part.astype(jnp.bfloat16), 'freq', scatter_dimensi...  12 us
    ppermute x6, starting transfers between devices, padded_2(): lax.ppermute(head, axis, [((i + 1) % count, i) for i in range(ends)])  11.7 us
    ppermute x6, waiting for transfers between devices, padded_2(): lax.ppermute(head, axis, [((i + 1) % count, i) for i in range(ends)])  11 us
    dot_general x8, matrix products, one_block(): jnp.einsum('srh,zh->zsr', onehot, bin_weight, precision=lax.Precision.HIG...  8.44 us
    squeeze x18, local copies, waits for them, and re-layouts, operator_pair(): real_part = jnp.concatenate([matrices[0], -matrices[1]], axis=-1)  5.86 us
    eq x8, local copies, waits for them, and re-layouts, one_block(): bins_block[:, :, None] == jnp.arange(bin_count, dtype=jnp.int32)  5.75 us
    reshape x6, local copies, waits for them, and re-layouts, banded(): padded.reshape(leading + (block_count, block_size * (tap_count + block_si...  5.41 us
  transfers between devices with their start and end apart: 13, of which 6 were waited for; matrix products, arithmetic and copies ran while one was open for 29% of the time, Pallas kernels for 0%

commit v1 on v0

v1 whole, which is shorter than its diff:
```python
import functools
import math

import jax
import jax.numpy as jnp
from jax import lax
from jax.experimental import pallas as pl
from jax.experimental.pallas import tpu as pltpu
from jax.sharding import PartitionSpec as P

TAPS = 33
DEPTHS = 3
HALF = TAPS // 2
HALO = DEPTHS * HALF
LANES = 128
SPAN = 2 * LANES
IDX_ROWS = 16
BF = jnp.bfloat16
F32 = jnp.float32


def pairs_of(axis, odd):
    count, groups = lax.axis_size(axis), lax.axis_size("freq")
    pairs, alone = [], list(range(count))
    for i in range(odd, count - 1, 2):
        alone.remove(i)
        alone.remove(i + 1)
        for g in range(groups):
            pairs += [(i * groups + g, (i + 1) * groups + g), ((i + 1) * groups + g, i * groups + g)]
    for i in alone:
        for g in range(0, groups - 1, 2):
            pairs += [(i * groups + g, i * groups + g + 1), (i * groups + g + 1, i * groups + g)]
    return pairs


def swap(cells, axis, odd):
    return lax.ppermute(cells, (axis, "freq"), pairs_of(axis, odd))


def parity(axis):
    return lax.rem(lax.axis_index(axis), 2)


def has_left(axis):
    return lax.axis_index(axis) > 0


def has_right(axis):
    return lax.axis_index(axis) < lax.axis_size(axis) - 1


def lane_of(shape):
    return lax.broadcasted_iota(jnp.int32, shape, len(shape) - 1)


def shifted(cells, amount):
    amount = amount % LANES
    return pltpu.roll(cells, amount, 1) if amount else cells


def left_right(a_ref, b_ref, axis):
    even = parity(axis) == 0
    a, b = a_ref[...], b_ref[...]
    return jnp.where(even, b, a), jnp.where(even, a, b)


def pack_kernel(x_ref, ridx_ref, sa_ref, sb_ref, ra_ref, rb_ref):
    planes, rows, cols = x_ref.shape
    even = parity("src") == 0
    low = rows - HALO
    at = pl.multiple_of(jnp.where(even, low, 0), 16)
    other = pl.multiple_of(jnp.where(even, 0, low), 16)
    for p in range(planes):
        sa_ref[p * HALO:(p + 1) * HALO, :] = x_ref[p, pl.ds(at, HALO), :]
        sb_ref[p * HALO:(p + 1) * HALO, :] = x_ref[p, pl.ds(other, HALO), :]
    even = parity("rec") == 0
    tail_at = cols - LANES
    for p in range(planes):
        head, tail = x_ref[p, :, 0:LANES], x_ref[p, :, tail_at:cols]
        ra_ref[p * rows:(p + 1) * rows, :] = jnp.where(even, tail, head)
        rb_ref[p * rows:(p + 1) * rows, :] = jnp.where(even, head, tail)
    base = planes * rows
    head = ridx_ref[:, 0:LANES].astype(F32).astype(BF)
    tail = ridx_ref[:, tail_at:cols].astype(F32).astype(BF)
    for ref in (ra_ref, rb_ref):
        ref[base:base + IDX_ROWS, :] = jnp.zeros((IDX_ROWS, LANES), BF)
    ra_ref[base:base + DEPTHS, :] = jnp.where(even, tail, head)
    rb_ref[base:base + DEPTHS, :] = jnp.where(even, head, tail)


def corner_kernel(rows, ra_ref, rb_ref, sidx_ref, ca_ref, cb_ref, edge_ref):
    left, right = left_right(ra_ref, rb_ref, "rec")
    total = (left.shape[0] - IDX_ROWS)
    planes = total // rows
    lane = lane_of((total, LANES))
    left = shifted(left[:total].astype(F32), HALO)
    right = shifted(right[:total].astype(F32), HALO)
    in_left = (lane < HALO) & has_left("rec")
    in_right = (lane >= HALO) & (lane < 2 * HALO) & has_right("rec")
    edge_ref[...] = jnp.where(in_left, left, jnp.where(in_right, right, 0.0)).astype(BF)
    even = parity("src") == 0
    low = rows - HALO
    at = jnp.where(even, low, 0)
    other = jnp.where(even, 0, low)
    for p in range(planes):
        ca_ref[p * HALO:(p + 1) * HALO, :] = edge_ref[pl.ds(pl.multiple_of(p * rows + at, 16), HALO), :]
        cb_ref[p * HALO:(p + 1) * HALO, :] = edge_ref[pl.ds(pl.multiple_of(p * rows + other, 16), HALO), :]
    base = planes * HALO
    idx = sidx_ref[...].astype(F32).astype(BF)
    for ref in (ca_ref, cb_ref):
        ref[base:base + IDX_ROWS, :] = jnp.zeros((IDX_ROWS, LANES), BF)
        ref[base:base + DEPTHS, 0:rows] = idx


def wide_tiles(own, left, right, amount, fill):
    count = len(own)
    lane = lane_of(own[0].shape)
    moved = [shifted(t, amount) for t in own]
    if amount == 0:
        return moved
    tiles = [jnp.where(lane < amount, shifted(left, amount), moved[0])]
    for t in range(1, count):
        tiles.append(jnp.where(lane < amount, moved[t - 1], moved[t]))
    last = jnp.where(lane < 2 * amount, shifted(right, amount), fill)
    tiles.append(jnp.where(lane < amount, moved[count - 1], last))
    return tiles


def bands(idx_row, table, entries):
    onehot = (lax.broadcasted_iota(jnp.int32, (entries, LANES), 0) == idx_row).astype(F32).astype(BF)
    taps = lax.dot_general(onehot, table, (((0,), (0,)), ((), ())), preferred_element_type=F32)
    out = lax.broadcasted_iota(jnp.int32, (LANES, LANES), 0)
    lane = lane_of((LANES, LANES))
    found = []
    for part in range(taps.shape[1] // LANES):
        skewed = pltpu.roll(taps[:, part * LANES:(part + 1) * LANES], 0, 1, stride=1, stride_axis=0)
        first = jnp.where(lane >= out, skewed, 0.0).astype(BF)
        second = jnp.where(lane < out, skewed, 0.0).astype(BF)
        found.append((first, second))
    return found


NT = (((1,), (1,)), ((), ()))
NN = (((1,), (0,)), ((), ()))


def dot(a, b, dims=NN):
    return lax.dot_general(a, b, dims, preferred_element_type=F32)


def step_blocks(cols, z):
    return -(-(cols + 2 * HALF * (DEPTHS - 1 - z)) // LANES)


def receiver_steps(x_ref, outs, w_ref, freqs, cols):
    block = 0
    source = x_ref
    for z in range(DEPTHS):
        for b in range(step_blocks(cols, z)):
            window = pl.ds(b * LANES, SPAN)
            for f in range(freqs):
                got = dot(source[f, :, window], w_ref[block, f, 0], NT)
                got += dot(source[freqs + f, :, window], w_ref[block, f, 1], NT)
                outs(z, f, b, got[:, :LANES].astype(BF))
                outs(z, freqs + f, b, got[:, LANES:].astype(BF))
            block += 1
        source = outs.source(z)


class Store:
    def __init__(self, refs, places):
        self.refs, self.places = refs, places

    def __call__(self, z, plane, b, value):
        for at, start, size in self.places:
            self.refs[z][plane, at:at + size, b * LANES:(b + 1) * LANES] = value[start:start + size]

    def source(self, z):
        return self.refs[z]


def own_kernel(
    x_ref, edge_ref, ra_ref, rb_ref, ridx_ref, table_ref, bins_ref, weight_ref,
    w_ref, a0_ref, a1_ref, a2_ref, pair_ref, wide_ref, widx_ref, wt_ref,
):
    planes, rows, cols = x_ref.shape
    freqs = planes // 2
    tiles = cols // LANES
    entries = table_ref.shape[0]
    wt_ref[...] = jnp.zeros(wt_ref.shape, F32)
    wt_ref[0:DEPTHS, 0:weight_ref.shape[1]] = weight_ref[...]
    for t in range(tiles):
        bins = bins_ref[:, t * LANES:(t + 1) * LANES]
        for z in range(DEPTHS):
            row = jnp.broadcast_to(wt_ref[z:z + 1, :], (rows, LANES))
            pair_ref[z, :, t * LANES:(t + 1) * LANES] = jnp.take_along_axis(row, bins, axis=1)
    lane = lane_of((rows, LANES))
    for p in range(planes):
        edge = edge_ref[p * rows:(p + 1) * rows, :].astype(F32)
        own = [x_ref[p, :, t * LANES:(t + 1) * LANES].astype(F32) for t in range(tiles)]
        moved = [shifted(o, HALO) for o in own]
        before = [edge] + moved
        after = moved + [edge]
        for t in range(tiles + 1):
            wide_ref[p, :, t * LANES:(t + 1) * LANES] = jnp.where(lane < HALO, before[t], after[t]).astype(BF)
        wide_ref[p, :, (tiles + 1) * LANES:] = jnp.zeros((rows, LANES), BF)
    base = planes * rows
    even = parity("rec") == 0
    got_a, got_b = ra_ref[base:base + IDX_ROWS, :], rb_ref[base:base + IDX_ROWS, :]
    left = jnp.where(even, got_b, got_a).astype(F32)[0:8]
    right = jnp.where(even, got_a, got_b).astype(F32)[0:8]
    left = jnp.where(has_left("rec"), left, -1.0)
    right = jnp.where(has_right("rec"), right, -1.0)
    widx_ref[...] = jnp.zeros(widx_ref.shape, F32)
    widx_ref[0:DEPTHS, :] = ridx_ref[...].astype(F32)
    own = [widx_ref[:, t * LANES:(t + 1) * LANES] for t in range(tiles)]
    table = table_ref[...]
    block = 0
    for z in range(DEPTHS):
        index = wide_tiles(own, left, right, HALF * (DEPTHS - 1 - z), -1.0)
        for b in range(step_blocks(cols, z)):
            found = bands(index[b][z:z + 1].astype(jnp.int32), table, entries)
            for f in range(freqs):
                re, im = found[2 * f], found[2 * f + 1]
                for half in range(2):
                    at = pl.ds(half * LANES, LANES)
                    w_ref[block, f, 0, 0:LANES, at] = re[half]
                    w_ref[block, f, 0, LANES:SPAN, at] = im[half]
                    w_ref[block, f, 1, 0:LANES, at] = -im[half]
                    w_ref[block, f, 1, LANES:SPAN, at] = re[half]
            block += 1
    for ref in (a0_ref, a1_ref):
        for p in range(planes):
            ref[p, :, (tiles + 1) * LANES:] = jnp.zeros((rows, LANES), BF)
    store = Store((a0_ref, a1_ref, a2_ref), ((0, 0, rows),))
    receiver_steps(wide_ref, store, w_ref, freqs, cols)


def last_kernel(
    rows, cols, sa_ref, sb_ref, ca_ref, cb_ref, sidx_ref, table_ref, w_ref, o0_ref, o1_ref, o2_ref, pair_ref,
    final_ref, send_ref, keep_ref, wide_ref, a0_ref, a1_ref, a2_ref, sx_ref, part_ref,
):
    planes = o0_ref.shape[0]
    freqs = planes // 2
    tiles = cols // LANES
    entries = table_ref.shape[0]
    even = parity("src") == 0
    lane = lane_of((HALO, LANES))
    for side in range(2):
        there = has_left("src") if side == 0 else has_right("src")
        for p in range(planes):
            at = slice(p * HALO, (p + 1) * HALO)

            def got(a_ref, b_ref, lanes):
                a, b = a_ref[at, lanes], b_ref[at, lanes]
                return jnp.where(even, b, a) if side == 0 else jnp.where(even, a, b)

            edge = got(ca_ref, cb_ref, slice(0, LANES)).astype(F32)
            moved = [
                shifted(got(sa_ref, sb_ref, slice(t * LANES, (t + 1) * LANES)).astype(F32), HALO)
                for t in range(tiles)
            ]
            before, after = [edge] + moved, moved + [edge]
            to = slice(side * HALO, (side + 1) * HALO)
            for t in range(tiles + 1):
                value = jnp.where(lane < HALO, before[t], after[t])
                wide_ref[p, to, t * LANES:(t + 1) * LANES] = jnp.where(there, value, 0.0).astype(BF)
            wide_ref[p, to, (tiles + 1) * LANES:] = jnp.zeros((HALO, LANES), BF)
    full = rows + 2 * HALO
    for ref, own in ((a0_ref, o0_ref), (a1_ref, o1_ref), (a2_ref, o2_ref)):
        width = ref.shape[2]
        for p in range(planes):
            ref[p, HALO:HALO + rows, :] = own[p]
            ref[p, full:, :] = jnp.zeros((ref.shape[1] - full, width), BF)
            if width > (tiles + 1) * LANES:
                for to in (0, HALO + rows):
                    ref[p, to:to + HALO, (tiles + 1) * LANES:] = jnp.zeros((HALO, LANES), BF)
    base = planes * HALO
    got_a, got_b = ca_ref[base:base + IDX_ROWS, :], cb_ref[base:base + IDX_ROWS, :]
    left = jnp.where(even, got_b, got_a).astype(F32)[0:8]
    right = jnp.where(even, got_a, got_b).astype(F32)[0:8]
    left = jnp.where(has_left("src"), left, -1.0)
    right = jnp.where(has_right("src"), right, -1.0)
    sx_ref[...] = jnp.zeros(sx_ref.shape, F32)
    sx_ref[0:DEPTHS, 0:rows] = sidx_ref[...].astype(F32)
    reach = HALO - HALF
    lane8 = lane_of((8, LANES))
    index = jnp.where(
        lane8 < reach,
        shifted(left, reach - rows),
        jnp.where(lane8 < reach + rows, shifted(sx_ref[...], reach), shifted(right, reach + rows)),
    )
    table = table_ref[...]
    ops = []
    for z in range(DEPTHS):
        row = shifted(index, -z * HALF)[z:z + 1].astype(jnp.int32)
        ops.append(bands(row, table, entries))
    sums = []
    for f in range(freqs):
        (s0r, s0r2), (s0i, s0i2) = ops[0][2 * f], ops[0][2 * f + 1]
        s1r, s1i = ops[1][2 * f][0], ops[1][2 * f + 1][0]
        s2r, s2i = ops[2][2 * f][0][:rows], ops[2][2 * f + 1][0][:rows]
        s12r = (dot(s2r, s1r) - dot(s2i, s1i)).astype(BF)
        s12i = (dot(s2r, s1i) + dot(s2i, s1r)).astype(BF)
        lr = jnp.concatenate([s12r, s1r[HALF:HALF + rows]], axis=0)
        li = jnp.concatenate([s12i, s1i[HALF:HALF + rows]], axis=0)
        s0r = jnp.concatenate([s0r, s0r2], axis=1)
        s0i = jnp.concatenate([s0i, s0i2], axis=1)
        pr = (dot(lr, s0r) - dot(li, s0i)).astype(BF)
        pi = (dot(lr, s0i) + dot(li, s0r)).astype(BF)
        sums.append((
            (s0r[reach:reach + rows], s0i[reach:reach + rows]),
            (pr[rows:], pi[rows:]),
            (pr[:rows], pi[:rows]),
        ))
    store = Store((a0_ref, a1_ref, a2_ref), ((0, 0, HALO), (HALO + rows, HALO, HALO)))
    receiver_halo(wide_ref, store, w_ref, freqs, cols, rows)
    lane = lane_of((rows, LANES))
    images = []
    for z in range(DEPTHS - 1):
        ref = (a0_ref, a1_ref)[z]
        width = (tiles + 1) * LANES
        total = None
        for f in range(freqs):
            re, im = sums[f][z]
            term = dot(re, ref[f, :, 0:width]) - dot(im, ref[freqs + f, :, 0:width])
            total = term if total is None else total + term
        back = HALF * (DEPTHS - 1 - z)
        moved = [shifted(total[:, t * LANES:(t + 1) * LANES], -back) for t in range(tiles + 1)]
        images.append([jnp.where(lane < LANES - back, moved[t], moved[t + 1]) for t in range(tiles)])
    real = None
    for f in range(freqs):
        re, im = sums[f][DEPTHS - 1]
        first = dot(jnp.concatenate([re, im], axis=0), a2_ref[f])
        second = dot(jnp.concatenate([-im, re], axis=0), a2_ref[freqs + f])
        both = (first + second).astype(BF)
        final_ref[f] = both[:rows]
        final_ref[freqs + f] = both[rows:]
        term = both[:rows].astype(F32)
        real = term if real is None else real + term
    for t in range(tiles):
        at = slice(t * LANES, (t + 1) * LANES)
        value = pair_ref[DEPTHS - 1, :, at] * real[:, at]
        for z in range(DEPTHS - 1):
            value += pair_ref[z, :, at] * images[z][t]
        part_ref[:, at] = value
    count = lax.axis_size("freq")
    share = rows // count
    me = lax.axis_index("freq")
    keep_ref[...] = part_ref[pl.ds(pl.multiple_of(me * share, 8), share), :]
    for j in range(1, count):
        there = partner(me, j, count)
        send_ref[j - 1] = part_ref[pl.ds(pl.multiple_of(there * share, 8), share), :].astype(BF)


def receiver_halo(x_ref, store, w_ref, freqs, cols, rows):
    block = 0
    for z in range(DEPTHS):
        for b in range(step_blocks(cols, z)):
            window = slice(b * LANES, b * LANES + SPAN)
            for f in range(freqs):
                if z == 0:
                    re, im = x_ref[f, :, window], x_ref[freqs + f, :, window]
                else:
                    ref = store.refs[z - 1]
                    re, im = (
                        jnp.concatenate([ref[p, 0:HALO, window], ref[p, HALO + rows:2 * HALO + rows, window]], axis=0)
                        for p in (f, freqs + f)
                    )
                got = dot(re, w_ref[block, f, 0], NT) + dot(im, w_ref[block, f, 1], NT)
                store(z, f, b, got[:, :LANES].astype(BF))
                store(z, freqs + f, b, got[:, LANES:].astype(BF))
            block += 1


def partner(me, j, count):
    if count & (count - 1) == 0:
        return me ^ j
    return (me + j) % count


def local_call(kernel, outs, scratch=(), flops=0, moved=0, vmem=16):
    return pl.pallas_call(
        kernel,
        out_shape=[jax.ShapeDtypeStruct(s, d) for s, d in outs],
        scratch_shapes=[pltpu.VMEM(s, d) for s, d in scratch],
        compiler_params=pltpu.CompilerParams(vmem_limit_bytes=vmem << 20),
        cost_estimate=pl.CostEstimate(flops=flops, bytes_accessed=moved, transcendentals=0),
    )


def shards(wave, tap_table, src_index, rec_index, offset_bin, bin_weight):
    freqs, rows, cols = wave.shape[1:]
    planes = 2 * freqs
    tiles = cols // LANES
    entries = tap_table.shape[1]
    count = lax.axis_size("freq")
    share = rows // count
    x = wave.reshape(planes, rows, cols)
    table = jnp.transpose(tap_table.astype(BF), (1, 2, 0, 3))
    table = jnp.pad(table, ((0, 0), (0, 0), (0, 0), (0, LANES - TAPS))).reshape(entries, planes * LANES)

    main = (planes * HALO, cols)
    beside = (planes * rows + IDX_ROWS, LANES)
    sa, sb, ra, rb = local_call(pack_kernel, [(main, BF), (main, BF), (beside, BF), (beside, BF)], moved=1 << 20)(
        x, rec_index
    )
    ra, rb = swap(ra, "rec", 0), swap(rb, "rec", 1)
    sa, sb = swap(sa, "src", 0), swap(sb, "src", 1)
    corner = (planes * HALO + IDX_ROWS, LANES)
    ca, cb, edge = local_call(
        functools.partial(corner_kernel, rows),
        [(corner, BF), (corner, BF), ((planes * rows, LANES), BF)],
        moved=1 << 18,
    )(ra, rb, src_index)
    ca, cb = swap(ca, "src", 0), swap(cb, "src", 1)

    blocks = sum(step_blocks(cols, z) for z in range(DEPTHS))
    wide = (tiles + 2) * LANES
    w, o0, o1, o2, pair = local_call(
        own_kernel,
        [
            ((blocks, freqs, 2, SPAN, SPAN), BF),
            ((planes, rows, wide), BF),
            ((planes, rows, wide), BF),
            ((planes, rows, cols), BF),
            ((DEPTHS, rows, cols), F32),
        ],
        [((planes, rows, wide), BF), ((8, cols), F32), ((8, LANES), F32)],
        flops=1 << 31,
        moved=10 << 20,
        vmem=24,
    )(x, edge, ra, rb, rec_index, table, offset_bin, bin_weight)
    deep = -(-(rows + 2 * HALO) // SPAN) * SPAN
    final, send, keep = local_call(
        functools.partial(last_kernel, rows, cols),
        [((planes, rows, cols), BF), ((max(count - 1, 1), share, cols), BF), ((share, cols), F32)],
        [
            ((planes, 2 * HALO, wide), BF),
            ((planes, deep, wide), BF),
            ((planes, deep, wide), BF),
            ((planes, deep, cols), BF),
            ((8, LANES), F32),
            ((rows, cols), F32),
        ],
        flops=1 << 31,
        moved=10 << 20,
        vmem=28,
    )(sa, sb, ca, cb, src_index, table, w, o0, o1, o2, pair)
    total = keep
    for j in range(1, count):
        got = lax.ppermute(send[j - 1], "freq", [(i, partner(i, j, count)) for i in range(count)])
        total = total + got.astype(F32)
    scale = 1.0 / math.sqrt(freqs * count * DEPTHS)
    return final.reshape(wave.shape), total * scale


def solution(mesh):
    placed = (
        P(None, "freq", "src", "rec"),
        P(None, None, "freq", None),
        P(None, "src"),
        P(None, "rec"),
        P("src", "rec"),
        P(),
    )
    return jax.shard_map(
        shards,
        mesh=mesh,
        in_specs=placed,
        out_specs=(P(None, "freq", "src", "rec"), P(("src", "freq"), "rec")),
        check_vma=False,
    )
```

time: 119 us -> 26.1 us (0.22); the launches traced: 117 us -> 25.7 us
  starting transfers between devices: 31.4 us -> 8.43 us
  local copies, waits for them, and re-layouts: 28 us -> 5.78 us
  waiting for transfers between devices: 23.1 us -> 1.22 us
  between operations: 15 us -> 0.75 us
  matrix products: 13.1 us -> 0 us
  Pallas kernels: 0 us -> 7.99 us
  other arithmetic: 6.36 us -> 1.54 us
    ppermute x12 -> x7, starting transfers between devices: 31.4 us -> 8.43 us  [the longest x6 8.42 us: swap(): return lax.ppermute(cells, (axis, 'freq'), pairs_of(axis, odd))]
    dot_general x26 -> x0, matrix products: 13.1 us -> none  [the longest x8 8.44 us: one_block(): jnp.einsum('srh,zh->zsr', onehot, bin_weight, precision=lax.Precision.HIG...]
    reduce_scatter x1 -> x0, waiting for transfers between devices: 12 us -> none  [shards(): lax.psum_scatter(image_part.astype(jnp.bfloat16), 'freq', scatter_dimensi...]
    ppermute x12 -> x7, waiting for transfers between devices: 11 us -> 1.22 us  [the longest x1 1.2 us: shards(): lax.ppermute(send[j - 1], 'freq', [(i, partner(i, j, count)) for i in ran...]
    pallas_call x0 -> x4, Pallas kernels: none -> 7.99 us  [the longest x1 4.26 us: shards(): local_call(functools.partial(last_kernel, rows, cols), [((planes, rows, c...]
    reshape x9 -> x1, local copies, waits for them, and re-layouts: 6.53 us -> 0.03 us  [shards(): jnp.pad(table, ((0, 0), (0, 0), (0, 0), (0, LANES - TAPS)))]
    squeeze x21 -> x0, local copies, waits for them, and re-layouts: 5.98 us -> none  [the longest x18 5.86 us: operator_pair(): real_part = jnp.concatenate([matrices[0], -matrices[1]], axis=-1)]
    eq x9 -> x0, local copies, waits for them, and re-layouts: 5.75 us -> none  [the longest x8 5.75 us: one_block(): bins_block[:, :, None] == jnp.arange(bin_count, dtype=jnp.int32)]
  transfers between devices with their start and end apart: 13 -> 7, of which waited for: 6 -> 1; matrix products, arithmetic and copies ran while one was open for 29% -> 4% of each run, Pallas kernels for 0% -> 14%
where the time goes in v1:
time: 26.1 us; the launch traced here: 25.7 us
  starting transfers between devices  8.43 us (32%)
  Pallas kernels  7.99 us (31%)
  local copies, waits for them, and re-layouts  5.78 us (22%)
  other arithmetic  1.54 us (6%)
  waiting for transfers between devices  1.22 us (5%)
  between operations  0.75 us (3%)
    ppermute x6, starting transfers between devices, swap(): return lax.ppermute(cells, (axis, 'freq'), pairs_of(axis, odd))  8.42 us
    unnamed x17, local copies, waits for them, and re-layouts  5.68 us
    pallas_call x1, Pallas kernels, shards(): local_call(functools.partial(last_kernel, rows, cols), [((planes, rows, c...  4.26 us
    pallas_call x1, Pallas kernels, shards(): local_call(own_kernel, [((blocks, freqs, 2, SPAN, SPAN), BF), ((planes, r...  3.54 us
    ppermute x1, waiting for transfers between devices, shards(): lax.ppermute(send[j - 1], 'freq', [(i, partner(i, j, count)) for i in ran...  1.2 us
    transpose x1, other arithmetic, shards(): table = jnp.transpose(tap_table.astype(BF), (1, 2, 0, 3))  0.91 us
    mul x1, other arithmetic, shards(): return (final.reshape(wave.shape), total * scale)  0.64 us
  transfers between devices with their start and end apart: 7, of which 1 were waited for; matrix products, arithmetic and copies ran while one was open for 4% of the time, Pallas kernels for 14%

profile of v1, /device:TPU:9, one launch (start us, length us, event | category | flops | bytes accessed | tf_op | source)
XLA Modules:
  0.0 25.7 jit_solution(15351511872799411908)
XLA Ops:
  0.6 0.0 copy-start
  0.6 0.9 %copy-done = bf16[2,2,64,512]{3,2,1,0:T(8,128)(2,1)S(1)} copy-done((bf16[2,2,64,512]{3,2,1,0:T(8,128)(2,1)S(1)}, bf16[2,2,64,512]{3,2,1,0:T(8,128)(2,1)}, u32[]{:S(2)}) %copy-start) | copy-done | bytes 262168
  1.6 0.7 %copy-done.4 = s32[3,512]{1,0:T(4,128)S(1)} copy-done((s32[3,512]{1,0:T(4,128)S(1)}, s32[3,512]{1,0:T(4,128)}, u32[]{:S(2)}) %copy-start.4) | copy-done | bytes 6168
  2.3 0.1 shard_map.77
  2.3 0.1 collective-permute-start.2
  2.4 2.6 %collective-permute-start.3 = (bf16[272,128]{1,0:T(8,128)(2,1)S(1)}, bf16[272,128]{1,0:T(8,128)(2,1)S(1)}, u32[]{:S(2)}, u32[]{:S(2)}) collective-permute-start(bf16[272,128]{1,0:T(8,128)(2,1)S(1)} %get-tuple-element.20), channel_id=1, source_target_pairs={{2,4},{4,2},{3,5},{5,3},{0,1},{1,0},{6,7},{7,6},{10,12},{12,10},{1... | collective-permute-start | bytes 208904 | tf_op jit(solution)/shard_map/ppermute | solution.py:37
  5.0 1.2 %collective-permute-start = (bf16[192,512]{1,0:T(8,128)(2,1)S(1)}, bf16[192,512]{1,0:T(8,128)(2,1)S(1)}, u32[]{:S(2)}, u32[]{:S(2)}) collective-permute-start(bf16[192,512]{1,0:T(8,128)(2,1)S(1)} %get-tuple-element.17), channel_id=1, source_target_pairs={{0,8},{8,0},{1,9},{9,1},{16,24},{24,16},{17,25},{25,17},{2,10},{10... | collective-permute-start | bytes 589832 | tf_op jit(solution)/shard_map/ppermute | solution.py:37
  6.2 1.5 %collective-permute-start.1 = (bf16[192,512]{1,0:T(8,128)(2,1)S(1)}, bf16[192,512]{1,0:T(8,128)(2,1)S(1)}, u32[]{:S(2)}, u32[]{:S(2)}) collective-permute-start(bf16[192,512]{1,0:T(8,128)(2,1)S(1)} %get-tuple-element.18), channel_id=1, source_target_pairs={{8,16},{16,8},{9,17},{17,9},{0,1},{1,0},{24,25},{25,24},{10,18},{1... | collective-permute-start | bytes 589832 | tf_op jit(solution)/shard_map/ppermute | solution.py:37
  7.7 0.9 %convert_bitcast_fusion = bf16[64,2,2,33]{0,1,3,2:T(2,128)(2,1)S(1)} fusion(f32[2,64,2,33]{1,2,3,0:T(2,128)} %param.7), kind=kLoop, calls=%fused_computation.1 | loop fusion | flops 8448 | bytes 50688 | tf_op jit(solution)/shard_map/transpose | solution.py:400
  8.6 0.1 copy.9
  8.8 0.1 pad.4.clone
  8.9 0.0 collective-permute-done.2.ra_ref
  8.9 0.0 collective-permute-done.3.rb_ref
  8.9 0.0 copy-start.2
  8.9 0.7 %copy-done.2 = s32[3,64]{1,0:T(4,128)S(1)} copy-done((s32[3,64]{1,0:T(4,128)S(1)}, s32[3,64]{1,0:T(4,128)}, u32[]{:S(2)}) %copy-start.2) | copy-done | bytes 792
  9.6 0.1 shard_map.78
  9.7 1.0 %collective-permute-start.4 = (bf16[208,128]{1,0:T(8,128)(2,1)S(1)}, bf16[208,128]{1,0:T(8,128)(2,1)S(1)}, u32[]{:S(2)}, u32[]{:S(2)}) collective-permute-start(bf16[208,128]{1,0:T(8,128)(2,1)S(1)} %get-tuple-element.21), channel_id=1, source_target_pairs={{0,8},{8,0},{1,9},{9,1},{16,24},{24,16},{17,25},{25,17},{2,10},{10... | collective-permute-start | bytes 159752 | tf_op jit(solution)/shard_map/ppermute | solution.py:37
  10.7 2.1 %collective-permute-start.5 = (bf16[208,128]{1,0:T(8,128)(2,1)S(1)}, bf16[208,128]{1,0:T(8,128)(2,1)S(1)}, u32[]{:S(2)}, u32[]{:S(2)}) collective-permute-start(bf16[208,128]{1,0:T(8,128)(2,1)S(1)} %get-tuple-element.22), channel_id=1, source_target_pairs={{8,16},{16,8},{9,17},{17,9},{0,1},{1,0},{24,25},{25,24},{10,18},{1... | collective-permute-start | bytes 159752 | tf_op jit(solution)/shard_map/ppermute | solution.py:37
  12.8 0.9 %copy-done.1 = bf16[2,2,64,512]{3,2,1,0:T(8,128)(2,1)S(1)} copy-done((bf16[2,2,64,512]{3,2,1,0:T(8,128)(2,1)S(1)}, bf16[2,2,64,512]{3,2,1,0:T(8,128)(2,1)}, u32[]{:S(2)}) %copy-start.1) | copy-done | bytes 262168
  13.7 0.7 %copy-done.5 = s32[3,512]{1,0:T(4,128)S(1)} copy-done((s32[3,512]{1,0:T(4,128)S(1)}, s32[3,512]{1,0:T(4,128)}, u32[]{:S(2)}) %copy-start.5) | copy-done | bytes 6168
  14.4 0.9 %copy-done.6 = s32[64,512]{1,0:T(8,128)S(1)} copy-done((s32[64,512]{1,0:T(8,128)S(1)}, s32[64,512]{1,0:T(8,128)}, u32[]{:S(2)}) %copy-start.6) | copy-done | bytes 131096
  15.3 0.7 %copy-done.7 = f32[3,64]{1,0:T(4,128)S(1)} copy-done((f32[3,64]{1,0:T(4,128)S(1)}, f32[3,64]{1,0:T(4,128)}, u32[]{:S(2)}) %copy-start.7) | copy-done | bytes 792
  16.0 3.5 %shard_map.79 = (bf16[14,2,2,256,256]{4,3,2,1,0:T(8,128)(2,1)S(1)}, bf16[4,64,768]{2,1,0:T(8,128)(2,1)S(1)}, bf16[4,64,768]{2,1,0:T(8,128)(2,1)S(1)}, bf16[4,64,512]{2,1,0:T(8,128)(2,1)S(1)}, f32[3,64,512]{2,1,0:T(8,128)S(1)}) custom-call(bf16[4,64,512]{2,1,0:T(8,128)(2,1)S(1)} %bitcast.6, bf16[256,128]{1,0:T(8,128)(2,1)S(1)} %get-tuple-element.23.edge_ref, ...), custom_call_target="tpu_custom_call" | custom-call | flops 2147483648 | bytes 10485760 | tf_op jit(solution)/shard_map/pallas_call | solution.py:420
  19.6 0.0 collective-permute-done.4.ca_ref
  19.6 0.0 collective-permute-done.5.cb_ref
  19.6 0.0 collective-permute-done.sa_ref
  19.6 0.0 collective-permute-done.1.sb_ref
  19.6 0.0 copy-done.3
  19.6 4.3 %shard_map.80 = (bf16[4,64,512]{2,1,0:T(8,128)(2,1)}, bf16[1,32,512]{2,1,0:T(8,128)(2,1)S(1)}, f32[32,512]{1,0:T(8,128)S(1)}) custom-call(bf16[192,512]{1,0:T(8,128)(2,1)S(1)} %collective-permute-done.sa_ref, bf16[192,512]{1,0:T(8,128)(2,1)S(1)} %collective-permute-done.1.sb_ref, bf16[208,128]{1,0:T(8,128)(2,1)S(1)} %collective-permute-done.4.ca_ref, ...), custom_call_target="tpu_custom_call" | custom-call | flops 2147483648 | bytes 10485760 | tf_op jit(solution)/shard_map/pallas_call | solution.py:435
  23.9 0.0 collective-permute-start.6
  23.9 1.2 %collective-permute-done.6 = bf16[32,512]{1,0:T(8,128)(2,1)S(1)} collective-permute-done((bf16[32,512]{1,0:T(8,128)(2,1)S(1)}, bf16[32,512]{1,0:T(8,128)(2,1)S(1)}, u32[]{:S(2)}, u32[]{:S(2)}) %collective-permute-start.6) | collective-permute-done | bytes 32800 | tf_op jit(solution)/shard_map/ppermute | solution.py:452
  25.1 0.6 %add_multiply_fusion = f32[32,512]{1,0:T(8,128)} fusion(f32[32,512]{1,0:T(8,128)S(1)} %get-tuple-element.30, bf16[32,512]{1,0:T(8,128)(2,1)S(1)} %collective-permute-done.6), kind=kLoop, calls=%fused_computation | loop fusion | flops 49152 | bytes 163840 | tf_op jit(solution)/shard_map/mul | solution.py:455
  (7 shorter events, 0.0 us)
Async XLA Ops:
  0.6 1.0 %copy-start = (bf16[2,2,64,512]{3,2,1,0:T(8,128)(2,1)S(1)}, bf16[2,2,64,512]{3,2,1,0:T(8,128)(2,1)}, u32[]{:S(2)}) copy-start(bf16[2,2,64,512]{3,2,1,0:T(8,128)(2,1)} %param.6) | copy-start | bytes 786436
  1.6 0.7 %copy-start.4 = (s32[3,512]{1,0:T(4,128)S(1)}, s32[3,512]{1,0:T(4,128)}, u32[]{:S(2)}) copy-start(s32[3,512]{1,0:T(4,128)} %ridx_ref.3) | copy-start | bytes 18436
  2.3 17.3 %copy-start.3 = (s32[3,64]{1,0:T(4,128)S(1)}, s32[3,64]{1,0:T(4,128)}, u32[]{:S(2)}) copy-start(s32[3,64]{1,0:T(4,128)} %sidx_ref.3) | copy-start | bytes 2308
  2.3 6.5 %collective-permute-start.2 = (bf16[272,128]{1,0:T(8,128)(2,1)S(1)}, bf16[272,128]{1,0:T(8,128)(2,1)S(1)}, u32[]{:S(2)}, u32[]{:S(2)}) collective-permute-start(bf16[272,128]{1,0:T(8,128)(2,1)S(1)} %get-tuple-element.19), channel_id=1, source_target_pairs={{0,2},{2,0},{1,3},{3,1},{4,6},{6,4},{5,7},{7,5},{8,10},{10,8},{9,1... | collective-permute-start | bytes 208904 | tf_op jit(solution)/shard_map/ppermute | solution.py:37
  2.4 6.5 %collective-permute-start.3 = (bf16[272,128]{1,0:T(8,128)(2,1)S(1)}, bf16[272,128]{1,0:T(8,128)(2,1)S(1)}, u32[]{:S(2)}, u32[]{:S(2)}) collective-permute-start(bf16[272,128]{1,0:T(8,128)(2,1)S(1)} %get-tuple-element.20), channel_id=1, source_target_pairs={{2,4},{4,2},{3,5},{5,3},{0,1},{1,0},{6,7},{7,6},{10,12},{12,10},{1... | collective-permute-start | bytes 208904 | tf_op jit(solution)/shard_map/ppermute | solution.py:37
  5.0 14.6 %collective-permute-start = (bf16[192,512]{1,0:T(8,128)(2,1)S(1)}, bf16[192,512]{1,0:T(8,128)(2,1)S(1)}, u32[]{:S(2)}, u32[]{:S(2)}) collective-permute-start(bf16[192,512]{1,0:T(8,128)(2,1)S(1)} %get-tuple-element.17), channel_id=1, source_target_pairs={{0,8},{8,0},{1,9},{9,1},{16,24},{24,16},{17,25},{25,17},{2,10},{10... | collective-permute-start | bytes 589832 | tf_op jit(solution)/shard_map/ppermute | solution.py:37
  6.2 13.4 %collective-permute-start.1 = (bf16[192,512]{1,0:T(8,128)(2,1)S(1)}, bf16[192,512]{1,0:T(8,128)(2,1)S(1)}, u32[]{:S(2)}, u32[]{:S(2)}) collective-permute-start(bf16[192,512]{1,0:T(8,128)(2,1)S(1)} %get-tuple-element.18), channel_id=1, source_target_pairs={{8,16},{16,8},{9,17},{17,9},{0,1},{1,0},{24,25},{25,24},{10,18},{1... | collective-permute-start | bytes 589832 | tf_op jit(solution)/shard_map/ppermute | solution.py:37
  8.9 0.7 %copy-start.2 = (s32[3,64]{1,0:T(4,128)S(1)}, s32[3,64]{1,0:T(4,128)}, u32[]{:S(2)}) copy-start(s32[3,64]{1,0:T(4,128)} %sidx_ref.3) | copy-start | bytes 2308
  9.7 9.8 %collective-permute-start.4 = (bf16[208,128]{1,0:T(8,128)(2,1)S(1)}, bf16[208,128]{1,0:T(8,128)(2,1)S(1)}, u32[]{:S(2)}, u32[]{:S(2)}) collective-permute-start(bf16[208,128]{1,0:T(8,128)(2,1)S(1)} %get-tuple-element.21), channel_id=1, source_target_pairs={{0,8},{8,0},{1,9},{9,1},{16,24},{24,16},{17,25},{25,17},{2,10},{10... | collective-permute-start | bytes 159752 | tf_op jit(solution)/shard_map/ppermute | solution.py:37
  10.7 8.9 %collective-permute-start.5 = (bf16[208,128]{1,0:T(8,128)(2,1)S(1)}, bf16[208,128]{1,0:T(8,128)(2,1)S(1)}, u32[]{:S(2)}, u32[]{:S(2)}) collective-permute-start(bf16[208,128]{1,0:T(8,128)(2,1)S(1)} %get-tuple-element.22), channel_id=1, source_target_pairs={{8,16},{16,8},{9,17},{17,9},{0,1},{1,0},{24,25},{25,24},{10,18},{1... | collective-permute-start | bytes 159752 | tf_op jit(solution)/shard_map/ppermute | solution.py:37
  12.8 0.9 %copy-start.1 = (bf16[2,2,64,512]{3,2,1,0:T(8,128)(2,1)S(1)}, bf16[2,2,64,512]{3,2,1,0:T(8,128)(2,1)}, u32[]{:S(2)}) copy-start(bf16[2,2,64,512]{3,2,1,0:T(8,128)(2,1)} %param.6) | copy-start | bytes 786436
  13.7 0.7 %copy-start.5 = (s32[3,512]{1,0:T(4,128)S(1)}, s32[3,512]{1,0:T(4,128)}, u32[]{:S(2)}) copy-start(s32[3,512]{1,0:T(4,128)} %ridx_ref.3) | copy-start | bytes 18436
  14.4 0.9 %copy-start.6 = (s32[64,512]{1,0:T(8,128)S(1)}, s32[64,512]{1,0:T(8,128)}, u32[]{:S(2)}) copy-start(s32[64,512]{1,0:T(8,128)} %bins_ref.1) | copy-start | bytes 393220
  15.3 0.7 %copy-start.7 = (f32[3,64]{1,0:T(4,128)S(1)}, f32[3,64]{1,0:T(4,128)}, u32[]{:S(2)}) copy-start(f32[3,64]{1,0:T(4,128)} %weight_ref.1) | copy-start | bytes 2308
  23.9 1.2 %collective-permute-start.6 = (bf16[32,512]{1,0:T(8,128)(2,1)S(1)}, bf16[32,512]{1,0:T(8,128)(2,1)S(1)}, u32[]{:S(2)}, u32[]{:S(2)}) collective-permute-start(bf16[32,512]{1,0:T(8,128)(2,1)S(1)} %bitcast.7), channel_id=1, source_target_pairs={{0,1},{1,0},{2,3},{3,2},{4,5},{5,4},{6,7},{7,6},{8,9},{9,8},{10,11... | collective-permute-start | bytes 98312 | tf_op jit(solution)/shard_map/ppermute | solution.py:452

commit v2 on v1

--- a/solution.py
+++ b/solution.py
@@ -64,8 +64,16 @@
     return jnp.where(even, b, a), jnp.where(even, a, b)
 
 
-def pack_kernel(x_ref, ridx_ref, sa_ref, sb_ref, ra_ref, rb_ref):
+def pack_kernel(*refs):
+    sources, targets = refs[:5], refs[9:14]
+    sa_ref, sb_ref, ra_ref, rb_ref = refs[5:9]
+    sem = refs[14]
+    copies = [pltpu.make_async_copy(s, t, sem.at[i]) for i, (s, t) in enumerate(zip(sources, targets))]
+    for copy in copies:
+        copy.start()
+    x_ref, ridx_ref = targets[:2]
     planes, rows, cols = x_ref.shape
+    copies[0].wait()
     even = parity("src") == 0
     low = rows - HALO
     at = pl.multiple_of(jnp.where(even, low, 0), 16)
@@ -75,6 +83,7 @@
         sb_ref[p * HALO:(p + 1) * HALO, :] = x_ref[p, pl.ds(other, HALO), :]
     even = parity("rec") == 0
     tail_at = cols - LANES
+    copies[1].wait()
     for p in range(planes):
         head, tail = x_ref[p, :, 0:LANES], x_ref[p, :, tail_at:cols]
         ra_ref[p * rows:(p + 1) * rows, :] = jnp.where(even, tail, head)
@@ -86,6 +95,8 @@
         ref[base:base + IDX_ROWS, :] = jnp.zeros((IDX_ROWS, LANES), BF)
     ra_ref[base:base + DEPTHS, :] = jnp.where(even, tail, head)
     rb_ref[base:base + DEPTHS, :] = jnp.where(even, head, tail)
+    for copy in copies[2:]:
+        copy.wait()
 
 
 def corner_kernel(rows, ra_ref, rb_ref, sidx_ref, ca_ref, cb_ref, edge_ref):
@@ -379,17 +390,18 @@
     return (me + j) % count
 
 
-def local_call(kernel, outs, scratch=(), flops=0, moved=0, vmem=16):
+def local_call(kernel, outs, scratch=(), flops=0, moved=0, vmem=16, **others):
     return pl.pallas_call(
         kernel,
         out_shape=[jax.ShapeDtypeStruct(s, d) for s, d in outs],
-        scratch_shapes=[pltpu.VMEM(s, d) for s, d in scratch],
+        scratch_shapes=[pltpu.VMEM(*s) if isinstance(s, tuple) else s for s in scratch],
+        **others,
         compiler_params=pltpu.CompilerParams(vmem_limit_bytes=vmem << 20),
         cost_estimate=pl.CostEstimate(flops=flops, bytes_accessed=moved, transcendentals=0),
     )
 
 
-def shards(wave, tap_table, src_index, rec_index, offset_bin, bin_weight):
+def migrate(wave, tap_table, src_index, rec_index, offset_bin, bin_weight):
     freqs, rows, cols = wave.shape[1:]
     planes = 2 * freqs
     tiles = cols // LANES
@@ -402,11 +414,18 @@
 
     main = (planes * HALO, cols)
     beside = (planes * rows + IDX_ROWS, LANES)
-    sa, sb, ra, rb = local_call(pack_kernel, [(main, BF), (main, BF), (beside, BF), (beside, BF)], moved=1 << 20)(
-        x, rec_index
-    )
-    ra, rb = swap(ra, "rec", 0), swap(rb, "rec", 1)
-    sa, sb = swap(sa, "src", 0), swap(sb, "src", 1)
+    inputs = tuple(pltpu.with_memory_space_constraint(a, pltpu.HBM) for a in (x, rec_index, src_index, offset_bin, bin_weight))
+    sa, sb, ra, rb, x, rec_index, src_index, offset_bin, bin_weight = local_call(
+        pack_kernel,
+        [(main, BF), (main, BF), (beside, BF), (beside, BF)] + [(a.shape, a.dtype) for a in inputs],
+        [pltpu.SemaphoreType.DMA((len(inputs),))],
+        moved=1 << 20,
+        in_specs=[pl.BlockSpec(memory_space=pltpu.HBM)] * len(inputs),
+    )(*inputs)
+    sa = swap(sa, "src", 0)
+    sb = swap(sb, "src", 1)
+    ra = swap(ra, "rec", 0)
+    rb = swap(rb, "rec", 1)
     corner = (planes * HALO + IDX_ROWS, LANES)
     ca, cb, edge = local_call(
         functools.partial(corner_kernel, rows),
@@ -465,7 +484,7 @@
         P(),
     )
     return jax.shard_map(
-        shards,
+        migrate,
         mesh=mesh,
         in_specs=placed,
         out_specs=(P(None, "freq", "src", "rec"), P(("src", "freq"), "rec")),

time: 26.1 us -> 25.1 us (0.962)
  the two profiles are of different devices: /device:TPU:9 before, /device:TPU:11 now
where the time goes in v2:
time: 25.1 us; the launch traced here: 24.9 us
  Pallas kernels  9.01 us (36%)
  starting transfers between devices  9.01 us (36%)
  waiting for transfers between devices  4.41 us (18%)
  other arithmetic  1.54 us (6%)
  between operations  0.69 us (3%)
    ppermute x6, starting transfers between devices, swap(): return lax.ppermute(cells, (axis, 'freq'), pairs_of(axis, odd))  6.91 us
    pallas_call x1, Pallas kernels, migrate(): local_call(functools.partial(last_kernel, rows, cols), [((planes, rows, c...  4.25 us
    ppermute x6, waiting for transfers between devices, swap(): return lax.ppermute(cells, (axis, 'freq'), pairs_of(axis, odd))  3.55 us
    pallas_call x1, Pallas kernels, migrate(): local_call(own_kernel, [((blocks, freqs, 2, SPAN, SPAN), BF), ((planes, r...  3.55 us
    ppermute x1, starting transfers between devices, migrate(): lax.ppermute(send[j - 1], 'freq', [(i, partner(i, j, count)) for i in ran...  2.1 us
    pallas_call x1, Pallas kernels, migrate(): local_call(pack_kernel, [(main, BF), (main, BF), (beside, BF), (beside, B...  1.06 us
    transpose x1, other arithmetic, migrate(): table = jnp.transpose(tap_table.astype(BF), (1, 2, 0, 3))  0.91 us
    ppermute x1, waiting for transfers between devices, migrate(): lax.ppermute(send[j - 1], 'freq', [(i, partner(i, j, count)) for i in ran...  0.86 us
  transfers between devices with their start and end apart: 7, of which 2 were waited for; matrix products, arithmetic and copies ran while one was open for 5% of the time, Pallas kernels for 15%

profile of v2, /device:TPU:11, one launch (start us, length us, event | category | flops | bytes accessed | tf_op | source)
XLA Modules:
  0.0 24.9 jit_solution(13248324961227928496)
XLA Ops:
  0.6 1.1 %shard_map.77 = (bf16[192,512]{1,0:T(8,128)(2,1)S(1)}, bf16[192,512]{1,0:T(8,128)(2,1)S(1)}, bf16[272,128]{1,0:T(8,128)(2,1)S(1)}, bf16[272,128]{1,0:T(8,128)(2,...) custom-call(bf16[4,64,512]{2,1,0:T(8,128)(2,1)} %bitcast.6, ...), custom_call_target="tpu_custom_call" | custom-call | bytes 1048576 | tf_op jit(solution)/shard_map/pallas_call | solution.py:418
  1.7 0.2 collective-permute-start.2
  1.9 2.4 %collective-permute-start.3 = (bf16[272,128]{1,0:T(8,128)(2,1)S(1)}, bf16[272,128]{1,0:T(8,128)(2,1)S(1)}, u32[]{:S(2)}, u32[]{:S(2)}) collective-permute-start(bf16[272,128]{1,0:T(8,128)(2,1)S(1)} %get-tuple-element.25), channel_id=1, source_target_pairs={{2,4},{4,2},{3,5},{5,3},{0,1},{1,0},{6,7},{7,6},{10,12},{12,10},{1... | collective-permute-start | bytes 208904 | tf_op jit(solution)/shard_map/ppermute | solution.py:37
  4.4 0.3 %collective-permute-start = (bf16[192,512]{1,0:T(8,128)(2,1)S(1)}, bf16[192,512]{1,0:T(8,128)(2,1)S(1)}, u32[]{:S(2)}, u32[]{:S(2)}) collective-permute-start(bf16[192,512]{1,0:T(8,128)(2,1)S(1)} %get-tuple-element.22), channel_id=1, source_target_pairs={{0,8},{8,0},{1,9},{9,1},{16,24},{24,16},{17,25},{25,17},{2,10},{10... | collective-permute-start | bytes 589832 | tf_op jit(solution)/shard_map/ppermute | solution.py:37
  4.6 2.2 %collective-permute-start.1 = (bf16[192,512]{1,0:T(8,128)(2,1)S(1)}, bf16[192,512]{1,0:T(8,128)(2,1)S(1)}, u32[]{:S(2)}, u32[]{:S(2)}) collective-permute-start(bf16[192,512]{1,0:T(8,128)(2,1)S(1)} %get-tuple-element.23), channel_id=1, source_target_pairs={{8,16},{16,8},{9,17},{17,9},{0,1},{1,0},{24,25},{25,24},{10,18},{1... | collective-permute-start | bytes 589832 | tf_op jit(solution)/shard_map/ppermute | solution.py:37
  6.8 0.9 %convert_bitcast_fusion = bf16[64,2,2,33]{0,1,3,2:T(2,128)(2,1)S(1)} fusion(f32[2,64,2,33]{1,2,3,0:T(2,128)} %param.7), kind=kLoop, calls=%fused_computation.1 | loop fusion | flops 8448 | bytes 50688 | tf_op jit(solution)/shard_map/transpose | solution.py:412
  7.7 0.1 copy.9
  7.8 0.1 pad.4.clone
  7.9 0.0 collective-permute-done.2.ra_ref
  7.9 0.0 collective-permute-done.3.rb_ref
  8.0 0.1 shard_map.78
  8.1 0.6 %collective-permute-start.4 = (bf16[208,128]{1,0:T(8,128)(2,1)S(1)}, bf16[208,128]{1,0:T(8,128)(2,1)S(1)}, u32[]{:S(2)}, u32[]{:S(2)}) collective-permute-start(bf16[208,128]{1,0:T(8,128)(2,1)S(1)} %get-tuple-element.27), channel_id=1, source_target_pairs={{0,8},{8,0},{1,9},{9,1},{16,24},{24,16},{17,25},{25,17},{2,10},{10... | collective-permute-start | bytes 159752 | tf_op jit(solution)/shard_map/ppermute | solution.py:37
  8.7 1.2 %collective-permute-start.5 = (bf16[208,128]{1,0:T(8,128)(2,1)S(1)}, bf16[208,128]{1,0:T(8,128)(2,1)S(1)}, u32[]{:S(2)}, u32[]{:S(2)}) collective-permute-start(bf16[208,128]{1,0:T(8,128)(2,1)S(1)} %get-tuple-element.28), channel_id=1, source_target_pairs={{8,16},{16,8},{9,17},{17,9},{0,1},{1,0},{24,25},{25,24},{10,18},{1... | collective-permute-start | bytes 159752 | tf_op jit(solution)/shard_map/ppermute | solution.py:37
  9.9 3.6 %shard_map.79 = (bf16[14,2,2,256,256]{4,3,2,1,0:T(8,128)(2,1)S(1)}, bf16[4,64,768]{2,1,0:T(8,128)(2,1)S(1)}, bf16[4,64,768]{2,1,0:T(8,128)(2,1)S(1)}, bf16[4,64,512]{2,1,0:T(8,128)(2,1)S(1)}, f32[3,64,512]{2,1,0:T(8,128)S(1)}) custom-call(bf16[4,64,512]{2,1,0:T(8,128)(2,1)S(1)} %get-tuple-element.29.x_ref, bf16[256,128]{1,0:T(8,128)(2,1)S(1)} %get-tuple-element.30.edge_ref, ...), custom_call_target="tpu_custom_call" | custom-call | flops 2147483648 | bytes 10485760 | tf_op jit(solution)/shard_map/pallas_call | solution.py:439
  13.5 0.0 collective-permute-done.4.ca_ref
  13.5 3.5 %collective-permute-done.5.cb_ref = bf16[208,128]{1,0:T(8,128)(2,1)S(1)} collective-permute-done((bf16[208,128]{1,0:T(8,128)(2,1)S(1)}, bf16[208,128]{1,0:T(8,128)(2,1)S(1)}, u32[]{:S(2)}, u32[]{:S(2)}) %collective-permute-start.5) | collective-permute-done | bytes 53280 | tf_op jit(solution)/shard_map/ppermute | solution.py:37
  17.0 0.0 collective-permute-done.sa_ref
  17.0 0.0 collective-permute-done.1.sb_ref
  17.0 4.3 %shard_map.80 = (bf16[4,64,512]{2,1,0:T(8,128)(2,1)}, bf16[1,32,512]{2,1,0:T(8,128)(2,1)S(1)}, f32[32,512]{1,0:T(8,128)S(1)}) custom-call(bf16[192,512]{1,0:T(8,128)(2,1)S(1)} %collective-permute-done.sa_ref, bf16[192,512]{1,0:T(8,128)(2,1)S(1)} %collective-permute-done.1.sb_ref, bf16[208,128]{1,0:T(8,128)(2,1)S(1)} %collective-permute-done.4.ca_ref, ...), custom_call_target="tpu_custom_call" | custom-call | flops 2147483648 | bytes 10485760 | tf_op jit(solution)/shard_map/pallas_call | solution.py:454
  21.3 2.1 %collective-permute-start.6 = (bf16[32,512]{1,0:T(8,128)(2,1)S(1)}, bf16[32,512]{1,0:T(8,128)(2,1)S(1)}, u32[]{:S(2)}, u32[]{:S(2)}) collective-permute-start(bf16[32,512]{1,0:T(8,128)(2,1)S(1)} %bitcast.5), channel_id=1, source_target_pairs={{0,1},{1,0},{2,3},{3,2},{4,5},{5,4},{6,7},{7,6},{8,9},{9,8},{10,11... | collective-permute-start | bytes 98312 | tf_op jit(solution)/shard_map/ppermute | solution.py:471
  23.4 0.9 %collective-permute-done.6 = bf16[32,512]{1,0:T(8,128)(2,1)S(1)} collective-permute-done((bf16[32,512]{1,0:T(8,128)(2,1)S(1)}, bf16[32,512]{1,0:T(8,128)(2,1)S(1)}, u32[]{:S(2)}, u32[]{:S(2)}) %collective-permute-start.6) | collective-permute-done | bytes 32800 | tf_op jit(solution)/shard_map/ppermute | solution.py:471
  24.3 0.6 %add_multiply_fusion = f32[32,512]{1,0:T(8,128)} fusion(f32[32,512]{1,0:T(8,128)S(1)} %get-tuple-element.40, bf16[32,512]{1,0:T(8,128)(2,1)S(1)} %collective-permute-done.6), kind=kLoop, calls=%fused_computation | loop fusion | flops 49152 | bytes 163840 | tf_op jit(solution)/shard_map/mul | solution.py:474
  (1 shorter events, 0.0 us)
Async XLA Ops:
  1.7 6.2 %collective-permute-start.2 = (bf16[272,128]{1,0:T(8,128)(2,1)S(1)}, bf16[272,128]{1,0:T(8,128)(2,1)S(1)}, u32[]{:S(2)}, u32[]{:S(2)}) collective-permute-start(bf16[272,128]{1,0:T(8,128)(2,1)S(1)} %get-tuple-element.24), channel_id=1, source_target_pairs={{0,2},{2,0},{1,3},{3,1},{4,6},{6,4},{5,7},{7,5},{8,10},{10,8},{9,1... | collective-permute-start | bytes 208904 | tf_op jit(solution)/shard_map/ppermute | solution.py:37
  1.9 6.0 %collective-permute-start.3 = (bf16[272,128]{1,0:T(8,128)(2,1)S(1)}, bf16[272,128]{1,0:T(8,128)(2,1)S(1)}, u32[]{:S(2)}, u32[]{:S(2)}) collective-permute-start(bf16[272,128]{1,0:T(8,128)(2,1)S(1)} %get-tuple-element.25), channel_id=1, source_target_pairs={{2,4},{4,2},{3,5},{5,3},{0,1},{1,0},{6,7},{7,6},{10,12},{12,10},{1... | collective-permute-start | bytes 208904 | tf_op jit(solution)/shard_map/ppermute | solution.py:37
  4.4 12.7 %collective-permute-start = (bf16[192,512]{1,0:T(8,128)(2,1)S(1)}, bf16[192,512]{1,0:T(8,128)(2,1)S(1)}, u32[]{:S(2)}, u32[]{:S(2)}) collective-permute-start(bf16[192,512]{1,0:T(8,128)(2,1)S(1)} %get-tuple-element.22), channel_id=1, source_target_pairs={{0,8},{8,0},{1,9},{9,1},{16,24},{24,16},{17,25},{25,17},{2,10},{10... | collective-permute-start | bytes 589832 | tf_op jit(solution)/shard_map/ppermute | solution.py:37
  4.6 12.4 %collective-permute-start.1 = (bf16[192,512]{1,0:T(8,128)(2,1)S(1)}, bf16[192,512]{1,0:T(8,128)(2,1)S(1)}, u32[]{:S(2)}, u32[]{:S(2)}) collective-permute-start(bf16[192,512]{1,0:T(8,128)(2,1)S(1)} %get-tuple-element.23), channel_id=1, source_target_pairs={{8,16},{16,8},{9,17},{17,9},{0,1},{1,0},{24,25},{25,24},{10,18},{1... | collective-permute-start | bytes 589832 | tf_op jit(solution)/shard_map/ppermute | solution.py:37
  8.1 5.4 %collective-permute-start.4 = (bf16[208,128]{1,0:T(8,128)(2,1)S(1)}, bf16[208,128]{1,0:T(8,128)(2,1)S(1)}, u32[]{:S(2)}, u32[]{:S(2)}) collective-permute-start(bf16[208,128]{1,0:T(8,128)(2,1)S(1)} %get-tuple-element.27), channel_id=1, source_target_pairs={{0,8},{8,0},{1,9},{9,1},{16,24},{24,16},{17,25},{25,17},{2,10},{10... | collective-permute-start | bytes 159752 | tf_op jit(solution)/shard_map/ppermute | solution.py:37
  8.7 8.3 %collective-permute-start.5 = (bf16[208,128]{1,0:T(8,128)(2,1)S(1)}, bf16[208,128]{1,0:T(8,128)(2,1)S(1)}, u32[]{:S(2)}, u32[]{:S(2)}) collective-permute-start(bf16[208,128]{1,0:T(8,128)(2,1)S(1)} %get-tuple-element.28), channel_id=1, source_target_pairs={{8,16},{16,8},{9,17},{17,9},{0,1},{1,0},{24,25},{25,24},{10,18},{1... | collective-permute-start | bytes 159752 | tf_op jit(solution)/shard_map/ppermute | solution.py:37
  21.3 3.0 %collective-permute-start.6 = (bf16[32,512]{1,0:T(8,128)(2,1)S(1)}, bf16[32,512]{1,0:T(8,128)(2,1)S(1)}, u32[]{:S(2)}, u32[]{:S(2)}) collective-permute-start(bf16[32,512]{1,0:T(8,128)(2,1)S(1)} %bitcast.5), channel_id=1, source_target_pairs={{0,1},{1,0},{2,3},{3,2},{4,5},{5,4},{6,7},{7,6},{8,9},{9,8},{10,11... | collective-permute-start | bytes 98312 | tf_op jit(solution)/shard_map/ppermute | solution.py:471

commit v3 on v0

v3 whole, which is shorter than its diff:
```python
import math

import jax
import jax.numpy as jnp
from jax import lax
from jax.experimental import pallas as pl
from jax.experimental.pallas import tpu as pltpu
from jax.sharding import PartitionSpec as P

TAPS = 33
DEPTHS = 3
HALF = TAPS // 2
HALO = DEPTHS * HALF
LANES = 128
MID = LANES // 2
OUT = LANES - 2 * HALF
WROWS = LANES + OUT
IDX_ROWS = 16
BF = jnp.bfloat16
F32 = jnp.float32
NT = (((1,), (1,)), ((), ()))
NN = (((1,), (0,)), ((), ()))
TN = (((0,), (0,)), ((), ()))


def dot(a, b, dims=NN):
    return lax.dot_general(a, b, dims, preferred_element_type=F32)


def pairs_of(axis, odd):
    count, groups = lax.axis_size(axis), lax.axis_size("freq")
    pairs, alone = [], list(range(count))
    for i in range(odd, count - 1, 2):
        alone.remove(i)
        alone.remove(i + 1)
        for g in range(groups):
            pairs += [(i * groups + g, (i + 1) * groups + g), ((i + 1) * groups + g, i * groups + g)]
    for i in alone:
        for g in range(0, groups - 1, 2):
            pairs += [(i * groups + g, i * groups + g + 1), (i * groups + g + 1, i * groups + g)]
    return pairs


def swaps(a, b, axis):
    a = lax.ppermute(a, (axis, "freq"), pairs_of(axis, 0))
    b = lax.ppermute(b, (axis, "freq"), pairs_of(axis, 1))
    return a, b


def is_even(axis):
    return lax.rem(lax.axis_index(axis), 2) == 0


def has_left(axis):
    return lax.axis_index(axis) > 0


def has_right(axis):
    return lax.axis_index(axis) < lax.axis_size(axis) - 1


def lane_of(shape):
    return lax.broadcasted_iota(jnp.int32, shape, len(shape) - 1)


def roll(cells, amount):
    amount = amount % LANES
    return pltpu.roll(cells, amount, 1) if amount else cells


def from_sides(a, b, axis):
    even = is_even(axis)
    return jnp.where(even, b, a), jnp.where(even, a, b)


def join(pieces):
    tile = None
    for cells, start, amount in pieces:
        moved = roll(cells, amount)
        tile = moved if start == 0 else jnp.where(lane_of(moved.shape) < start, tile, moved)
    return tile


def gather(blocks, first, valid=OUT):
    pieces, at = [], 0
    while at < LANES:
        k, lane = divmod(first + at, OUT)
        if k >= len(blocks):
            break
        pieces.append((blocks[k], at, at - lane))
        at += valid - lane
    return join(pieces)


def load_kernel(*refs):
    count = 5
    sources, targets = refs[:count], refs[count + 4:2 * count + 4]
    ma_ref, mb_ref, sa_ref, sb_ref = refs[count:count + 4]
    sem, wave_sem = refs[2 * count + 4:]
    wave, x_ref = sources[0], targets[0]
    planes, tiles, rows, _ = x_ref.shape
    first = []
    for p in range(planes):
        for t in range(tiles):
            piece = wave.at[p, :, pl.ds(t * LANES, LANES)]
            first.append(pltpu.make_async_copy(piece, x_ref.at[p, t], wave_sem.at[p, t]))
    others = [
        pltpu.make_async_copy(s, t, sem.at[i]) for i, (s, t) in enumerate(zip(sources[1:], targets[1:]))
    ]
    for copy in others[:1] + first + others[1:]:
        copy.start()
    for copy in first:
        copy.wait()
    even = is_even("src")
    low = rows - HALO
    at_a = pl.multiple_of(jnp.where(even, low, 0), 16)
    at_b = pl.multiple_of(jnp.where(even, 0, low), 16)
    lane = lane_of((HALO, LANES))
    for p in range(planes):
        for at, main, small in ((at_a, ma_ref, sa_ref), (at_b, mb_ref, sb_ref)):
            for t in range(tiles):
                main[p, t] = x_ref[p, t, pl.ds(at, HALO), :]
            head, tail = x_ref[p, 0, pl.ds(at, HALO), :], x_ref[p, tiles - 1, pl.ds(at, HALO), :]
            small[p * HALO:(p + 1) * HALO, :] = jnp.where(lane < MID, head, tail)
    others[0].wait()
    base = planes * HALO
    index = targets[1][...].astype(F32).astype(BF)
    for small in (sa_ref, sb_ref):
        small[base:base + IDX_ROWS, :] = jnp.zeros((IDX_ROWS, LANES), BF)
        small[base:base + DEPTHS, 0:rows] = index
    for copy in others[1:]:
        copy.wait()


def edge_kernel(x_ref, ridx_ref, sa_ref, sb_ref, ra_ref, rb_ref):
    planes, tiles, rows, _ = x_ref.shape
    freqs = planes // 2
    full = rows + 2 * HALO
    even = is_even("rec")
    ends = (ra_ref, rb_ref)
    for f in range(freqs):
        at = f * full
        for start, size, tail, head in (
            (0, rows, [x_ref[p, tiles - 1] for p in (f, freqs + f)], [x_ref[p, 0] for p in (f, freqs + f)]),
            (rows, HALO, *[[side_of(sa_ref, sb_ref, p, 0) for p in (f, freqs + f)]] * 2),
            (rows + HALO, HALO, *[[side_of(sa_ref, sb_ref, p, 1) for p in (f, freqs + f)]] * 2),
        ):
            lane = lane_of((size, LANES))
            right = jnp.where(lane < MID, roll(tail[1], MID), tail[0])
            left = jnp.where(lane < MID, head[0], roll(head[1], MID))
            place = slice(at + start, at + start + size)
            ends[0][place, :] = jnp.where(even, right, left)
            ends[1][place, :] = jnp.where(even, left, right)
    base = freqs * full
    cols = tiles * LANES
    head = ridx_ref[:, 0:LANES].astype(F32).astype(BF)
    tail = ridx_ref[:, cols - LANES:cols].astype(F32).astype(BF)
    for ref, value in zip(ends, (jnp.where(even, tail, head), jnp.where(even, head, tail))):
        ref[base:base + IDX_ROWS, :] = jnp.zeros((IDX_ROWS, LANES), BF)
        ref[base:base + DEPTHS, :] = value


def side_of(a_ref, b_ref, p, side):
    at = slice(p * HALO, (p + 1) * HALO)
    return from_sides(a_ref[at, :], b_ref[at, :], "src")[side]


def index_sides(a_ref, b_ref, base, axis):
    left, right = from_sides(a_ref[base:base + IDX_ROWS, :], b_ref[base:base + IDX_ROWS, :], axis)
    left = jnp.where(has_left(axis), left.astype(F32)[0:8], -1.0)
    right = jnp.where(has_right(axis), right.astype(F32)[0:8], -1.0)
    return left, right


def taps_of(index_tiles, table, entries):
    hot = [
        (lax.broadcasted_iota(jnp.int32, (entries, LANES), 0) == tile.astype(jnp.int32)).astype(F32).astype(BF)
        for tile in index_tiles
    ]
    return dot(hot[0] if len(hot) == 1 else jnp.concatenate(hot, axis=1), table, TN)


def skew(taps):
    return pltpu.roll(taps, 0, 1, stride=1, stride_axis=0)


def source_kernel(
    sa_ref, sb_ref, sidx_ref, table_ref, bins_ref, weight_ref, near_ref, mid_ref, far_ref, pair_ref, sx_ref, wt_ref
):
    rows, cols = bins_ref.shape
    freqs = near_ref.shape[0]
    tiles = cols // LANES
    table = table_ref[...]
    entries = table.shape[0]
    wt_ref[...] = jnp.zeros(wt_ref.shape, F32)
    wt_ref[0:DEPTHS, 0:weight_ref.shape[1]] = weight_ref[...]
    for t in range(tiles):
        bins = bins_ref[:, t * LANES:(t + 1) * LANES]
        for z in range(DEPTHS):
            row = jnp.broadcast_to(wt_ref[z:z + 1, :], (rows, LANES))
            pair_ref[z, t] = jnp.take_along_axis(row, bins, axis=1)
    left, right = index_sides(sa_ref, sb_ref, 2 * freqs * HALO, "src")
    sx_ref[...] = jnp.zeros(sx_ref.shape, F32)
    sx_ref[0:DEPTHS, 0:rows] = sidx_ref[...].astype(F32)
    reach = HALO - HALF
    index = join([(left, 0, reach - rows), (sx_ref[...], reach, reach), (right, reach + rows, reach + rows)])
    out = lax.broadcasted_iota(jnp.int32, (LANES, LANES), 0)
    lane = lane_of((LANES, LANES))
    ops = []
    for z in range(DEPTHS):
        taps = taps_of([roll(index, -z * HALF)[z:z + 1]], table, entries)
        found = []
        for part in range(2 * freqs):
            skewed = skew(taps[:, part * LANES:(part + 1) * LANES])
            found.append((jnp.where(lane >= out, skewed, 0.0), jnp.where(lane < out, skewed, 0.0)))
        ops.append(found)
    narrow = lane_of((rows, LANES))
    for f in range(freqs):
        s0 = [[tile.astype(BF) for tile in ops[0][2 * f + part]] for part in range(2)]
        s1 = [ops[1][2 * f + part][0].astype(BF) for part in range(2)]
        s2 = [ops[2][2 * f + part][0][:rows].astype(BF) for part in range(2)]
        got = dot(jnp.concatenate(s2, axis=0), jnp.concatenate(s1, axis=1))
        re = (got[:rows, :LANES] - got[rows:, LANES:]).astype(BF)
        im = (got[:rows, LANES:] + got[rows:, :LANES]).astype(BF)
        stack = jnp.concatenate([re, s1[0][HALF:HALF + rows], im, s1[1][HALF:HALF + rows]], axis=0)
        by_re = dot(stack, jnp.concatenate(s0[0], axis=1))
        by_im = dot(stack, jnp.concatenate(s0[1], axis=1))
        pr = by_re[:2 * rows] - by_im[2 * rows:]
        pi = by_im[:2 * rows] + by_re[2 * rows:]
        size = rows + 2 * HALF
        own = slice(reach, reach + rows)
        parts = [
            join([(ops[0][2 * f + part][0][own], 0, -reach), (ops[0][2 * f + part][1][own], LANES - reach, -reach)])
            for part in range(2)
        ]
        parts = [jnp.where(narrow < size, part, 0.0) for part in parts]
        minus = -parts[1]
        near_ref[f, :, 0:LANES] = jnp.where(narrow < size, parts[0], roll(minus, size)).astype(BF)
        near_ref[f, :, LANES:] = jnp.where(narrow < 2 * size - LANES, roll(minus, size), 0.0).astype(BF)
        mids = [
            join([(g[rows:, :LANES], 0, -HALF), (g[rows:, LANES:], LANES - HALF, -HALF)]) for g in (pr, pi)
        ]
        mid_ref[f, :, 0:LANES] = mids[0].astype(BF)
        mid_ref[f, :, LANES:] = (-mids[1]).astype(BF)
        re, im = pr[:rows].astype(BF), pi[:rows].astype(BF)
        far_ref[f, 0] = jnp.concatenate([re, im], axis=0)
        far_ref[f, 1] = jnp.concatenate([-im, re], axis=0)


def windows(own, left, right, blocks):
    tiles, found = len(own), []
    for b in range(blocks):
        first = b * OUT - HALO
        j, s = divmod(first, LANES)
        pieces = []
        if b == 0:
            pieces = [(left[0], 0, left[1]), (own[0], HALO, HALO)]
        else:
            pieces.append((own[j], 0, -s))
            if s and j + 1 < tiles:
                pieces.append((own[j + 1], LANES - s, -s))
            end = tiles * LANES - first
            if end < LANES:
                pieces.append((right[0], end, end + right[1]))
        found.append(join(pieces))
    return found


def receiver_steps(first, w_ref, freqs, rows, keep):
    source = first
    blocks = len(first[0])
    for z in range(DEPTHS):
        after = [[None] * blocks for _ in range(2 * freqs)]
        for b in range(blocks):
            for f in range(freqs):
                both = jnp.concatenate([source[f][b], source[freqs + f][b]], axis=1)
                w = jnp.concatenate([w_ref[z, b, f, 0], w_ref[z, b, f, 1]], axis=1)
                got = dot(both, w, NT)
                for p, lanes in ((f, got[:, :OUT]), (freqs + f, got[:, LANES:LANES + OUT])):
                    after[p][b] = jnp.concatenate([lanes, jnp.zeros((rows, LANES - OUT), F32)], axis=1).astype(BF)
        if z < DEPTHS - 1:
            lane = lane_of((rows, LANES))
            source = [
                [
                    jnp.where(lane < OUT, plane[b], roll(plane[b + 1], OUT)) if b + 1 < blocks else plane[b]
                    for b in range(blocks)
                ]
                for plane in after
            ]
        else:
            source = after
        for p in range(2 * freqs):
            for b in range(blocks):
                keep(z, p, b, source[p][b])


def halo_sides(ra_ref, rb_ref, at, part):
    left, right = from_sides(ra_ref[at, :], rb_ref[at, :], "rec")
    left = jnp.where(has_left("rec"), left, jnp.zeros_like(left))
    right = jnp.where(has_right("rec"), right, jnp.zeros_like(right))
    return (left, HALO + part * MID), (right, -part * MID)


def own_kernel(x_ref, ra_ref, rb_ref, ridx_ref, table_ref, w_ref, a_ref, widx_ref):
    planes, tiles, rows, _ = x_ref.shape
    freqs = planes // 2
    full = rows + 2 * HALO
    blocks = w_ref.shape[1]
    table = table_ref[...]
    entries = table.shape[0]
    left, right = index_sides(ra_ref, rb_ref, freqs * full, "rec")
    widx_ref[...] = jnp.zeros(widx_ref.shape, F32)
    widx_ref[0:DEPTHS, :] = ridx_ref[...].astype(F32)
    own = [widx_ref[:, t * LANES:(t + 1) * LANES] for t in range(tiles)]
    none = jnp.full((8, LANES), -1.0, F32)
    for z in range(DEPTHS):
        before = HALF * (DEPTHS - 1 - z)
        index = []
        for t in range(tiles + 1):
            pieces = []
            if before:
                pieces.append(((left, own[0])[min(t, 1)] if t < 2 else own[t - 1], 0, before))
            if t < tiles:
                pieces.append((own[t], before, before))
            else:
                if before:
                    pieces.append((right, before, before))
                pieces.append((none, 2 * before, 0))
            index.append(join(pieces)[z:z + 1])
        taps = taps_of(index, table, entries)
        for b in range(blocks):
            at = slice(b * OUT, (b + 1) * OUT)
            for f in range(freqs):
                re, im = (
                    skew(taps[at, part * LANES:(part + 1) * LANES]) for part in (2 * f, 2 * f + 1)
                )
                minus, re, im = (-im).astype(BF), re.astype(BF), im.astype(BF)
                for half, (top, low) in enumerate(((re, im), (minus, re))):
                    w_ref[z, b, f, half, 0:OUT, :] = top
                    w_ref[z, b, f, half, OUT:LANES, :] = jnp.zeros((LANES - OUT, LANES), BF)
                    w_ref[z, b, f, half, LANES:, :] = low
    first = []
    for p in range(planes):
        part, f = divmod(p, freqs)
        sides = halo_sides(ra_ref, rb_ref, slice(f * full, f * full + rows), part)
        first.append(windows([x_ref[p, t] for t in range(tiles)], *sides, blocks))

    def keep(z, p, b, value):
        a_ref[z, p, b] = value

    receiver_steps(first, w_ref, freqs, rows, keep)


def last_kernel(
    ma_ref, mb_ref, ra_ref, rb_ref, w_ref, own_ref, near_ref, mid_ref, far_ref, pair_ref,
    final_ref, send_ref, keep_ref, a_ref, part_ref,
):
    _, planes, blocks, rows, _ = own_ref.shape
    freqs = planes // 2
    tiles = pair_ref.shape[1]
    full = rows + 2 * HALO
    first = []
    for p in range(planes):
        part, f = divmod(p, freqs)
        main = []
        for t in range(tiles):
            left, right = from_sides(ma_ref[p, t], mb_ref[p, t], "src")
            left = jnp.where(has_left("src"), left, jnp.zeros_like(left))
            right = jnp.where(has_right("src"), right, jnp.zeros_like(right))
            main.append(jnp.concatenate([left, right], axis=0))
        at = f * full + rows
        sides = []
        for cells, amount in halo_sides(ra_ref, rb_ref, slice(at, at + 2 * HALO), part):
            top = jnp.where(has_left("src"), cells[:HALO], jnp.zeros_like(cells[:HALO]))
            low = jnp.where(has_right("src"), cells[HALO:], jnp.zeros_like(cells[HALO:]))
            sides.append((jnp.concatenate([top, low], axis=0), amount))
        first.append(windows(main, *sides, blocks))

    def keep(z, p, b, value):
        a_ref[z, p, b, 0:HALO] = value[:HALO]
        a_ref[z, p, b, HALO:HALO + rows] = own_ref[z, p, b]
        a_ref[z, p, b, HALO + rows:] = value[HALO:]

    receiver_steps(first, w_ref, freqs, 2 * HALO, keep)

    def field(z, p, b, reach):
        at = slice(HALO - reach, HALO + rows + reach)
        return jnp.concatenate([a_ref[z, p, b, at], a_ref[z, p, b + 1, at]], axis=1)

    images = []
    for z, ref in ((0, near_ref), (1, mid_ref)):
        reach = HALF * (z + 1)
        size = rows + 2 * reach
        out = []
        for b in range(0, blocks, 2):
            total = None
            for f in range(freqs):
                both = jnp.concatenate([field(z, f, b, reach), field(z, freqs + f, b, reach)], axis=0)
                term = dot(ref[f, :, 0:2 * size], both)
                total = term if total is None else total + term
            out += [total[:, :LANES], total[:, LANES:]]
        images.append([gather(out, t * LANES + HALF * (DEPTHS - 1 - z), LANES) for t in range(tiles)])
    real = [None] * tiles
    for f in range(freqs):
        out = []
        for b in range(0, blocks, 2):
            got = dot(far_ref[f, 0][:, :full], field(2, f, b, HALO))
            got += dot(far_ref[f, 1][:, :full], field(2, freqs + f, b, HALO))
            got = got.astype(BF)
            out += [got[:, :LANES], got[:, LANES:]]
        for t in range(tiles):
            both = gather(out, t * LANES)
            final_ref[f, :, t * LANES:(t + 1) * LANES] = both[:rows]
            final_ref[freqs + f, :, t * LANES:(t + 1) * LANES] = both[rows:]
            term = both[:rows].astype(F32)
            real[t] = term if real[t] is None else real[t] + term
    for t in range(tiles):
        value = pair_ref[DEPTHS - 1, t] * real[t]
        for z in range(DEPTHS - 1):
            value += pair_ref[z, t] * images[z][t]
        part_ref[:, t * LANES:(t + 1) * LANES] = value
    count = lax.axis_size("freq")
    share = rows // count
    me = lax.axis_index("freq")
    keep_ref[...] = part_ref[pl.ds(pl.multiple_of(me * share, 8), share), :]
    for j in range(1, count):
        there = partner(me, j, count)
        send_ref[j - 1] = part_ref[pl.ds(pl.multiple_of(there * share, 8), share), :].astype(BF)


def partner(me, j, count):
    if count & (count - 1) == 0:
        return me ^ j
    return (me + j) % count


def local_call(kernel, outs, scratch=(), flops=0, moved=0, vmem=16, **others):
    return pl.pallas_call(
        kernel,
        out_shape=[jax.ShapeDtypeStruct(s, d) for s, d in outs],
        scratch_shapes=[pltpu.VMEM(*s) if isinstance(s, tuple) else s for s in scratch],
        **others,
        compiler_params=pltpu.CompilerParams(vmem_limit_bytes=vmem << 20),
        cost_estimate=pl.CostEstimate(flops=flops, bytes_accessed=moved, transcendentals=0),
    )


def migrate(wave, tap_table, src_index, rec_index, offset_bin, bin_weight):
    freqs, rows, cols = wave.shape[1:]
    planes = 2 * freqs
    tiles = cols // LANES
    entries = tap_table.shape[1]
    count = lax.axis_size("freq")
    share = rows // count
    full = rows + 2 * HALO
    blocks = -(-(cols + 2 * (HALO - HALF)) // OUT)
    table = jnp.transpose(tap_table.astype(BF), (1, 2, 0, 3))
    table = jnp.pad(table, ((0, 0), (0, 0), (0, 0), (0, LANES - TAPS))).reshape(entries, planes * LANES)

    main = ((planes, tiles, HALO, LANES), BF)
    small = ((planes * HALO + IDX_ROWS, LANES), BF)
    inputs = (wave.reshape(planes, rows, cols), src_index, rec_index, offset_bin, bin_weight)
    inputs = tuple(pltpu.with_memory_space_constraint(a, pltpu.HBM) for a in inputs)
    ma, mb, sa, sb, x, src_index, rec_index, offset_bin, bin_weight = local_call(
        load_kernel,
        [main, main, small, small, ((planes, tiles, rows, LANES), BF)] + [(a.shape, a.dtype) for a in inputs[1:]],
        [pltpu.SemaphoreType.DMA((len(inputs) - 1,)), pltpu.SemaphoreType.DMA((planes, tiles))],
        moved=1 << 20,
        in_specs=[pl.BlockSpec(memory_space=pltpu.HBM)] * len(inputs),
    )(*inputs)
    sa, sb = swaps(sa, sb, "src")
    ma, mb = swaps(ma, mb, "src")
    edge = ((freqs * full + IDX_ROWS, LANES), BF)
    ra, rb = local_call(edge_kernel, [edge, edge], moved=1 << 18)(x, rec_index, sa, sb)
    ra, rb = swaps(ra, rb, "rec")

    near, mid, far, pair = local_call(
        source_kernel,
        [
            ((freqs, rows, 2 * LANES), BF),
            ((freqs, rows, 2 * LANES), BF),
            ((freqs, 2, 2 * rows, 2 * LANES), BF),
            ((DEPTHS, tiles, rows, LANES), F32),
        ],
        [((8, LANES), F32), ((8, LANES), F32)],
        flops=1 << 28,
        moved=2 << 20,
    )(sa, sb, src_index, table, offset_bin, bin_weight)
    w, own = local_call(
        own_kernel,
        [
            ((DEPTHS, blocks, freqs, 2, WROWS, LANES), BF),
            ((DEPTHS, planes, blocks, rows, LANES), BF),
        ],
        [((8, cols), F32)],
        flops=1 << 31,
        moved=5 << 20,
    )(x, ra, rb, rec_index, table)
    final, send, keep = local_call(
        last_kernel,
        [((planes, rows, cols), BF), ((max(count - 1, 1), share, cols), BF), ((share, cols), F32)],
        [((DEPTHS, planes, blocks, full, LANES), BF), ((rows, cols), F32)],
        flops=1 << 31,
        moved=8 << 20,
        vmem=24,
    )(ma, mb, ra, rb, w, own, near, mid, far, pair)
    total = keep
    for j in range(1, count):
        got = lax.ppermute(send[j - 1], "freq", [(i, partner(i, j, count)) for i in range(count)])
        total = total + got.astype(F32)
    scale = 1.0 / math.sqrt(freqs * count * DEPTHS)
    return final.reshape(wave.shape), total * scale


def solution(mesh):
    placed = (
        P(None, "freq", "src", "rec"),
        P(None, None, "freq", None),
        P(None, "src"),
        P(None, "rec"),
        P("src", "rec"),
        P(),
    )
    return jax.shard_map(
        migrate,
        mesh=mesh,
        in_specs=placed,
        out_specs=(P(None, "freq", "src", "rec"), P(("src", "freq"), "rec")),
        check_vma=False,
    )
```

time: 119 us -> 22.4 us (0.19)
  the two profiles are of different devices: /device:TPU:9 before, /device:TPU:21 now
where the time goes in v3:
time: 22.4 us; the launch traced here: 22.3 us
  starting transfers between devices  8.16 us (36%)
  Pallas kernels  7.08 us (32%)
  waiting for transfers between devices  4.54 us (20%)
  other arithmetic  1.55 us (7%)
  between operations  0.69 us (3%)
  local copies, waits for them, and re-layouts  0.23 us (1%)
    ppermute x3, waiting for transfers between devices, swaps(): b = lax.ppermute(b, (axis, 'freq'), pairs_of(axis, 1))  3.67 us
    ppermute x3, starting transfers between devices, swaps(): a = lax.ppermute(a, (axis, 'freq'), pairs_of(axis, 0))  3.65 us
    ppermute x1, starting transfers between devices, migrate(): lax.ppermute(send[j - 1], 'freq', [(i, partner(i, j, count)) for i in ran...  3.16 us
    pallas_call x1, Pallas kernels, migrate(): local_call(last_kernel, [((planes, rows, cols), BF), ((max(count - 1, 1),...  2.65 us
    pallas_call x1, Pallas kernels, migrate(): local_call(own_kernel, [((DEPTHS, blocks, freqs, 2, WROWS, LANES), BF), (...  2.08 us
    ppermute x3, starting transfers between devices, swaps(): b = lax.ppermute(b, (axis, 'freq'), pairs_of(axis, 1))  1.36 us
    pallas_call x1, Pallas kernels, migrate(): local_call(load_kernel, [main, main, small, small, ((planes, tiles, rows,...  1.27 us
    pallas_call x1, Pallas kernels, migrate(): local_call(source_kernel, [((freqs, rows, 2 * LANES), BF), ((freqs, rows,...  0.96 us
  transfers between devices with their start and end apart: 7, of which 4 were waited for; matrix products, arithmetic and copies ran while one was open for 5% of the time, Pallas kernels for 14%

profile of v3, /device:TPU:21, one launch (start us, length us, event | category | flops | bytes accessed | tf_op | source)
XLA Modules:
  0.0 22.3 jit_solution(7875103373184984428)
XLA Ops:
  0.6 1.3 %shard_map.77 = (bf16[4,4,48,128]{3,2,1,0:T(8,128)(2,1)S(1)}, bf16[4,4,48,128]{3,2,1,0:T(8,128)(2,1)S(1)}, bf16[208,128]{1,0:T(8,128)(2,1)S(1)}, bf16[208,128]{1...) custom-call(bf16[4,64,512]{2,1,0:T(8,128)(2,1)} %bitcast.6, ...), custom_call_target="tpu_custom_call" | custom-call | bytes 1048576 | tf_op jit(solution)/shard_map/pallas_call | solution.py:464
  1.9 1.3 %collective-permute-start.2 = (bf16[208,128]{1,0:T(8,128)(2,1)S(1)}, bf16[208,128]{1,0:T(8,128)(2,1)S(1)}, u32[]{:S(2)}, u32[]{:S(2)}) collective-permute-start(bf16[208,128]{1,0:T(8,128)(2,1)S(1)} %get-tuple-element.26), channel_id=1, source_target_pairs={{0,8},{8,0},{1,9},{9,1},{16,24},{24,16},{17,25},{25,17},{2,10},{10... | collective-permute-start | bytes 159752 | tf_op jit(solution)/shard_map/ppermute | solution.py:45
  3.2 0.2 collective-permute-start.3
  3.4 1.0 %collective-permute-start = (bf16[4,4,48,128]{3,2,1,0:T(8,128)(2,1)S(1)}, bf16[4,4,48,128]{3,2,1,0:T(8,128)(2,1)S(1)}, u32[]{:S(2)}, u32[]{:S(2)}) collective-permute-start(bf16[4,4,48,128]{3,2,1,0:T(8,128)(2,1)S(1)} %get-tuple-element.22), channel_id=1, source_target_pairs={{0,8},{8,0},{1,9},{9,1},{16,24},{24,16},{17,25},{25,17},{2,10},{10... | collective-permute-start | bytes 589832 | tf_op jit(solution)/shard_map/ppermute | solution.py:45
  4.4 1.2 %collective-permute-start.1 = (bf16[4,4,48,128]{3,2,1,0:T(8,128)(2,1)S(1)}, bf16[4,4,48,128]{3,2,1,0:T(8,128)(2,1)S(1)}, u32[]{:S(2)}, u32[]{:S(2)}) collective-permute-start(bf16[4,4,48,128]{3,2,1,0:T(8,128)(2,1)S(1)} %get-tuple-element.23), channel_id=1, source_target_pairs={{8,16},{16,8},{9,17},{17,9},{0,1},{1,0},{24,25},{25,24},{10,18},{1... | collective-permute-start | bytes 589832 | tf_op jit(solution)/shard_map/ppermute | solution.py:46
  5.6 0.0 collective-permute-done.2.sa_ref
  5.6 1.5 %collective-permute-done.3.sb_ref = bf16[208,128]{1,0:T(8,128)(2,1)S(1)} collective-permute-done((bf16[208,128]{1,0:T(8,128)(2,1)S(1)}, bf16[208,128]{1,0:T(8,128)(2,1)S(1)}, u32[]{:S(2)}, u32[]{:S(2)}) %collective-permute-start.3) | collective-permute-done | bytes 53280 | tf_op jit(solution)/shard_map/ppermute | solution.py:46
  7.1 0.1 shard_map.78
  7.2 1.4 %collective-permute-start.4 = (bf16[336,128]{1,0:T(8,128)(2,1)S(1)}, bf16[336,128]{1,0:T(8,128)(2,1)S(1)}, u32[]{:S(2)}, u32[]{:S(2)}) collective-permute-start(bf16[336,128]{1,0:T(8,128)(2,1)S(1)} %get-tuple-element.28), channel_id=1, source_target_pairs={{0,2},{2,0},{1,3},{3,1},{4,6},{6,4},{5,7},{7,5},{8,10},{10,8},{9,1... | collective-permute-start | bytes 258056 | tf_op jit(solution)/shard_map/ppermute | solution.py:45
  8.6 0.0 collective-permute-start.5
  8.6 0.9 %convert_bitcast_fusion = bf16[64,2,2,33]{0,1,3,2:T(2,128)(2,1)S(1)} fusion(f32[2,64,2,33]{1,2,3,0:T(2,128)} %param.7), kind=kLoop, calls=%fused_computation.1 | loop fusion | flops 8448 | bytes 50688 | tf_op jit(solution)/shard_map/transpose | solution.py:457
  9.5 0.1 copy.9
  9.6 0.1 pad.4.clone
  9.7 1.0 %shard_map.80 = (bf16[2,64,256]{2,1,0:T(8,128)(2,1)S(1)}, bf16[2,64,256]{2,1,0:T(8,128)(2,1)S(1)}, bf16[2,2,128,256]{3,2,1,0:T(8,128)(2,1)S(1)}, f32[3,4,64,128]{3,2,1,0:T(8,128)S(1)}) custom-call(bf16[208,128]{1,0:T(8,128)(2,1)S(1)} %collective-permute-done.2.sa_ref, bf16[208,128]{1,0:T(8,128)(2,1)S(1)} %collective-permute-done.3.sb_ref, ...), custom_call_target="tpu_custom_call" | custom-call | flops 268435456 | bytes 2097152 | tf_op jit(solution)/shard_map/pallas_call | solution.py:477
  10.7 0.0 collective-permute-done.4.ra_ref
  10.7 1.2 %collective-permute-done.5.rb_ref = bf16[336,128]{1,0:T(8,128)(2,1)S(1)} collective-permute-done((bf16[336,128]{1,0:T(8,128)(2,1)S(1)}, bf16[336,128]{1,0:T(8,128)(2,1)S(1)}, u32[]{:S(2)}, u32[]{:S(2)}) %collective-permute-start.5) | collective-permute-done | bytes 86048 | tf_op jit(solution)/shard_map/ppermute | solution.py:46
  11.9 2.1 %shard_map.79 = (bf16[3,6,2,2,224,128]{5,4,3,2,1,0:T(8,128)(2,1)S(1)}, bf16[3,4,6,64,128]{4,3,2,1,0:T(8,128)(2,1)S(1)}) custom-call(bf16[4,4,64,128]{3,2,1,0:T(8,128)(2,1)S(1)} %get-tuple-element.24.x_ref, bf16[336,128]{1,0:T(8,128)(2,1)S(1)} %collective-permute-done.4.ra_ref, bf16[336,128]{1,0:T(8,128)(2,1)S(1)} %collective-permute-done.5.rb_ref, ...), custom_call_target="tpu_custom_call" | custom-call | flops 2147483648 | bytes 5242880 | tf_op jit(solution)/shard_map/pallas_call | solution.py:489
  14.0 0.0 collective-permute-done.ma_ref
  14.0 1.0 %collective-permute-done.1.mb_ref = bf16[4,4,48,128]{3,2,1,0:T(8,128)(2,1)S(1)} collective-permute-done((bf16[4,4,48,128]{3,2,1,0:T(8,128)(2,1)S(1)}, bf16[4,4,48,128]{3,2,1,0:T(8,128)(2,1)S(1)}, u32[]{:S(2)}, u32[]{:S(2)}) %collective-permute-start.1) | collective-permute-done | bytes 196640 | tf_op jit(solution)/shard_map/ppermute | solution.py:46
  14.9 2.6 %shard_map.81 = (bf16[4,64,512]{2,1,0:T(8,128)(2,1)}, bf16[1,32,512]{2,1,0:T(8,128)(2,1)S(1)}, f32[32,512]{1,0:T(8,128)S(1)}) custom-call(bf16[4,4,48,128]{3,2,1,0:T(8,128)(2,1)S(1)} %collective-permute-done.ma_ref, bf16[4,4,48,128]{3,2,1,0:T(8,128)(2,1)S(1)} %collective-permute-done.1.mb_ref, bf16[336,128]{1,0:T(8,128)(2,1)S(1)} %collective-permute-done.4.ra_ref, ...), custom_call_target="tpu_custom_call" | custom-call | flops 2147483648 | bytes 8388608 | tf_op jit(solution)/shard_map/pallas_call | solution.py:499
  17.6 3.2 %collective-permute-start.6 = (bf16[32,512]{1,0:T(8,128)(2,1)S(1)}, bf16[32,512]{1,0:T(8,128)(2,1)S(1)}, u32[]{:S(2)}, u32[]{:S(2)}) collective-permute-start(bf16[32,512]{1,0:T(8,128)(2,1)S(1)} %bitcast.5), channel_id=1, source_target_pairs={{0,1},{1,0},{2,3},{3,2},{4,5},{5,4},{6,7},{7,6},{8,9},{9,8},{10,11... | collective-permute-start | bytes 98312 | tf_op jit(solution)/shard_map/ppermute | solution.py:509
  20.8 0.9 %collective-permute-done.6 = bf16[32,512]{1,0:T(8,128)(2,1)S(1)} collective-permute-done((bf16[32,512]{1,0:T(8,128)(2,1)S(1)}, bf16[32,512]{1,0:T(8,128)(2,1)S(1)}, u32[]{:S(2)}, u32[]{:S(2)}) %collective-permute-start.6) | collective-permute-done | bytes 32800 | tf_op jit(solution)/shard_map/ppermute | solution.py:509
  21.6 0.6 %add_multiply_fusion = f32[32,512]{1,0:T(8,128)} fusion(f32[32,512]{1,0:T(8,128)S(1)} %get-tuple-element.40, bf16[32,512]{1,0:T(8,128)(2,1)S(1)} %collective-permute-done.6), kind=kLoop, calls=%fused_computation | loop fusion | flops 49152 | bytes 163840 | tf_op jit(solution)/shard_map/mul | solution.py:512
  (1 shorter events, 0.0 us)
Async XLA Ops:
  1.9 3.6 %collective-permute-start.2 = (bf16[208,128]{1,0:T(8,128)(2,1)S(1)}, bf16[208,128]{1,0:T(8,128)(2,1)S(1)}, u32[]{:S(2)}, u32[]{:S(2)}) collective-permute-start(bf16[208,128]{1,0:T(8,128)(2,1)S(1)} %get-tuple-element.26), channel_id=1, source_target_pairs={{0,8},{8,0},{1,9},{9,1},{16,24},{24,16},{17,25},{25,17},{2,10},{10... | collective-permute-start | bytes 159752 | tf_op jit(solution)/shard_map/ppermute | solution.py:45
  3.2 3.9 %collective-permute-start.3 = (bf16[208,128]{1,0:T(8,128)(2,1)S(1)}, bf16[208,128]{1,0:T(8,128)(2,1)S(1)}, u32[]{:S(2)}, u32[]{:S(2)}) collective-permute-start(bf16[208,128]{1,0:T(8,128)(2,1)S(1)} %get-tuple-element.27), channel_id=1, source_target_pairs={{8,16},{16,8},{9,17},{17,9},{0,1},{1,0},{24,25},{25,24},{10,18},{1... | collective-permute-start | bytes 159752 | tf_op jit(solution)/shard_map/ppermute | solution.py:46
  3.4 10.6 %collective-permute-start = (bf16[4,4,48,128]{3,2,1,0:T(8,128)(2,1)S(1)}, bf16[4,4,48,128]{3,2,1,0:T(8,128)(2,1)S(1)}, u32[]{:S(2)}, u32[]{:S(2)}) collective-permute-start(bf16[4,4,48,128]{3,2,1,0:T(8,128)(2,1)S(1)} %get-tuple-element.22), channel_id=1, source_target_pairs={{0,8},{8,0},{1,9},{9,1},{16,24},{24,16},{17,25},{25,17},{2,10},{10... | collective-permute-start | bytes 589832 | tf_op jit(solution)/shard_map/ppermute | solution.py:45
  4.4 10.5 %collective-permute-start.1 = (bf16[4,4,48,128]{3,2,1,0:T(8,128)(2,1)S(1)}, bf16[4,4,48,128]{3,2,1,0:T(8,128)(2,1)S(1)}, u32[]{:S(2)}, u32[]{:S(2)}) collective-permute-start(bf16[4,4,48,128]{3,2,1,0:T(8,128)(2,1)S(1)} %get-tuple-element.23), channel_id=1, source_target_pairs={{8,16},{16,8},{9,17},{17,9},{0,1},{1,0},{24,25},{25,24},{10,18},{1... | collective-permute-start | bytes 589832 | tf_op jit(solution)/shard_map/ppermute | solution.py:46
  7.2 3.5 %collective-permute-start.4 = (bf16[336,128]{1,0:T(8,128)(2,1)S(1)}, bf16[336,128]{1,0:T(8,128)(2,1)S(1)}, u32[]{:S(2)}, u32[]{:S(2)}) collective-permute-start(bf16[336,128]{1,0:T(8,128)(2,1)S(1)} %get-tuple-element.28), channel_id=1, source_target_pairs={{0,2},{2,0},{1,3},{3,1},{4,6},{6,4},{5,7},{7,5},{8,10},{10,8},{9,1... | collective-permute-start | bytes 258056 | tf_op jit(solution)/shard_map/ppermute | solution.py:45
  8.6 3.3 %collective-permute-start.5 = (bf16[336,128]{1,0:T(8,128)(2,1)S(1)}, bf16[336,128]{1,0:T(8,128)(2,1)S(1)}, u32[]{:S(2)}, u32[]{:S(2)}) collective-permute-start(bf16[336,128]{1,0:T(8,128)(2,1)S(1)} %get-tuple-element.29), channel_id=1, source_target_pairs={{2,4},{4,2},{3,5},{5,3},{0,1},{1,0},{6,7},{7,6},{10,12},{12,10},{1... | collective-permute-start | bytes 258056 | tf_op jit(solution)/shard_map/ppermute | solution.py:46
  17.6 4.0 %collective-permute-start.6 = (bf16[32,512]{1,0:T(8,128)(2,1)S(1)}, bf16[32,512]{1,0:T(8,128)(2,1)S(1)}, u32[]{:S(2)}, u32[]{:S(2)}) collective-permute-start(bf16[32,512]{1,0:T(8,128)(2,1)S(1)} %bitcast.5), channel_id=1, source_target_pairs={{0,1},{1,0},{2,3},{3,2},{4,5},{5,4},{6,7},{7,6},{8,9},{9,8},{10,11... | collective-permute-start | bytes 98312 | tf_op jit(solution)/shard_map/ppermute | solution.py:509

commit v4 on v3

--- a/solution.py
+++ b/solution.py
@@ -20,7 +20,7 @@
 F32 = jnp.float32
 NT = (((1,), (1,)), ((), ()))
 NN = (((1,), (0,)), ((), ()))
-TN = (((0,), (0,)), ((), ()))
+TT = (((0,), (1,)), ((), ()))
 
 
 def dot(a, b, dims=NN):
@@ -93,71 +93,71 @@
 
 
 def load_kernel(*refs):
-    count = 5
+    count = 6
     sources, targets = refs[:count], refs[count + 4:2 * count + 4]
     ma_ref, mb_ref, sa_ref, sb_ref = refs[count:count + 4]
-    sem, wave_sem = refs[2 * count + 4:]
-    wave, x_ref = sources[0], targets[0]
-    planes, tiles, rows, _ = x_ref.shape
-    first = []
-    for p in range(planes):
-        for t in range(tiles):
-            piece = wave.at[p, :, pl.ds(t * LANES, LANES)]
-            first.append(pltpu.make_async_copy(piece, x_ref.at[p, t], wave_sem.at[p, t]))
-    others = [
-        pltpu.make_async_copy(s, t, sem.at[i]) for i, (s, t) in enumerate(zip(sources[1:], targets[1:]))
-    ]
-    for copy in others[:1] + first + others[1:]:
+    sem = refs[2 * count + 4]
+    copies = [pltpu.make_async_copy(s, t, sem.at[i]) for i, (s, t) in enumerate(zip(sources, targets))]
+    for copy in copies:
         copy.start()
-    for copy in first:
-        copy.wait()
+    x_ref, sidx_ref = targets[:2]
+    planes, rows, cols = x_ref.shape
     even = is_even("src")
     low = rows - HALO
     at_a = pl.multiple_of(jnp.where(even, low, 0), 16)
     at_b = pl.multiple_of(jnp.where(even, 0, low), 16)
     lane = lane_of((HALO, LANES))
-    for p in range(planes):
-        for at, main, small in ((at_a, ma_ref, sa_ref), (at_b, mb_ref, sb_ref)):
-            for t in range(tiles):
-                main[p, t] = x_ref[p, t, pl.ds(at, HALO), :]
-            head, tail = x_ref[p, 0, pl.ds(at, HALO), :], x_ref[p, tiles - 1, pl.ds(at, HALO), :]
-            small[p * HALO:(p + 1) * HALO, :] = jnp.where(lane < MID, head, tail)
-    others[0].wait()
     base = planes * HALO
-    index = targets[1][...].astype(F32).astype(BF)
+    copies[1].wait()
+    index = sidx_ref[...].astype(F32).astype(BF)
     for small in (sa_ref, sb_ref):
         small[base:base + IDX_ROWS, :] = jnp.zeros((IDX_ROWS, LANES), BF)
         small[base:base + DEPTHS, 0:rows] = index
-    for copy in others[1:]:
+    copies[0].wait()
+    for p in range(planes):
+        for at, main, small in ((at_a, ma_ref, sa_ref), (at_b, mb_ref, sb_ref)):
+            tiles = [x_ref[p, pl.ds(at, HALO), t:t + LANES] for t in range(0, cols, LANES)]
+            for t, tile in enumerate(tiles):
+                main[p, t] = tile
+            small[p * HALO:(p + 1) * HALO, :] = jnp.where(lane < MID, tiles[0], tiles[-1])
+    for copy in copies[2:]:
         copy.wait()
 
 
-def edge_kernel(x_ref, ridx_ref, sa_ref, sb_ref, ra_ref, rb_ref):
-    planes, tiles, rows, _ = x_ref.shape
+def put_edges(ends, at, tail, head):
+    lane = lane_of(tail[0].shape)
+    right = jnp.where(lane < MID, roll(tail[1], MID), tail[0])
+    left = jnp.where(lane < MID, head[0], roll(head[1], MID))
+    even = is_even("rec")
+    place = slice(at, at + right.shape[0])
+    ends[0][place, :] = jnp.where(even, right, left)
+    ends[1][place, :] = jnp.where(even, left, right)
+
+
+def near_kernel(x_ref, ridx_ref, ra_ref, rb_ref):
+    planes, rows, cols = x_ref.shape
     freqs = planes // 2
-    full = rows + 2 * HALO
+    ends = (ra_ref, rb_ref)
+    last = cols - LANES
+    for f in range(freqs):
+        tail = [x_ref[p, :, last:] for p in (f, freqs + f)]
+        head = [x_ref[p, :, :LANES] for p in (f, freqs + f)]
+        put_edges(ends, f * rows, tail, head)
+    base = freqs * rows
+    head = ridx_ref[:, :LANES].astype(F32).astype(BF)
+    tail = ridx_ref[:, last:].astype(F32).astype(BF)
     even = is_even("rec")
-    ends = (ra_ref, rb_ref)
-    for f in range(freqs):
-        at = f * full
-        for start, size, tail, head in (
-            (0, rows, [x_ref[p, tiles - 1] for p in (f, freqs + f)], [x_ref[p, 0] for p in (f, freqs + f)]),
-            (rows, HALO, *[[side_of(sa_ref, sb_ref, p, 0) for p in (f, freqs + f)]] * 2),
-            (rows + HALO, HALO, *[[side_of(sa_ref, sb_ref, p, 1) for p in (f, freqs + f)]] * 2),
-        ):
-            lane = lane_of((size, LANES))
-            right = jnp.where(lane < MID, roll(tail[1], MID), tail[0])
-            left = jnp.where(lane < MID, head[0], roll(head[1], MID))
-            place = slice(at + start, at + start + size)
-            ends[0][place, :] = jnp.where(even, right, left)
-            ends[1][place, :] = jnp.where(even, left, right)
-    base = freqs * full
-    cols = tiles * LANES
-    head = ridx_ref[:, 0:LANES].astype(F32).astype(BF)
-    tail = ridx_ref[:, cols - LANES:cols].astype(F32).astype(BF)
     for ref, value in zip(ends, (jnp.where(even, tail, head), jnp.where(even, head, tail))):
         ref[base:base + IDX_ROWS, :] = jnp.zeros((IDX_ROWS, LANES), BF)
         ref[base:base + DEPTHS, :] = value
+
+
+def edge_kernel(sa_ref, sb_ref, ra_ref, rb_ref):
+    freqs = ra_ref.shape[0] // (2 * HALO)
+    for f in range(freqs):
+        for side in range(2):
+            both = [side_of(sa_ref, sb_ref, p, side) for p in (f, freqs + f)]
+            put_edges((ra_ref, rb_ref), (2 * f + side) * HALO, both, both)
 
 
 def side_of(a_ref, b_ref, p, side):
@@ -177,7 +177,7 @@
         (lax.broadcasted_iota(jnp.int32, (entries, LANES), 0) == tile.astype(jnp.int32)).astype(F32).astype(BF)
         for tile in index_tiles
     ]
-    return dot(hot[0] if len(hot) == 1 else jnp.concatenate(hot, axis=1), table, TN)
+    return dot(hot[0] if len(hot) == 1 else jnp.concatenate(hot, axis=1), table, TT)
 
 
 def skew(taps):
@@ -185,13 +185,19 @@
 
 
 def source_kernel(
-    sa_ref, sb_ref, sidx_ref, table_ref, bins_ref, weight_ref, near_ref, mid_ref, far_ref, pair_ref, sx_ref, wt_ref
+    sa_ref, sb_ref, sidx_ref, taps_ref, bins_ref, weight_ref,
+    near_ref, mid_ref, far_ref, pair_ref, table_ref, sx_ref, wt_ref,
 ):
     rows, cols = bins_ref.shape
     freqs = near_ref.shape[0]
     tiles = cols // LANES
+    for f in range(freqs):
+        for part in range(2):
+            at = (2 * f + part) * LANES
+            table_ref[at:at + LANES, :] = jnp.zeros((LANES, table_ref.shape[1]), BF)
+            table_ref[at:at + TAPS, :] = taps_ref[part, :, f, :].astype(BF)
     table = table_ref[...]
-    entries = table.shape[0]
+    entries = table.shape[1]
     wt_ref[...] = jnp.zeros(wt_ref.shape, F32)
     wt_ref[0:DEPTHS, 0:weight_ref.shape[1]] = weight_ref[...]
     for t in range(tiles):
@@ -302,13 +308,13 @@
 
 
 def own_kernel(x_ref, ra_ref, rb_ref, ridx_ref, table_ref, w_ref, a_ref, widx_ref):
-    planes, tiles, rows, _ = x_ref.shape
+    planes, rows, cols = x_ref.shape
+    tiles = cols // LANES
     freqs = planes // 2
-    full = rows + 2 * HALO
     blocks = w_ref.shape[1]
     table = table_ref[...]
-    entries = table.shape[0]
-    left, right = index_sides(ra_ref, rb_ref, freqs * full, "rec")
+    entries = table.shape[1]
+    left, right = index_sides(ra_ref, rb_ref, freqs * rows, "rec")
     widx_ref[...] = jnp.zeros(widx_ref.shape, F32)
     widx_ref[0:DEPTHS, :] = ridx_ref[...].astype(F32)
     own = [widx_ref[:, t * LANES:(t + 1) * LANES] for t in range(tiles)]
@@ -342,8 +348,8 @@
     first = []
     for p in range(planes):
         part, f = divmod(p, freqs)
-        sides = halo_sides(ra_ref, rb_ref, slice(f * full, f * full + rows), part)
-        first.append(windows([x_ref[p, t] for t in range(tiles)], *sides, blocks))
+        sides = halo_sides(ra_ref, rb_ref, slice(f * rows, (f + 1) * rows), part)
+        first.append(windows([x_ref[p, :, t:t + LANES] for t in range(0, cols, LANES)], *sides, blocks))
 
     def keep(z, p, b, value):
         a_ref[z, p, b] = value
@@ -351,9 +357,9 @@
     receiver_steps(first, w_ref, freqs, rows, keep)
 
 
-def last_kernel(
+def image_kernel(
     ma_ref, mb_ref, ra_ref, rb_ref, w_ref, own_ref, near_ref, mid_ref, far_ref, pair_ref,
-    final_ref, send_ref, keep_ref, a_ref, part_ref,
+    send_ref, keep_ref, deep_ref, a_ref, part_ref,
 ):
     _, planes, blocks, rows, _ = own_ref.shape
     freqs = planes // 2
@@ -368,24 +374,27 @@
             left = jnp.where(has_left("src"), left, jnp.zeros_like(left))
             right = jnp.where(has_right("src"), right, jnp.zeros_like(right))
             main.append(jnp.concatenate([left, right], axis=0))
-        at = f * full + rows
         sides = []
-        for cells, amount in halo_sides(ra_ref, rb_ref, slice(at, at + 2 * HALO), part):
+        for cells, amount in halo_sides(ra_ref, rb_ref, slice(2 * f * HALO, 2 * (f + 1) * HALO), part):
             top = jnp.where(has_left("src"), cells[:HALO], jnp.zeros_like(cells[:HALO]))
             low = jnp.where(has_right("src"), cells[HALO:], jnp.zeros_like(cells[HALO:]))
             sides.append((jnp.concatenate([top, low], axis=0), amount))
         first.append(windows(main, *sides, blocks))
 
+    def place(z, p, b):
+        return deep_ref.at[p, b] if z == DEPTHS - 1 else a_ref.at[z, p, b]
+
     def keep(z, p, b, value):
-        a_ref[z, p, b, 0:HALO] = value[:HALO]
-        a_ref[z, p, b, HALO:HALO + rows] = own_ref[z, p, b]
-        a_ref[z, p, b, HALO + rows:] = value[HALO:]
+        to = place(z, p, b)
+        to[0:HALO] = value[:HALO]
+        to[HALO:HALO + rows] = own_ref[z, p, b]
+        to[HALO + rows:] = value[HALO:]
 
     receiver_steps(first, w_ref, freqs, 2 * HALO, keep)
 
     def field(z, p, b, reach):
         at = slice(HALO - reach, HALO + rows + reach)
-        return jnp.concatenate([a_ref[z, p, b, at], a_ref[z, p, b + 1, at]], axis=1)
+        return jnp.concatenate([place(z, p, b)[at], place(z, p, b + 1)[at]], axis=1)
 
     images = []
     for z, ref in ((0, near_ref), (1, mid_ref)):
@@ -400,20 +409,16 @@
                 total = term if total is None else total + term
             out += [total[:, :LANES], total[:, LANES:]]
         images.append([gather(out, t * LANES + HALF * (DEPTHS - 1 - z), LANES) for t in range(tiles)])
-    real = [None] * tiles
-    for f in range(freqs):
-        out = []
-        for b in range(0, blocks, 2):
-            got = dot(far_ref[f, 0][:, :full], field(2, f, b, HALO))
-            got += dot(far_ref[f, 1][:, :full], field(2, freqs + f, b, HALO))
-            got = got.astype(BF)
-            out += [got[:, :LANES], got[:, LANES:]]
-        for t in range(tiles):
-            both = gather(out, t * LANES)
-            final_ref[f, :, t * LANES:(t + 1) * LANES] = both[:rows]
-            final_ref[freqs + f, :, t * LANES:(t + 1) * LANES] = both[rows:]
-            term = both[:rows].astype(F32)
-            real[t] = term if real[t] is None else real[t] + term
+    real = [None] * blocks
+    for b in range(0, blocks, 2):
+        for f in range(freqs):
+            got = dot(far_ref[f, 0][:rows, :full], field(2, f, b, HALO))
+            got += dot(far_ref[f, 1][:rows, :full], field(2, freqs + f, b, HALO))
+            got = got.astype(BF).astype(F32)
+            for k in range(2):
+                term = got[:, k * LANES:(k + 1) * LANES]
+                real[b + k] = term if real[b + k] is None else real[b + k] + term
+    real = [gather(real, t * LANES) for t in range(tiles)]
     for t in range(tiles):
         value = pair_ref[DEPTHS - 1, t] * real[t]
         for z in range(DEPTHS - 1):
@@ -428,6 +433,23 @@
         send_ref[j - 1] = part_ref[pl.ds(pl.multiple_of(there * share, 8), share), :].astype(BF)
 
 
+def final_kernel(deep_ref, far_ref, final_ref):
+    planes, blocks, full, _ = deep_ref.shape
+    _, rows, cols = final_ref.shape
+    freqs = planes // 2
+    for f in range(freqs):
+        out = []
+        for b in range(0, blocks, 2):
+            parts = [jnp.concatenate([deep_ref[p, b], deep_ref[p, b + 1]], axis=1) for p in (f, freqs + f)]
+            got = dot(far_ref[f, 0][:, :full], parts[0]) + dot(far_ref[f, 1][:, :full], parts[1])
+            got = got.astype(BF)
+            out += [got[:, :LANES], got[:, LANES:]]
+        for t in range(0, cols, LANES):
+            both = gather(out, t)
+            final_ref[f, :, t:t + LANES] = both[:rows]
+            final_ref[freqs + f, :, t:t + LANES] = both[rows:]
+
+
 def partner(me, j, count):
     if count & (count - 1) == 0:
         return me ^ j
@@ -454,38 +476,40 @@
     share = rows // count
     full = rows + 2 * HALO
     blocks = -(-(cols + 2 * (HALO - HALF)) // OUT)
-    table = jnp.transpose(tap_table.astype(BF), (1, 2, 0, 3))
-    table = jnp.pad(table, ((0, 0), (0, 0), (0, 0), (0, LANES - TAPS))).reshape(entries, planes * LANES)
 
     main = ((planes, tiles, HALO, LANES), BF)
     small = ((planes * HALO + IDX_ROWS, LANES), BF)
-    inputs = (wave.reshape(planes, rows, cols), src_index, rec_index, offset_bin, bin_weight)
+    inputs = (wave.reshape(planes, rows, cols), src_index, rec_index, jnp.transpose(tap_table, (0, 3, 2, 1)), offset_bin, bin_weight)
     inputs = tuple(pltpu.with_memory_space_constraint(a, pltpu.HBM) for a in inputs)
-    ma, mb, sa, sb, x, src_index, rec_index, offset_bin, bin_weight = local_call(
+    ma, mb, sa, sb, x, src_index, rec_index, tap_table, offset_bin, bin_weight = local_call(
         load_kernel,
-        [main, main, small, small, ((planes, tiles, rows, LANES), BF)] + [(a.shape, a.dtype) for a in inputs[1:]],
-        [pltpu.SemaphoreType.DMA((len(inputs) - 1,)), pltpu.SemaphoreType.DMA((planes, tiles))],
+        [main, main, small, small] + [(a.shape, a.dtype) for a in inputs],
+        [pltpu.SemaphoreType.DMA((len(inputs),))],
         moved=1 << 20,
         in_specs=[pl.BlockSpec(memory_space=pltpu.HBM)] * len(inputs),
     )(*inputs)
     sa, sb = swaps(sa, sb, "src")
     ma, mb = swaps(ma, mb, "src")
-    edge = ((freqs * full + IDX_ROWS, LANES), BF)
-    ra, rb = local_call(edge_kernel, [edge, edge], moved=1 << 18)(x, rec_index, sa, sb)
+    near = ((freqs * rows + IDX_ROWS, LANES), BF)
+    ra, rb = local_call(near_kernel, [near, near], moved=1 << 16)(x, rec_index)
     ra, rb = swaps(ra, rb, "rec")
-
-    near, mid, far, pair = local_call(
+    edge = ((freqs * 2 * HALO, LANES), BF)
+    ea, eb = local_call(edge_kernel, [edge, edge], moved=1 << 16)(sa, sb)
+    ea, eb = swaps(ea, eb, "rec")
+
+    near, mid, far, pair, table = local_call(
         source_kernel,
         [
             ((freqs, rows, 2 * LANES), BF),
             ((freqs, rows, 2 * LANES), BF),
             ((freqs, 2, 2 * rows, 2 * LANES), BF),
             ((DEPTHS, tiles, rows, LANES), F32),
+            ((planes * LANES, entries), BF),
         ],
         [((8, LANES), F32), ((8, LANES), F32)],
         flops=1 << 28,
         moved=2 << 20,
-    )(sa, sb, src_index, table, offset_bin, bin_weight)
+    )(sa, sb, src_index, tap_table, offset_bin, bin_weight)
     w, own = local_call(
         own_kernel,
         [
@@ -496,18 +520,23 @@
         flops=1 << 31,
         moved=5 << 20,
     )(x, ra, rb, rec_index, table)
-    final, send, keep = local_call(
-        last_kernel,
-        [((planes, rows, cols), BF), ((max(count - 1, 1), share, cols), BF), ((share, cols), F32)],
-        [((DEPTHS, planes, blocks, full, LANES), BF), ((rows, cols), F32)],
+    send, keep, deep = local_call(
+        image_kernel,
+        [
+            ((max(count - 1, 1), share, cols), BF),
+            ((share, cols), F32),
+            ((planes, blocks, full, LANES), BF),
+        ],
+        [((DEPTHS - 1, planes, blocks, full, LANES), BF), ((rows, cols), F32)],
         flops=1 << 31,
         moved=8 << 20,
         vmem=24,
-    )(ma, mb, ra, rb, w, own, near, mid, far, pair)
+    )(ma, mb, ea, eb, w, own, near, mid, far, pair)
     total = keep
     for j in range(1, count):
         got = lax.ppermute(send[j - 1], "freq", [(i, partner(i, j, count)) for i in range(count)])
         total = total + got.astype(F32)
+    (final,) = local_call(final_kernel, [((planes, rows, cols), BF)], flops=1 << 28, moved=1 << 20)(deep, far)
     scale = 1.0 / math.sqrt(freqs * count * DEPTHS)
     return final.reshape(wave.shape), total * scale
 

time: 22.4 us -> 22.3 us (level)
  the two profiles are of different devices: /device:TPU:21 before, /device:TPU:5 now
where the time goes in v4:
time: 22.3 us; the launch traced here: 22.1 us
  starting transfers between devices  10.7 us (48%)
  Pallas kernels  7.42 us (33%)
  waiting for transfers between devices  2.64 us (12%)
  between operations  0.7 us (3%)
  other arithmetic  0.64 us (3%)
    ppermute x4, starting transfers between devices, swaps(): b = lax.ppermute(b, (axis, 'freq'), pairs_of(axis, 1))  6.13 us
    ppermute x4, starting transfers between devices, swaps(): a = lax.ppermute(a, (axis, 'freq'), pairs_of(axis, 0))  3.96 us
    ppermute x4, waiting for transfers between devices, swaps(): b = lax.ppermute(b, (axis, 'freq'), pairs_of(axis, 1))  2.63 us
    pallas_call x1, Pallas kernels, migrate(): local_call(own_kernel, [((DEPTHS, blocks, freqs, 2, WROWS, LANES), BF), (...  2.17 us
    pallas_call x1, Pallas kernels, migrate(): local_call(image_kernel, [((max(count - 1, 1), share, cols), BF), ((share...  1.86 us
    pallas_call x1, Pallas kernels, migrate(): local_call(final_kernel, [((planes, rows, cols), BF)], flops=1 << 28, mov...  1.13 us
    pallas_call x1, Pallas kernels, migrate(): local_call(load_kernel, [main, main, small, small] + [(a.shape, a.dtype)...  1.11 us
    pallas_call x1, Pallas kernels, migrate(): local_call(source_kernel, [((freqs, rows, 2 * LANES), BF), ((freqs, rows,...  0.96 us
  transfers between devices with their start and end apart: 9, of which 1 were waited for; matrix products, arithmetic and copies ran while one was open for 0% of the time, Pallas kernels for 20%

profile of v4, /device:TPU:5, one launch (start us, length us, event | category | flops | bytes accessed | tf_op | source)
XLA Modules:
  0.0 22.1 jit_solution(2973869251650698934)
XLA Ops:
  0.6 1.1 %shard_map.77 = (bf16[4,4,48,128]{3,2,1,0:T(8,128)(2,1)S(1)}, bf16[4,4,48,128]{3,2,1,0:T(8,128)(2,1)S(1)}, bf16[208,128]{1,0:T(8,128)(2,1)S(1)}, bf16[208,128]{1...) custom-call(bf16[4,64,512]{2,1,0:T(8,128)(2,1)} %bitcast.5, ...), custom_call_target="tpu_custom_call" | custom-call | bytes 1048576 | tf_op jit(solution)/shard_map/pallas_call | solution.py:484
  1.7 1.3 %collective-permute-start.2 = (bf16[208,128]{1,0:T(8,128)(2,1)S(1)}, bf16[208,128]{1,0:T(8,128)(2,1)S(1)}, u32[]{:S(2)}, u32[]{:S(2)}) collective-permute-start(bf16[208,128]{1,0:T(8,128)(2,1)S(1)} %get-tuple-element.28), channel_id=1, source_target_pairs={{0,8},{8,0},{1,9},{9,1},{16,24},{24,16},{17,25},{25,17},{2,10},{10... | collective-permute-start | bytes 159752 | tf_op jit(solution)/shard_map/ppermute | solution.py:45
  3.0 0.0 collective-permute-start.3
  3.0 0.1 shard_map.79
  3.1 1.5 %collective-permute-start.6 = (bf16[144,128]{1,0:T(8,128)(2,1)S(1)}, bf16[144,128]{1,0:T(8,128)(2,1)S(1)}, u32[]{:S(2)}, u32[]{:S(2)}) collective-permute-start(bf16[144,128]{1,0:T(8,128)(2,1)S(1)} %get-tuple-element.34), channel_id=1, source_target_pairs={{0,2},{2,0},{1,3},{3,1},{4,6},{6,4},{5,7},{7,5},{8,10},{10,8},{9,1... | collective-permute-start | bytes 110600 | tf_op jit(solution)/shard_map/ppermute | solution.py:45
  4.7 1.5 %collective-permute-start.7 = (bf16[144,128]{1,0:T(8,128)(2,1)S(1)}, bf16[144,128]{1,0:T(8,128)(2,1)S(1)}, u32[]{:S(2)}, u32[]{:S(2)}) collective-permute-start(bf16[144,128]{1,0:T(8,128)(2,1)S(1)} %get-tuple-element.35), channel_id=1, source_target_pairs={{2,4},{4,2},{3,5},{5,3},{0,1},{1,0},{6,7},{7,6},{10,12},{12,10},{1... | collective-permute-start | bytes 110600 | tf_op jit(solution)/shard_map/ppermute | solution.py:46
  6.2 0.0 collective-permute-start
  6.2 0.0 collective-permute-done.2.sa_ref
  6.2 2.2 %collective-permute-start.1 = (bf16[4,4,48,128]{3,2,1,0:T(8,128)(2,1)S(1)}, bf16[4,4,48,128]{3,2,1,0:T(8,128)(2,1)S(1)}, u32[]{:S(2)}, u32[]{:S(2)}) collective-permute-start(bf16[4,4,48,128]{3,2,1,0:T(8,128)(2,1)S(1)} %get-tuple-element.27), channel_id=1, source_target_pairs={{8,16},{16,8},{9,17},{17,9},{0,1},{1,0},{24,25},{25,24},{10,18},{1... | collective-permute-start | bytes 589832 | tf_op jit(solution)/shard_map/ppermute | solution.py:46
  8.4 0.0 collective-permute-done.3.sb_ref
  8.4 0.1 shard_map.78
  8.5 1.1 %collective-permute-start.4 = (bf16[192,128]{1,0:T(8,128)(2,1)S(1)}, bf16[192,128]{1,0:T(8,128)(2,1)S(1)}, u32[]{:S(2)}, u32[]{:S(2)}) collective-permute-start(bf16[192,128]{1,0:T(8,128)(2,1)S(1)} %get-tuple-element.30), channel_id=1, source_target_pairs={{0,2},{2,0},{1,3},{3,1},{4,6},{6,4},{5,7},{7,5},{8,10},{10,8},{9,1... | collective-permute-start | bytes 147464 | tf_op jit(solution)/shard_map/ppermute | solution.py:45
  9.6 1.0 %shard_map.80 = (bf16[2,64,256]{2,1,0:T(8,128)(2,1)S(1)}, bf16[2,64,256]{2,1,0:T(8,128)(2,1)S(1)}, bf16[2,2,128,256]{3,2,1,0:T(8,128)(2,1)S(1)}, f32[3,4,64,128]{3,2,1,0:T(8,128)S(1)}, bf16[512,64]{1,0:T(8,128)(2,1)S(1)}) custom-call(bf16[208,128]{1,0:T(8,128)(2,1)S(1)} %collective-permute-done.2.sa_ref, bf16[208,128]{1,0:T(8,128)(2,1)S(1)} %collective-permute-done.3.sb_ref, ...), custom_call_target="tpu_custom_call" | custom-call | flops 268435456 | bytes 2097152 | tf_op jit(solution)/shard_map/pallas_call | solution.py:500
  10.6 0.0 collective-permute-done.6.ra_ref
  10.6 2.4 %collective-permute-start.5 = (bf16[192,128]{1,0:T(8,128)(2,1)S(1)}, bf16[192,128]{1,0:T(8,128)(2,1)S(1)}, u32[]{:S(2)}, u32[]{:S(2)}) collective-permute-start(bf16[192,128]{1,0:T(8,128)(2,1)S(1)} %get-tuple-element.31), channel_id=1, source_target_pairs={{2,4},{4,2},{3,5},{5,3},{0,1},{1,0},{6,7},{7,6},{10,12},{12,10},{1... | collective-permute-start | bytes 147464 | tf_op jit(solution)/shard_map/ppermute | solution.py:46
  13.0 0.0 collective-permute-done.7.rb_ref
  13.0 2.2 %shard_map.81 = (bf16[3,6,2,2,224,128]{5,4,3,2,1,0:T(8,128)(2,1)S(1)}, bf16[3,4,6,64,128]{4,3,2,1,0:T(8,128)(2,1)S(1)}) custom-call(bf16[4,64,512]{2,1,0:T(8,128)(2,1)S(1)} %get-tuple-element.32.x_ref, bf16[144,128]{1,0:T(8,128)(2,1)S(1)} %collective-permute-done.6.ra_ref, bf16[144,128]{1,0:T(8,128)(2,1)S(1)} %collective-permute-done.7.rb_ref, ...), custom_call_target="tpu_custom_call" | custom-call | flops 2147483648 | bytes 5242880 | tf_op jit(solution)/shard_map/pallas_call | solution.py:513
  15.2 0.0 collective-permute-done.4.ra_ref
  15.2 0.0 collective-permute-done.5.rb_ref
  15.2 0.0 collective-permute-done.ma_ref
  15.2 2.6 %collective-permute-done.1.mb_ref = bf16[4,4,48,128]{3,2,1,0:T(8,128)(2,1)S(1)} collective-permute-done((bf16[4,4,48,128]{3,2,1,0:T(8,128)(2,1)S(1)}, bf16[4,4,48,128]{3,2,1,0:T(8,128)(2,1)S(1)}, u32[]{:S(2)}, u32[]{:S(2)}) %collective-permute-start.1) | collective-permute-done | bytes 196640 | tf_op jit(solution)/shard_map/ppermute | solution.py:46
  17.8 1.9 %shard_map.82 = (bf16[1,32,512]{2,1,0:T(8,128)(2,1)S(1)}, f32[32,512]{1,0:T(8,128)S(1)}, bf16[4,6,160,128]{3,2,1,0:T(8,128)(2,1)S(1)}) custom-call(bf16[4,4,48,128]{3,2,1,0:T(8,128)(2,1)S(1)} %collective-permute-done.ma_ref, bf16[4,4,48,128]{3,2,1,0:T(8,128)(2,1)S(1)} %collective-permute-done.1.mb_ref, bf16[192,128]{1,0:T(8,128)(2,1)S(1)} %collective-permute-done.4.ra_ref, ...), custom_call_target="tpu_custom_call" | custom-call | flops 2147483648 | bytes 8388608 | tf_op jit(solution)/shard_map/pallas_call | solution.py:523
  19.7 0.6 %collective-permute-start.8 = (bf16[32,512]{1,0:T(8,128)(2,1)S(1)}, bf16[32,512]{1,0:T(8,128)(2,1)S(1)}, u32[]{:S(2)}, u32[]{:S(2)}) collective-permute-start(bf16[32,512]{1,0:T(8,128)(2,1)S(1)} %bitcast.4), channel_id=1, source_target_pairs={{0,1},{1,0},{2,3},{3,2},{4,5},{5,4},{6,7},{7,6},{8,9},{9,8},{10,11... | collective-permute-start | bytes 98312 | tf_op jit(solution)/shard_map/ppermute | solution.py:537
  20.3 1.1 %shard_map.83 = bf16[4,64,512]{2,1,0:T(8,128)(2,1)} custom-call(bf16[4,6,160,128]{3,2,1,0:T(8,128)(2,1)S(1)} %get-tuple-element.47.deep_ref, bf16[2,2,128,256]{3,2,1,0:T(8,128)(2,1)S(1)} %get-tuple-element.45.far_ref), custom_call_target="tpu_custom_call" | custom-call | flops 268435456 | bytes 1048576 | tf_op jit(solution)/shard_map/pallas_call | solution.py:539
  21.5 0.0 collective-permute-done.8
  21.5 0.6 %add_multiply_fusion = f32[32,512]{1,0:T(8,128)} fusion(f32[32,512]{1,0:T(8,128)S(1)} %get-tuple-element.48, bf16[32,512]{1,0:T(8,128)(2,1)S(1)} %collective-permute-done.8), kind=kLoop, calls=%fused_computation | loop fusion | flops 49152 | bytes 163840 | tf_op jit(solution)/shard_map/mul | solution.py:541
Async XLA Ops:
  1.7 4.5 %collective-permute-start.2 = (bf16[208,128]{1,0:T(8,128)(2,1)S(1)}, bf16[208,128]{1,0:T(8,128)(2,1)S(1)}, u32[]{:S(2)}, u32[]{:S(2)}) collective-permute-start(bf16[208,128]{1,0:T(8,128)(2,1)S(1)} %get-tuple-element.28), channel_id=1, source_target_pairs={{0,8},{8,0},{1,9},{9,1},{16,24},{24,16},{17,25},{25,17},{2,10},{10... | collective-permute-start | bytes 159752 | tf_op jit(solution)/shard_map/ppermute | solution.py:45
  3.0 5.3 %collective-permute-start.3 = (bf16[208,128]{1,0:T(8,128)(2,1)S(1)}, bf16[208,128]{1,0:T(8,128)(2,1)S(1)}, u32[]{:S(2)}, u32[]{:S(2)}) collective-permute-start(bf16[208,128]{1,0:T(8,128)(2,1)S(1)} %get-tuple-element.29), channel_id=1, source_target_pairs={{8,16},{16,8},{9,17},{17,9},{0,1},{1,0},{24,25},{25,24},{10,18},{1... | collective-permute-start | bytes 159752 | tf_op jit(solution)/shard_map/ppermute | solution.py:46
  3.1 7.5 %collective-permute-start.6 = (bf16[144,128]{1,0:T(8,128)(2,1)S(1)}, bf16[144,128]{1,0:T(8,128)(2,1)S(1)}, u32[]{:S(2)}, u32[]{:S(2)}) collective-permute-start(bf16[144,128]{1,0:T(8,128)(2,1)S(1)} %get-tuple-element.34), channel_id=1, source_target_pairs={{0,2},{2,0},{1,3},{3,1},{4,6},{6,4},{5,7},{7,5},{8,10},{10,8},{9,1... | collective-permute-start | bytes 110600 | tf_op jit(solution)/shard_map/ppermute | solution.py:45
  4.7 8.3 %collective-permute-start.7 = (bf16[144,128]{1,0:T(8,128)(2,1)S(1)}, bf16[144,128]{1,0:T(8,128)(2,1)S(1)}, u32[]{:S(2)}, u32[]{:S(2)}) collective-permute-start(bf16[144,128]{1,0:T(8,128)(2,1)S(1)} %get-tuple-element.35), channel_id=1, source_target_pairs={{2,4},{4,2},{3,5},{5,3},{0,1},{1,0},{6,7},{7,6},{10,12},{12,10},{1... | collective-permute-start | bytes 110600 | tf_op jit(solution)/shard_map/ppermute | solution.py:46
  6.2 9.0 %collective-permute-start = (bf16[4,4,48,128]{3,2,1,0:T(8,128)(2,1)S(1)}, bf16[4,4,48,128]{3,2,1,0:T(8,128)(2,1)S(1)}, u32[]{:S(2)}, u32[]{:S(2)}) collective-permute-start(bf16[4,4,48,128]{3,2,1,0:T(8,128)(2,1)S(1)} %get-tuple-element.26), channel_id=1, source_target_pairs={{0,8},{8,0},{1,9},{9,1},{16,24},{24,16},{17,25},{25,17},{2,10},{10... | collective-permute-start | bytes 589832 | tf_op jit(solution)/shard_map/ppermute | solution.py:45
  6.2 11.6 %collective-permute-start.1 = (bf16[4,4,48,128]{3,2,1,0:T(8,128)(2,1)S(1)}, bf16[4,4,48,128]{3,2,1,0:T(8,128)(2,1)S(1)}, u32[]{:S(2)}, u32[]{:S(2)}) collective-permute-start(bf16[4,4,48,128]{3,2,1,0:T(8,128)(2,1)S(1)} %get-tuple-element.27), channel_id=1, source_target_pairs={{8,16},{16,8},{9,17},{17,9},{0,1},{1,0},{24,25},{25,24},{10,18},{1... | collective-permute-start | bytes 589832 | tf_op jit(solution)/shard_map/ppermute | solution.py:46
  8.5 6.7 %collective-permute-start.4 = (bf16[192,128]{1,0:T(8,128)(2,1)S(1)}, bf16[192,128]{1,0:T(8,128)(2,1)S(1)}, u32[]{:S(2)}, u32[]{:S(2)}) collective-permute-start(bf16[192,128]{1,0:T(8,128)(2,1)S(1)} %get-tuple-element.30), channel_id=1, source_target_pairs={{0,2},{2,0},{1,3},{3,1},{4,6},{6,4},{5,7},{7,5},{8,10},{10,8},{9,1... | collective-permute-start | bytes 147464 | tf_op jit(solution)/shard_map/ppermute | solution.py:45
  10.6 4.6 %collective-permute-start.5 = (bf16[192,128]{1,0:T(8,128)(2,1)S(1)}, bf16[192,128]{1,0:T(8,128)(2,1)S(1)}, u32[]{:S(2)}, u32[]{:S(2)}) collective-permute-start(bf16[192,128]{1,0:T(8,128)(2,1)S(1)} %get-tuple-element.31), channel_id=1, source_target_pairs={{2,4},{4,2},{3,5},{5,3},{0,1},{1,0},{6,7},{7,6},{10,12},{12,10},{1... | collective-permute-start | bytes 147464 | tf_op jit(solution)/shard_map/ppermute | solution.py:46
  19.7 1.8 %collective-permute-start.8 = (bf16[32,512]{1,0:T(8,128)(2,1)S(1)}, bf16[32,512]{1,0:T(8,128)(2,1)S(1)}, u32[]{:S(2)}, u32[]{:S(2)}) collective-permute-start(bf16[32,512]{1,0:T(8,128)(2,1)S(1)} %bitcast.4), channel_id=1, source_target_pairs={{0,1},{1,0},{2,3},{3,2},{4,5},{5,4},{6,7},{7,6},{8,9},{9,8},{10,11... | collective-permute-start | bytes 98312 | tf_op jit(solution)/shard_map/ppermute | solution.py:537

commit v5 on v4

--- a/solution.py
+++ b/solution.py
@@ -1,3 +1,4 @@
+import functools
 import math
 
 import jax
@@ -117,8 +118,9 @@
     for p in range(planes):
         for at, main, small in ((at_a, ma_ref, sa_ref), (at_b, mb_ref, sb_ref)):
             tiles = [x_ref[p, pl.ds(at, HALO), t:t + LANES] for t in range(0, cols, LANES)]
-            for t, tile in enumerate(tiles):
-                main[p, t] = tile
+            main[p, 0] = jnp.where(lane < MID, tiles[-1], tiles[0])
+            for t, tile in enumerate(tiles[1:-1]):
+                main[p, t + 1] = tile
             small[p * HALO:(p + 1) * HALO, :] = jnp.where(lane < MID, tiles[0], tiles[-1])
     for copy in copies[2:]:
         copy.wait()
@@ -184,20 +186,67 @@
     return pltpu.roll(taps, 0, 1, stride=1, stride_axis=0)
 
 
-def source_kernel(
-    sa_ref, sb_ref, sidx_ref, taps_ref, bins_ref, weight_ref,
-    near_ref, mid_ref, far_ref, pair_ref, table_ref, sx_ref, wt_ref,
-):
+def block_places(cols, blocks):
+    places, counts = {}, [0, 0]
+    for z in range(DEPTHS):
+        before = HALF * (DEPTHS - 1 - z)
+        for b in range(blocks):
+            outside = b * OUT < before or (before > 0 and (b + 1) * OUT - before > cols)
+            places[z, b] = (outside, counts[outside])
+            counts[outside] += 1
+    return places, counts
+
+
+def index_window(own, left, right, z, b):
+    before = HALF * (DEPTHS - 1 - z)
+    first = b * OUT - before
+    tiles = len(own)
+    j, s = divmod(first, LANES)
+    pieces = [(left if j < 0 else own[j], 0, -s)]
+    if s and j + 1 < tiles:
+        pieces.append((own[j + 1], LANES - s, -s))
+    end = tiles * LANES - first
+    if end < LANES:
+        if before:
+            pieces.append((right, end, end))
+        pieces.append((jnp.full((8, LANES), -1.0, F32), end + before, 0))
+    return join(pieces)[z:z + 1]
+
+
+def put_operators(outside, own, left, right, table, w_ref, cols, blocks):
+    places, _ = block_places(cols, blocks)
+    for z in range(DEPTHS):
+        mine = [b for b in range(blocks) if places[z, b][0] == outside]
+        if not mine:
+            continue
+        taps = taps_of([index_window(own, left, right, z, b) for b in mine], table, table.shape[1])
+        for i, b in enumerate(mine):
+            place = places[z, b][1]
+            at = slice(i * LANES, i * LANES + OUT)
+            for f in range(w_ref.shape[1]):
+                re, im = (skew(taps[at, part * LANES:(part + 1) * LANES]) for part in (2 * f, 2 * f + 1))
+                minus, re, im = (-im).astype(BF), re.astype(BF), im.astype(BF)
+                for half, (top, low) in enumerate(((re, im), (minus, re))):
+                    w_ref[place, f, half, 0:OUT, :] = top
+                    w_ref[place, f, half, OUT:LANES, :] = jnp.zeros((LANES - OUT, LANES), BF)
+                    w_ref[place, f, half, LANES:, :] = low
+
+
+def wide_index(ridx_ref, widx_ref):
+    widx_ref[...] = jnp.zeros(widx_ref.shape, F32)
+    widx_ref[0:DEPTHS, :] = ridx_ref[...].astype(F32)
+    return [widx_ref[:, t:t + LANES] for t in range(0, widx_ref.shape[1], LANES)]
+
+
+def prep_kernel(blocks, taps_ref, ridx_ref, bins_ref, weight_ref, table_ref, pair_ref, w_ref, widx_ref, wt_ref):
     rows, cols = bins_ref.shape
-    freqs = near_ref.shape[0]
+    freqs = w_ref.shape[1]
     tiles = cols // LANES
     for f in range(freqs):
         for part in range(2):
             at = (2 * f + part) * LANES
             table_ref[at:at + LANES, :] = jnp.zeros((LANES, table_ref.shape[1]), BF)
             table_ref[at:at + TAPS, :] = taps_ref[part, :, f, :].astype(BF)
-    table = table_ref[...]
-    entries = table.shape[1]
     wt_ref[...] = jnp.zeros(wt_ref.shape, F32)
     wt_ref[0:DEPTHS, 0:weight_ref.shape[1]] = weight_ref[...]
     for t in range(tiles):
@@ -205,6 +254,14 @@
         for z in range(DEPTHS):
             row = jnp.broadcast_to(wt_ref[z:z + 1, :], (rows, LANES))
             pair_ref[z, t] = jnp.take_along_axis(row, bins, axis=1)
+    own = wide_index(ridx_ref, widx_ref)
+    put_operators(False, own, None, None, table_ref[...], w_ref, cols, blocks)
+
+
+def source_kernel(sa_ref, sb_ref, sidx_ref, table_ref, near_ref, mid_ref, far_ref, sx_ref):
+    freqs, rows, _ = near_ref.shape
+    table = table_ref[...]
+    entries = table.shape[1]
     left, right = index_sides(sa_ref, sb_ref, 2 * freqs * HALO, "src")
     sx_ref[...] = jnp.zeros(sx_ref.shape, F32)
     sx_ref[0:DEPTHS, 0:rows] = sidx_ref[...].astype(F32)
@@ -272,7 +329,8 @@
     return found
 
 
-def receiver_steps(first, w_ref, freqs, rows, keep):
+def receiver_steps(first, w_refs, freqs, rows, cols, keep):
+    places, _ = block_places(cols, len(first[0]))
     source = first
     blocks = len(first[0])
     for z in range(DEPTHS):
@@ -280,7 +338,8 @@
         for b in range(blocks):
             for f in range(freqs):
                 both = jnp.concatenate([source[f][b], source[freqs + f][b]], axis=1)
-                w = jnp.concatenate([w_ref[z, b, f, 0], w_ref[z, b, f, 1]], axis=1)
+                outside, place = places[z, b]
+                w = jnp.concatenate([w_refs[outside][place, f, half] for half in range(2)], axis=1)
                 got = dot(both, w, NT)
                 for p, lanes in ((f, got[:, :OUT]), (freqs + f, got[:, LANES:LANES + OUT])):
                     after[p][b] = jnp.concatenate([lanes, jnp.zeros((rows, LANES - OUT), F32)], axis=1).astype(BF)
@@ -307,44 +366,13 @@
     return (left, HALO + part * MID), (right, -part * MID)
 
 
-def own_kernel(x_ref, ra_ref, rb_ref, ridx_ref, table_ref, w_ref, a_ref, widx_ref):
+def own_kernel(x_ref, ra_ref, rb_ref, ridx_ref, table_ref, wi_ref, wo_ref, a_ref, widx_ref):
     planes, rows, cols = x_ref.shape
-    tiles = cols // LANES
     freqs = planes // 2
-    blocks = w_ref.shape[1]
-    table = table_ref[...]
-    entries = table.shape[1]
+    blocks = a_ref.shape[2]
     left, right = index_sides(ra_ref, rb_ref, freqs * rows, "rec")
-    widx_ref[...] = jnp.zeros(widx_ref.shape, F32)
-    widx_ref[0:DEPTHS, :] = ridx_ref[...].astype(F32)
-    own = [widx_ref[:, t * LANES:(t + 1) * LANES] for t in range(tiles)]
-    none = jnp.full((8, LANES), -1.0, F32)
-    for z in range(DEPTHS):
-        before = HALF * (DEPTHS - 1 - z)
-        index = []
-        for t in range(tiles + 1):
-            pieces = []
-            if before:
-                pieces.append(((left, own[0])[min(t, 1)] if t < 2 else own[t - 1], 0, before))
-            if t < tiles:
-                pieces.append((own[t], before, before))
-            else:
-                if before:
-                    pieces.append((right, before, before))
-                pieces.append((none, 2 * before, 0))
-            index.append(join(pieces)[z:z + 1])
-        taps = taps_of(index, table, entries)
-        for b in range(blocks):
-            at = slice(b * OUT, (b + 1) * OUT)
-            for f in range(freqs):
-                re, im = (
-                    skew(taps[at, part * LANES:(part + 1) * LANES]) for part in (2 * f, 2 * f + 1)
-                )
-                minus, re, im = (-im).astype(BF), re.astype(BF), im.astype(BF)
-                for half, (top, low) in enumerate(((re, im), (minus, re))):
-                    w_ref[z, b, f, half, 0:OUT, :] = top
-                    w_ref[z, b, f, half, OUT:LANES, :] = jnp.zeros((LANES - OUT, LANES), BF)
-                    w_ref[z, b, f, half, LANES:, :] = low
+    own = wide_index(ridx_ref, widx_ref)
+    put_operators(True, own, left, right, table_ref[...], wo_ref, cols, blocks)
     first = []
     for p in range(planes):
         part, f = divmod(p, freqs)
@@ -354,11 +382,11 @@
     def keep(z, p, b, value):
         a_ref[z, p, b] = value
 
-    receiver_steps(first, w_ref, freqs, rows, keep)
+    receiver_steps(first, (wi_ref, wo_ref), freqs, rows, cols, keep)
 
 
 def image_kernel(
-    ma_ref, mb_ref, ra_ref, rb_ref, w_ref, own_ref, near_ref, mid_ref, far_ref, pair_ref,
+    ma_ref, mb_ref, sa_ref, sb_ref, ra_ref, rb_ref, wi_ref, wo_ref, own_ref, near_ref, mid_ref, far_ref, pair_ref,
     send_ref, keep_ref, deep_ref, a_ref, part_ref,
 ):
     _, planes, blocks, rows, _ = own_ref.shape
@@ -368,12 +396,17 @@
     first = []
     for p in range(planes):
         part, f = divmod(p, freqs)
+        at = slice(p * HALO, (p + 1) * HALO)
+        parts = [(sa_ref[at, :], sb_ref[at, :])] + [(ma_ref[p, t], mb_ref[p, t]) for t in range(tiles - 1)]
         main = []
-        for t in range(tiles):
-            left, right = from_sides(ma_ref[p, t], mb_ref[p, t], "src")
+        for a, b in parts:
+            left, right = from_sides(a, b, "src")
             left = jnp.where(has_left("src"), left, jnp.zeros_like(left))
             right = jnp.where(has_right("src"), right, jnp.zeros_like(right))
             main.append(jnp.concatenate([left, right], axis=0))
+        ends, mixed = main[:2]
+        lane = lane_of(ends.shape)
+        main = [jnp.where(lane < MID, ends, mixed)] + main[2:] + [jnp.where(lane < MID, mixed, ends)]
         sides = []
         for cells, amount in halo_sides(ra_ref, rb_ref, slice(2 * f * HALO, 2 * (f + 1) * HALO), part):
             top = jnp.where(has_left("src"), cells[:HALO], jnp.zeros_like(cells[:HALO]))
@@ -390,7 +423,7 @@
         to[HALO:HALO + rows] = own_ref[z, p, b]
         to[HALO + rows:] = value[HALO:]
 
-    receiver_steps(first, w_ref, freqs, 2 * HALO, keep)
+    receiver_steps(first, (wi_ref, wo_ref), freqs, 2 * HALO, tiles * LANES, keep)
 
     def field(z, p, b, reach):
         at = slice(HALO - reach, HALO + rows + reach)
@@ -477,7 +510,7 @@
     full = rows + 2 * HALO
     blocks = -(-(cols + 2 * (HALO - HALF)) // OUT)
 
-    main = ((planes, tiles, HALO, LANES), BF)
+    main = ((planes, tiles - 1, HALO, LANES), BF)
     small = ((planes * HALO + IDX_ROWS, LANES), BF)
     inputs = (wave.reshape(planes, rows, cols), src_index, rec_index, jnp.transpose(tap_table, (0, 3, 2, 1)), offset_bin, bin_weight)
     inputs = tuple(pltpu.with_memory_space_constraint(a, pltpu.HBM) for a in inputs)
@@ -497,29 +530,35 @@
     ea, eb = local_call(edge_kernel, [edge, edge], moved=1 << 16)(sa, sb)
     ea, eb = swaps(ea, eb, "rec")
 
-    near, mid, far, pair, table = local_call(
+    _, (inner, outer) = block_places(cols, blocks)
+    table, pair, wi = local_call(
+        functools.partial(prep_kernel, blocks),
+        [((planes * LANES, entries), BF), ((DEPTHS, tiles, rows, LANES), F32), ((inner, freqs, 2, WROWS, LANES), BF)],
+        [((8, cols), F32), ((8, LANES), F32)],
+        flops=1 << 28,
+        moved=4 << 20,
+    )(tap_table, rec_index, offset_bin, bin_weight)
+    near, mid, far = local_call(
         source_kernel,
         [
             ((freqs, rows, 2 * LANES), BF),
             ((freqs, rows, 2 * LANES), BF),
             ((freqs, 2, 2 * rows, 2 * LANES), BF),
-            ((DEPTHS, tiles, rows, LANES), F32),
-            ((planes * LANES, entries), BF),
         ],
-        [((8, LANES), F32), ((8, LANES), F32)],
+        [((8, LANES), F32)],
         flops=1 << 28,
-        moved=2 << 20,
-    )(sa, sb, src_index, tap_table, offset_bin, bin_weight)
-    w, own = local_call(
+        moved=1 << 20,
+    )(sa, sb, src_index, table)
+    wo, own = local_call(
         own_kernel,
         [
-            ((DEPTHS, blocks, freqs, 2, WROWS, LANES), BF),
+            ((outer, freqs, 2, WROWS, LANES), BF),
             ((DEPTHS, planes, blocks, rows, LANES), BF),
         ],
         [((8, cols), F32)],
         flops=1 << 31,
         moved=5 << 20,
-    )(x, ra, rb, rec_index, table)
+    )(x, ra, rb, rec_index, table, wi)
     send, keep, deep = local_call(
         image_kernel,
         [
@@ -531,7 +570,7 @@
         flops=1 << 31,
         moved=8 << 20,
         vmem=24,
-    )(ma, mb, ea, eb, w, own, near, mid, far, pair)
+    )(ma, mb, sa, sb, ea, eb, wi, wo, own, near, mid, far, pair)
     total = keep
     for j in range(1, count):
         got = lax.ppermute(send[j - 1], "freq", [(i, partner(i, j, count)) for i in range(count)])

time: 22.3 us -> 21.8 us (0.978)
  the two profiles are of different devices: /device:TPU:5 before, /device:TPU:0 now
where the time goes in v5:
time: 21.8 us; the launch traced here: 21.7 us
  starting transfers between devices  11.5 us (53%)
  Pallas kernels  8.77 us (40%)
  between operations  0.71 us (3%)
  other arithmetic  0.64 us (3%)
    ppermute x4, starting transfers between devices, swaps(): a = lax.ppermute(a, (axis, 'freq'), pairs_of(axis, 0))  10.4 us
    pallas_call x1, Pallas kernels, migrate(): local_call(image_kernel, [((max(count - 1, 1), share, cols), BF), ((share...  1.93 us
    pallas_call x1, Pallas kernels, migrate(): local_call(own_kernel, [((outer, freqs, 2, WROWS, LANES), BF), ((DEPTHS,...  1.88 us
    pallas_call x1, Pallas kernels, migrate(): local_call(functools.partial(prep_kernel, blocks), [((planes * LANES, ent...  1.59 us
    pallas_call x1, Pallas kernels, migrate(): local_call(final_kernel, [((planes, rows, cols), BF)], flops=1 << 28, mov...  1.13 us
    pallas_call x1, Pallas kernels, migrate(): local_call(load_kernel, [main, main, small, small] + [(a.shape, a.dtype)...  1.11 us
    pallas_call x1, Pallas kernels, migrate(): local_call(source_kernel, [((freqs, rows, 2 * LANES), BF), ((freqs, rows,...  0.94 us
    ppermute x4, starting transfers between devices, swaps(): b = lax.ppermute(b, (axis, 'freq'), pairs_of(axis, 1))  0.74 us
  transfers between devices with their start and end apart: 9, of which 0 were waited for; matrix products, arithmetic and copies ran while one was open for 0% of the time, Pallas kernels for 26%

profile of v5, /device:TPU:0, one launch (start us, length us, event | category | flops | bytes accessed | tf_op | source)
XLA Modules:
  0.0 21.7 jit_solution(7006271309704858900)
XLA Ops:
  0.6 1.1 %shard_map.77 = (bf16[4,3,48,128]{3,2,1,0:T(8,128)(2,1)S(1)}, bf16[4,3,48,128]{3,2,1,0:T(8,128)(2,1)S(1)}, bf16[208,128]{1,0:T(8,128)(2,1)S(1)}, bf16[208,128]{1...) custom-call(bf16[4,64,512]{2,1,0:T(8,128)(2,1)} %bitcast.5, ...), custom_call_target="tpu_custom_call" | custom-call | bytes 1048576 | tf_op jit(solution)/shard_map/pallas_call | solution.py:517
  1.7 3.0 %collective-permute-start.2 = (bf16[208,128]{1,0:T(8,128)(2,1)S(1)}, bf16[208,128]{1,0:T(8,128)(2,1)S(1)}, u32[]{:S(2)}, u32[]{:S(2)}) collective-permute-start(bf16[208,128]{1,0:T(8,128)(2,1)S(1)} %get-tuple-element.29), channel_id=1, source_target_pairs={{0,8},{8,0},{1,9},{9,1},{16,24},{24,16},{17,25},{25,17},{2,10},{10... | collective-permute-start | bytes 159752 | tf_op jit(solution)/shard_map/ppermute | solution.py:46
  4.8 0.0 collective-permute-start.3
  4.8 0.1 shard_map.80
  4.9 1.6 %collective-permute-start.6 = (bf16[144,128]{1,0:T(8,128)(2,1)S(1)}, bf16[144,128]{1,0:T(8,128)(2,1)S(1)}, u32[]{:S(2)}, u32[]{:S(2)}) collective-permute-start(bf16[144,128]{1,0:T(8,128)(2,1)S(1)} %get-tuple-element.39), channel_id=1, source_target_pairs={{0,2},{2,0},{1,3},{3,1},{4,6},{6,4},{5,7},{7,5},{8,10},{10,8},{9,1... | collective-permute-start | bytes 110600 | tf_op jit(solution)/shard_map/ppermute | solution.py:46
  6.5 0.2 %collective-permute-start.7 = (bf16[144,128]{1,0:T(8,128)(2,1)S(1)}, bf16[144,128]{1,0:T(8,128)(2,1)S(1)}, u32[]{:S(2)}, u32[]{:S(2)}) collective-permute-start(bf16[144,128]{1,0:T(8,128)(2,1)S(1)} %get-tuple-element.40), channel_id=1, source_target_pairs={{2,4},{4,2},{3,5},{5,3},{0,1},{1,0},{6,7},{7,6},{10,12},{12,10},{1... | collective-permute-start | bytes 110600 | tf_op jit(solution)/shard_map/ppermute | solution.py:47
  6.7 2.8 %collective-permute-start = (bf16[4,3,48,128]{3,2,1,0:T(8,128)(2,1)S(1)}, bf16[4,3,48,128]{3,2,1,0:T(8,128)(2,1)S(1)}, u32[]{:S(2)}, u32[]{:S(2)}) collective-permute-start(bf16[4,3,48,128]{3,2,1,0:T(8,128)(2,1)S(1)} %get-tuple-element.27), channel_id=1, source_target_pairs={{0,8},{8,0},{1,9},{9,1},{16,24},{24,16},{17,25},{25,17},{2,10},{10... | collective-permute-start | bytes 442376 | tf_op jit(solution)/shard_map/ppermute | solution.py:46
  9.5 1.6 %shard_map.79 = (bf16[512,64]{1,0:T(8,128)(2,1)S(1)}, f32[3,4,64,128]{3,2,1,0:T(8,128)S(1)}, bf16[14,2,2,224,128]{4,3,2,1,0:T(8,128)(2,1)S(1)}) custom-call(f32[2,33,2,64]{3,2,1,0:T(2,128)S(1)} %get-tuple-element.33.taps_ref, s32[3,512]{1,0:T(4,128)S(1)} %get-tuple-element.34.ridx_ref, s32[64,512]{1,0:T(8,128)S(1)} %get-tuple-element.35.bins_ref, ...), custom_call_target="tpu_custom_call" | custom-call | flops 268435456 | bytes 4194304 | tf_op jit(solution)/shard_map/pallas_call | solution.py:534
  11.1 0.0 collective-permute-done.2.sa_ref
  11.1 0.3 %collective-permute-start.1 = (bf16[4,3,48,128]{3,2,1,0:T(8,128)(2,1)S(1)}, bf16[4,3,48,128]{3,2,1,0:T(8,128)(2,1)S(1)}, u32[]{:S(2)}, u32[]{:S(2)}) collective-permute-start(bf16[4,3,48,128]{3,2,1,0:T(8,128)(2,1)S(1)} %get-tuple-element.28), channel_id=1, source_target_pairs={{8,16},{16,8},{9,17},{17,9},{0,1},{1,0},{24,25},{25,24},{10,18},{1... | collective-permute-start | bytes 442376 | tf_op jit(solution)/shard_map/ppermute | solution.py:47
  11.4 0.0 collective-permute-done.3.sb_ref
  11.4 0.1 shard_map.78
  11.5 3.0 %collective-permute-start.4 = (bf16[192,128]{1,0:T(8,128)(2,1)S(1)}, bf16[192,128]{1,0:T(8,128)(2,1)S(1)}, u32[]{:S(2)}, u32[]{:S(2)}) collective-permute-start(bf16[192,128]{1,0:T(8,128)(2,1)S(1)} %get-tuple-element.31), channel_id=1, source_target_pairs={{0,2},{2,0},{1,3},{3,1},{4,6},{6,4},{5,7},{7,5},{8,10},{10,8},{9,1... | collective-permute-start | bytes 147464 | tf_op jit(solution)/shard_map/ppermute | solution.py:46
  14.5 0.0 collective-permute-done.6.ra_ref
  14.5 0.2 collective-permute-start.5
  14.7 0.0 collective-permute-done.7.rb_ref
  14.7 1.9 %shard_map.81 = (bf16[4,2,2,224,128]{4,3,2,1,0:T(8,128)(2,1)S(1)}, bf16[3,4,6,64,128]{4,3,2,1,0:T(8,128)(2,1)S(1)}) custom-call(bf16[4,64,512]{2,1,0:T(8,128)(2,1)S(1)} %get-tuple-element.38.x_ref, bf16[144,128]{1,0:T(8,128)(2,1)S(1)} %collective-permute-done.6.ra_ref, bf16[144,128]{1,0:T(8,128)(2,1)S(1)} %collective-permute-done.7.rb_ref, ...), custom_call_target="tpu_custom_call" | custom-call | flops 2147483648 | bytes 5242880 | tf_op jit(solution)/shard_map/pallas_call | solution.py:552
  16.6 0.9 %shard_map.82 = (bf16[2,64,256]{2,1,0:T(8,128)(2,1)S(1)}, bf16[2,64,256]{2,1,0:T(8,128)(2,1)S(1)}, bf16[2,2,128,256]{3,2,1,0:T(8,128)(2,1)S(1)}) custom-call(bf16[208,128]{1,0:T(8,128)(2,1)S(1)} %collective-permute-done.2.sa_ref, bf16[208,128]{1,0:T(8,128)(2,1)S(1)} %collective-permute-done.3.sb_ref, s32[3,64]{1,0:T(4,128)S(1)} %get-tuple-element.44.sidx_ref, ...), custom_call_target="tpu_custom_call" | custom-call | flops 268435456 | bytes 1048576 | tf_op jit(solution)/shard_map/pallas_call | solution.py:541
  17.6 0.0 collective-permute-done.4.ra_ref
  17.6 0.0 collective-permute-done.5.rb_ref
  17.6 0.0 collective-permute-done.ma_ref
  17.6 0.0 collective-permute-done.1.mb_ref
  17.6 1.9 %shard_map.83 = (bf16[1,32,512]{2,1,0:T(8,128)(2,1)S(1)}, f32[32,512]{1,0:T(8,128)S(1)}, bf16[4,6,160,128]{3,2,1,0:T(8,128)(2,1)S(1)}) custom-call(bf16[4,3,48,128]{3,2,1,0:T(8,128)(2,1)S(1)} %collective-permute-done.ma_ref, bf16[4,3,48,128]{3,2,1,0:T(8,128)(2,1)S(1)} %collective-permute-done.1.mb_ref, bf16[208,128]{1,0:T(8,128)(2,1)S(1)} %collective-permute-done.2.sa_ref, ...), custom_call_target="tpu_custom_call" | custom-call | flops 2147483648 | bytes 8388608 | tf_op jit(solution)/shard_map/pallas_call | solution.py:562
  19.5 0.4 %collective-permute-start.8 = (bf16[32,512]{1,0:T(8,128)(2,1)S(1)}, bf16[32,512]{1,0:T(8,128)(2,1)S(1)}, u32[]{:S(2)}, u32[]{:S(2)}) collective-permute-start(bf16[32,512]{1,0:T(8,128)(2,1)S(1)} %bitcast.4), channel_id=1, source_target_pairs={{0,1},{1,0},{2,3},{3,2},{4,5},{5,4},{6,7},{7,6},{8,9},{9,8},{10,11... | collective-permute-start | bytes 98312 | tf_op jit(solution)/shard_map/ppermute | solution.py:576
  19.9 1.1 %shard_map.84 = bf16[4,64,512]{2,1,0:T(8,128)(2,1)} custom-call(bf16[4,6,160,128]{3,2,1,0:T(8,128)(2,1)S(1)} %get-tuple-element.49.deep_ref, bf16[2,2,128,256]{3,2,1,0:T(8,128)(2,1)S(1)} %get-tuple-element.47.far_ref), custom_call_target="tpu_custom_call" | custom-call | flops 268435456 | bytes 1048576 | tf_op jit(solution)/shard_map/pallas_call | solution.py:578
  21.0 0.0 collective-permute-done.8
  21.0 0.6 %add_multiply_fusion = f32[32,512]{1,0:T(8,128)} fusion(f32[32,512]{1,0:T(8,128)S(1)} %get-tuple-element.50, bf16[32,512]{1,0:T(8,128)(2,1)S(1)} %collective-permute-done.8), kind=kLoop, calls=%fused_computation | loop fusion | flops 49152 | bytes 163840 | tf_op jit(solution)/shard_map/mul | solution.py:580
Async XLA Ops:
  1.7 9.4 %collective-permute-start.2 = (bf16[208,128]{1,0:T(8,128)(2,1)S(1)}, bf16[208,128]{1,0:T(8,128)(2,1)S(1)}, u32[]{:S(2)}, u32[]{:S(2)}) collective-permute-start(bf16[208,128]{1,0:T(8,128)(2,1)S(1)} %get-tuple-element.29), channel_id=1, source_target_pairs={{0,8},{8,0},{1,9},{9,1},{16,24},{24,16},{17,25},{25,17},{2,10},{10... | collective-permute-start | bytes 159752 | tf_op jit(solution)/shard_map/ppermute | solution.py:46
  4.8 6.6 %collective-permute-start.3 = (bf16[208,128]{1,0:T(8,128)(2,1)S(1)}, bf16[208,128]{1,0:T(8,128)(2,1)S(1)}, u32[]{:S(2)}, u32[]{:S(2)}) collective-permute-start(bf16[208,128]{1,0:T(8,128)(2,1)S(1)} %get-tuple-element.30), channel_id=1, source_target_pairs={{8,16},{16,8},{9,17},{17,9},{0,1},{1,0},{24,25},{25,24},{10,18},{1... | collective-permute-start | bytes 159752 | tf_op jit(solution)/shard_map/ppermute | solution.py:47
  4.9 9.7 %collective-permute-start.6 = (bf16[144,128]{1,0:T(8,128)(2,1)S(1)}, bf16[144,128]{1,0:T(8,128)(2,1)S(1)}, u32[]{:S(2)}, u32[]{:S(2)}) collective-permute-start(bf16[144,128]{1,0:T(8,128)(2,1)S(1)} %get-tuple-element.39), channel_id=1, source_target_pairs={{0,2},{2,0},{1,3},{3,1},{4,6},{6,4},{5,7},{7,5},{8,10},{10,8},{9,1... | collective-permute-start | bytes 110600 | tf_op jit(solution)/shard_map/ppermute | solution.py:46
  6.5 8.2 %collective-permute-start.7 = (bf16[144,128]{1,0:T(8,128)(2,1)S(1)}, bf16[144,128]{1,0:T(8,128)(2,1)S(1)}, u32[]{:S(2)}, u32[]{:S(2)}) collective-permute-start(bf16[144,128]{1,0:T(8,128)(2,1)S(1)} %get-tuple-element.40), channel_id=1, source_target_pairs={{2,4},{4,2},{3,5},{5,3},{0,1},{1,0},{6,7},{7,6},{10,12},{12,10},{1... | collective-permute-start | bytes 110600 | tf_op jit(solution)/shard_map/ppermute | solution.py:47
  6.7 10.8 %collective-permute-start = (bf16[4,3,48,128]{3,2,1,0:T(8,128)(2,1)S(1)}, bf16[4,3,48,128]{3,2,1,0:T(8,128)(2,1)S(1)}, u32[]{:S(2)}, u32[]{:S(2)}) collective-permute-start(bf16[4,3,48,128]{3,2,1,0:T(8,128)(2,1)S(1)} %get-tuple-element.27), channel_id=1, source_target_pairs={{0,8},{8,0},{1,9},{9,1},{16,24},{24,16},{17,25},{25,17},{2,10},{10... | collective-permute-start | bytes 442376 | tf_op jit(solution)/shard_map/ppermute | solution.py:46
  11.1 6.5 %collective-permute-start.1 = (bf16[4,3,48,128]{3,2,1,0:T(8,128)(2,1)S(1)}, bf16[4,3,48,128]{3,2,1,0:T(8,128)(2,1)S(1)}, u32[]{:S(2)}, u32[]{:S(2)}) collective-permute-start(bf16[4,3,48,128]{3,2,1,0:T(8,128)(2,1)S(1)} %get-tuple-element.28), channel_id=1, source_target_pairs={{8,16},{16,8},{9,17},{17,9},{0,1},{1,0},{24,25},{25,24},{10,18},{1... | collective-permute-start | bytes 442376 | tf_op jit(solution)/shard_map/ppermute | solution.py:47
  11.5 6.0 %collective-permute-start.4 = (bf16[192,128]{1,0:T(8,128)(2,1)S(1)}, bf16[192,128]{1,0:T(8,128)(2,1)S(1)}, u32[]{:S(2)}, u32[]{:S(2)}) collective-permute-start(bf16[192,128]{1,0:T(8,128)(2,1)S(1)} %get-tuple-element.31), channel_id=1, source_target_pairs={{0,2},{2,0},{1,3},{3,1},{4,6},{6,4},{5,7},{7,5},{8,10},{10,8},{9,1... | collective-permute-start | bytes 147464 | tf_op jit(solution)/shard_map/ppermute | solution.py:46
  14.5 3.0 %collective-permute-start.5 = (bf16[192,128]{1,0:T(8,128)(2,1)S(1)}, bf16[192,128]{1,0:T(8,128)(2,1)S(1)}, u32[]{:S(2)}, u32[]{:S(2)}) collective-permute-start(bf16[192,128]{1,0:T(8,128)(2,1)S(1)} %get-tuple-element.32), channel_id=1, source_target_pairs={{2,4},{4,2},{3,5},{5,3},{0,1},{1,0},{6,7},{7,6},{10,12},{12,10},{1... | collective-permute-start | bytes 147464 | tf_op jit(solution)/shard_map/ppermute | solution.py:47
  19.5 1.5 %collective-permute-start.8 = (bf16[32,512]{1,0:T(8,128)(2,1)S(1)}, bf16[32,512]{1,0:T(8,128)(2,1)S(1)}, u32[]{:S(2)}, u32[]{:S(2)}) collective-permute-start(bf16[32,512]{1,0:T(8,128)(2,1)S(1)} %bitcast.4), channel_id=1, source_target_pairs={{0,1},{1,0},{2,3},{3,2},{4,5},{5,4},{6,7},{7,6},{8,9},{9,8},{10,11... | collective-permute-start | bytes 98312 | tf_op jit(solution)/shard_map/ppermute | solution.py:576

commit v6 on v4

--- a/solution.py
+++ b/solution.py
@@ -117,8 +117,9 @@
     for p in range(planes):
         for at, main, small in ((at_a, ma_ref, sa_ref), (at_b, mb_ref, sb_ref)):
             tiles = [x_ref[p, pl.ds(at, HALO), t:t + LANES] for t in range(0, cols, LANES)]
-            for t, tile in enumerate(tiles):
-                main[p, t] = tile
+            main[p, 0] = jnp.where(lane < MID, tiles[-1], tiles[0])
+            for t, tile in enumerate(tiles[1:-1]):
+                main[p, t + 1] = tile
             small[p * HALO:(p + 1) * HALO, :] = jnp.where(lane < MID, tiles[0], tiles[-1])
     for copy in copies[2:]:
         copy.wait()
@@ -358,7 +359,7 @@
 
 
 def image_kernel(
-    ma_ref, mb_ref, ra_ref, rb_ref, w_ref, own_ref, near_ref, mid_ref, far_ref, pair_ref,
+    ma_ref, mb_ref, sa_ref, sb_ref, ra_ref, rb_ref, w_ref, own_ref, near_ref, mid_ref, far_ref, pair_ref,
     send_ref, keep_ref, deep_ref, a_ref, part_ref,
 ):
     _, planes, blocks, rows, _ = own_ref.shape
@@ -368,12 +369,17 @@
     first = []
     for p in range(planes):
         part, f = divmod(p, freqs)
+        at = slice(p * HALO, (p + 1) * HALO)
+        parts = [(sa_ref[at, :], sb_ref[at, :])] + [(ma_ref[p, t], mb_ref[p, t]) for t in range(tiles - 1)]
         main = []
-        for t in range(tiles):
-            left, right = from_sides(ma_ref[p, t], mb_ref[p, t], "src")
+        for a, b in parts:
+            left, right = from_sides(a, b, "src")
             left = jnp.where(has_left("src"), left, jnp.zeros_like(left))
             right = jnp.where(has_right("src"), right, jnp.zeros_like(right))
             main.append(jnp.concatenate([left, right], axis=0))
+        ends, mixed = main[:2]
+        lane = lane_of(ends.shape)
+        main = [jnp.where(lane < MID, ends, mixed)] + main[2:] + [jnp.where(lane < MID, mixed, ends)]
         sides = []
         for cells, amount in halo_sides(ra_ref, rb_ref, slice(2 * f * HALO, 2 * (f + 1) * HALO), part):
             top = jnp.where(has_left("src"), cells[:HALO], jnp.zeros_like(cells[:HALO]))
@@ -477,7 +483,7 @@
     full = rows + 2 * HALO
     blocks = -(-(cols + 2 * (HALO - HALF)) // OUT)
 
-    main = ((planes, tiles, HALO, LANES), BF)
+    main = ((planes, tiles - 1, HALO, LANES), BF)
     small = ((planes * HALO + IDX_ROWS, LANES), BF)
     inputs = (wave.reshape(planes, rows, cols), src_index, rec_index, jnp.transpose(tap_table, (0, 3, 2, 1)), offset_bin, bin_weight)
     inputs = tuple(pltpu.with_memory_space_constraint(a, pltpu.HBM) for a in inputs)
@@ -531,7 +537,7 @@
         flops=1 << 31,
         moved=8 << 20,
         vmem=24,
-    )(ma, mb, ea, eb, w, own, near, mid, far, pair)
+    )(ma, mb, sa, sb, ea, eb, w, own, near, mid, far, pair)
     total = keep
     for j in range(1, count):
         got = lax.ppermute(send[j - 1], "freq", [(i, partner(i, j, count)) for i in range(count)])

time: 22.3 us -> 20.6 us (0.924)
  the two profiles are of different devices: /device:TPU:5 before, /device:TPU:0 now
where the time goes in v6:
time: 20.6 us; the launch traced here: 20.4 us
  starting transfers between devices  11.5 us (56%)
  Pallas kernels  7.52 us (37%)
  between operations  0.71 us (3%)
  other arithmetic  0.64 us (3%)
    ppermute x4, starting transfers between devices, swaps(): a = lax.ppermute(a, (axis, 'freq'), pairs_of(axis, 0))  10.4 us
    pallas_call x1, Pallas kernels, migrate(): local_call(own_kernel, [((DEPTHS, blocks, freqs, 2, WROWS, LANES), BF), (...  2.21 us
    pallas_call x1, Pallas kernels, migrate(): local_call(image_kernel, [((max(count - 1, 1), share, cols), BF), ((share...  1.92 us
    pallas_call x1, Pallas kernels, migrate(): local_call(final_kernel, [((planes, rows, cols), BF)], flops=1 << 28, mov...  1.13 us
    pallas_call x1, Pallas kernels, migrate(): local_call(load_kernel, [main, main, small, small] + [(a.shape, a.dtype)...  1.11 us
    pallas_call x1, Pallas kernels, migrate(): local_call(source_kernel, [((freqs, rows, 2 * LANES), BF), ((freqs, rows,...  0.96 us
    ppermute x4, starting transfers between devices, swaps(): b = lax.ppermute(b, (axis, 'freq'), pairs_of(axis, 1))  0.74 us
    mul x1, other arithmetic, migrate(): return (final.reshape(wave.shape), total * scale)  0.64 us
  transfers between devices with their start and end apart: 9, of which 0 were waited for; matrix products, arithmetic and copies ran while one was open for 0% of the time, Pallas kernels for 22%

profile of v6, /device:TPU:0, one launch (start us, length us, event | category | flops | bytes accessed | tf_op | source)
XLA Modules:
  0.0 20.4 jit_solution(5732697220203181453)
XLA Ops:
  0.6 1.1 %shard_map.77 = (bf16[4,3,48,128]{3,2,1,0:T(8,128)(2,1)S(1)}, bf16[4,3,48,128]{3,2,1,0:T(8,128)(2,1)S(1)}, bf16[208,128]{1,0:T(8,128)(2,1)S(1)}, bf16[208,128]{1...) custom-call(bf16[4,64,512]{2,1,0:T(8,128)(2,1)} %bitcast.5, ...), custom_call_target="tpu_custom_call" | custom-call | bytes 1048576 | tf_op jit(solution)/shard_map/pallas_call | solution.py:490
  1.7 3.0 %collective-permute-start.2 = (bf16[208,128]{1,0:T(8,128)(2,1)S(1)}, bf16[208,128]{1,0:T(8,128)(2,1)S(1)}, u32[]{:S(2)}, u32[]{:S(2)}) collective-permute-start(bf16[208,128]{1,0:T(8,128)(2,1)S(1)} %get-tuple-element.28), channel_id=1, source_target_pairs={{0,8},{8,0},{1,9},{9,1},{16,24},{24,16},{17,25},{25,17},{2,10},{10... | collective-permute-start | bytes 159752 | tf_op jit(solution)/shard_map/ppermute | solution.py:45
  4.8 0.0 collective-permute-start.3
  4.8 0.1 shard_map.79
  4.9 1.6 %collective-permute-start.6 = (bf16[144,128]{1,0:T(8,128)(2,1)S(1)}, bf16[144,128]{1,0:T(8,128)(2,1)S(1)}, u32[]{:S(2)}, u32[]{:S(2)}) collective-permute-start(bf16[144,128]{1,0:T(8,128)(2,1)S(1)} %get-tuple-element.34), channel_id=1, source_target_pairs={{0,2},{2,0},{1,3},{3,1},{4,6},{6,4},{5,7},{7,5},{8,10},{10,8},{9,1... | collective-permute-start | bytes 110600 | tf_op jit(solution)/shard_map/ppermute | solution.py:45
  6.5 0.2 %collective-permute-start.7 = (bf16[144,128]{1,0:T(8,128)(2,1)S(1)}, bf16[144,128]{1,0:T(8,128)(2,1)S(1)}, u32[]{:S(2)}, u32[]{:S(2)}) collective-permute-start(bf16[144,128]{1,0:T(8,128)(2,1)S(1)} %get-tuple-element.35), channel_id=1, source_target_pairs={{2,4},{4,2},{3,5},{5,3},{0,1},{1,0},{6,7},{7,6},{10,12},{12,10},{1... | collective-permute-start | bytes 110600 | tf_op jit(solution)/shard_map/ppermute | solution.py:46
  6.7 2.8 %collective-permute-start = (bf16[4,3,48,128]{3,2,1,0:T(8,128)(2,1)S(1)}, bf16[4,3,48,128]{3,2,1,0:T(8,128)(2,1)S(1)}, u32[]{:S(2)}, u32[]{:S(2)}) collective-permute-start(bf16[4,3,48,128]{3,2,1,0:T(8,128)(2,1)S(1)} %get-tuple-element.26), channel_id=1, source_target_pairs={{0,8},{8,0},{1,9},{9,1},{16,24},{24,16},{17,25},{25,17},{2,10},{10... | collective-permute-start | bytes 442376 | tf_op jit(solution)/shard_map/ppermute | solution.py:45
  9.5 0.0 collective-permute-done.2.sa_ref
  9.5 0.2 %collective-permute-start.1 = (bf16[4,3,48,128]{3,2,1,0:T(8,128)(2,1)S(1)}, bf16[4,3,48,128]{3,2,1,0:T(8,128)(2,1)S(1)}, u32[]{:S(2)}, u32[]{:S(2)}) collective-permute-start(bf16[4,3,48,128]{3,2,1,0:T(8,128)(2,1)S(1)} %get-tuple-element.27), channel_id=1, source_target_pairs={{8,16},{16,8},{9,17},{17,9},{0,1},{1,0},{24,25},{25,24},{10,18},{1... | collective-permute-start | bytes 442376 | tf_op jit(solution)/shard_map/ppermute | solution.py:46
  9.7 0.0 collective-permute-done.3.sb_ref
  9.7 0.1 shard_map.78
  9.8 3.0 %collective-permute-start.4 = (bf16[192,128]{1,0:T(8,128)(2,1)S(1)}, bf16[192,128]{1,0:T(8,128)(2,1)S(1)}, u32[]{:S(2)}, u32[]{:S(2)}) collective-permute-start(bf16[192,128]{1,0:T(8,128)(2,1)S(1)} %get-tuple-element.30), channel_id=1, source_target_pairs={{0,2},{2,0},{1,3},{3,1},{4,6},{6,4},{5,7},{7,5},{8,10},{10,8},{9,1... | collective-permute-start | bytes 147464 | tf_op jit(solution)/shard_map/ppermute | solution.py:45
  12.8 1.0 %shard_map.80 = (bf16[2,64,256]{2,1,0:T(8,128)(2,1)S(1)}, bf16[2,64,256]{2,1,0:T(8,128)(2,1)S(1)}, bf16[2,2,128,256]{3,2,1,0:T(8,128)(2,1)S(1)}, f32[3,4,64,128]{3,2,1,0:T(8,128)S(1)}, bf16[512,64]{1,0:T(8,128)(2,1)S(1)}) custom-call(bf16[208,128]{1,0:T(8,128)(2,1)S(1)} %collective-permute-done.2.sa_ref, bf16[208,128]{1,0:T(8,128)(2,1)S(1)} %collective-permute-done.3.sb_ref, ...), custom_call_target="tpu_custom_call" | custom-call | flops 268435456 | bytes 2097152 | tf_op jit(solution)/shard_map/pallas_call | solution.py:506
  13.8 0.0 collective-permute-done.6.ra_ref
  13.8 0.3 %collective-permute-start.5 = (bf16[192,128]{1,0:T(8,128)(2,1)S(1)}, bf16[192,128]{1,0:T(8,128)(2,1)S(1)}, u32[]{:S(2)}, u32[]{:S(2)}) collective-permute-start(bf16[192,128]{1,0:T(8,128)(2,1)S(1)} %get-tuple-element.31), channel_id=1, source_target_pairs={{2,4},{4,2},{3,5},{5,3},{0,1},{1,0},{6,7},{7,6},{10,12},{12,10},{1... | collective-permute-start | bytes 147464 | tf_op jit(solution)/shard_map/ppermute | solution.py:46
  14.1 0.0 collective-permute-done.7.rb_ref
  14.1 2.2 %shard_map.81 = (bf16[3,6,2,2,224,128]{5,4,3,2,1,0:T(8,128)(2,1)S(1)}, bf16[3,4,6,64,128]{4,3,2,1,0:T(8,128)(2,1)S(1)}) custom-call(bf16[4,64,512]{2,1,0:T(8,128)(2,1)S(1)} %get-tuple-element.32.x_ref, bf16[144,128]{1,0:T(8,128)(2,1)S(1)} %collective-permute-done.6.ra_ref, bf16[144,128]{1,0:T(8,128)(2,1)S(1)} %collective-permute-done.7.rb_ref, ...), custom_call_target="tpu_custom_call" | custom-call | flops 2147483648 | bytes 5242880 | tf_op jit(solution)/shard_map/pallas_call | solution.py:519
  16.3 0.0 collective-permute-done.4.ra_ref
  16.3 0.0 collective-permute-done.5.rb_ref
  16.3 0.0 collective-permute-done.ma_ref
  16.4 0.0 collective-permute-done.1.mb_ref
  16.4 1.9 %shard_map.82 = (bf16[1,32,512]{2,1,0:T(8,128)(2,1)S(1)}, f32[32,512]{1,0:T(8,128)S(1)}, bf16[4,6,160,128]{3,2,1,0:T(8,128)(2,1)S(1)}) custom-call(bf16[4,3,48,128]{3,2,1,0:T(8,128)(2,1)S(1)} %collective-permute-done.ma_ref, bf16[4,3,48,128]{3,2,1,0:T(8,128)(2,1)S(1)} %collective-permute-done.1.mb_ref, bf16[208,128]{1,0:T(8,128)(2,1)S(1)} %collective-permute-done.2.sa_ref, ...), custom_call_target="tpu_custom_call" | custom-call | flops 2147483648 | bytes 8388608 | tf_op jit(solution)/shard_map/pallas_call | solution.py:529
  18.3 0.4 %collective-permute-start.8 = (bf16[32,512]{1,0:T(8,128)(2,1)S(1)}, bf16[32,512]{1,0:T(8,128)(2,1)S(1)}, u32[]{:S(2)}, u32[]{:S(2)}) collective-permute-start(bf16[32,512]{1,0:T(8,128)(2,1)S(1)} %bitcast.4), channel_id=1, source_target_pairs={{0,1},{1,0},{2,3},{3,2},{4,5},{5,4},{6,7},{7,6},{8,9},{9,8},{10,11... | collective-permute-start | bytes 98312 | tf_op jit(solution)/shard_map/ppermute | solution.py:543
  18.6 1.1 %shard_map.83 = bf16[4,64,512]{2,1,0:T(8,128)(2,1)} custom-call(bf16[4,6,160,128]{3,2,1,0:T(8,128)(2,1)S(1)} %get-tuple-element.47.deep_ref, bf16[2,2,128,256]{3,2,1,0:T(8,128)(2,1)S(1)} %get-tuple-element.45.far_ref), custom_call_target="tpu_custom_call" | custom-call | flops 268435456 | bytes 1048576 | tf_op jit(solution)/shard_map/pallas_call | solution.py:545
  19.8 0.0 collective-permute-done.8
  19.8 0.6 %add_multiply_fusion = f32[32,512]{1,0:T(8,128)} fusion(f32[32,512]{1,0:T(8,128)S(1)} %get-tuple-element.48, bf16[32,512]{1,0:T(8,128)(2,1)S(1)} %collective-permute-done.8), kind=kLoop, calls=%fused_computation | loop fusion | flops 49152 | bytes 163840 | tf_op jit(solution)/shard_map/mul | solution.py:547
Async XLA Ops:
  1.7 7.8 %collective-permute-start.2 = (bf16[208,128]{1,0:T(8,128)(2,1)S(1)}, bf16[208,128]{1,0:T(8,128)(2,1)S(1)}, u32[]{:S(2)}, u32[]{:S(2)}) collective-permute-start(bf16[208,128]{1,0:T(8,128)(2,1)S(1)} %get-tuple-element.28), channel_id=1, source_target_pairs={{0,8},{8,0},{1,9},{9,1},{16,24},{24,16},{17,25},{25,17},{2,10},{10... | collective-permute-start | bytes 159752 | tf_op jit(solution)/shard_map/ppermute | solution.py:45
  4.8 5.0 %collective-permute-start.3 = (bf16[208,128]{1,0:T(8,128)(2,1)S(1)}, bf16[208,128]{1,0:T(8,128)(2,1)S(1)}, u32[]{:S(2)}, u32[]{:S(2)}) collective-permute-start(bf16[208,128]{1,0:T(8,128)(2,1)S(1)} %get-tuple-element.29), channel_id=1, source_target_pairs={{8,16},{16,8},{9,17},{17,9},{0,1},{1,0},{24,25},{25,24},{10,18},{1... | collective-permute-start | bytes 159752 | tf_op jit(solution)/shard_map/ppermute | solution.py:46
  4.9 8.9 %collective-permute-start.6 = (bf16[144,128]{1,0:T(8,128)(2,1)S(1)}, bf16[144,128]{1,0:T(8,128)(2,1)S(1)}, u32[]{:S(2)}, u32[]{:S(2)}) collective-permute-start(bf16[144,128]{1,0:T(8,128)(2,1)S(1)} %get-tuple-element.34), channel_id=1, source_target_pairs={{0,2},{2,0},{1,3},{3,1},{4,6},{6,4},{5,7},{7,5},{8,10},{10,8},{9,1... | collective-permute-start | bytes 110600 | tf_op jit(solution)/shard_map/ppermute | solution.py:45
  6.5 7.6 %collective-permute-start.7 = (bf16[144,128]{1,0:T(8,128)(2,1)S(1)}, bf16[144,128]{1,0:T(8,128)(2,1)S(1)}, u32[]{:S(2)}, u32[]{:S(2)}) collective-permute-start(bf16[144,128]{1,0:T(8,128)(2,1)S(1)} %get-tuple-element.35), channel_id=1, source_target_pairs={{2,4},{4,2},{3,5},{5,3},{0,1},{1,0},{6,7},{7,6},{10,12},{12,10},{1... | collective-permute-start | bytes 110600 | tf_op jit(solution)/shard_map/ppermute | solution.py:46
  6.7 9.6 %collective-permute-start = (bf16[4,3,48,128]{3,2,1,0:T(8,128)(2,1)S(1)}, bf16[4,3,48,128]{3,2,1,0:T(8,128)(2,1)S(1)}, u32[]{:S(2)}, u32[]{:S(2)}) collective-permute-start(bf16[4,3,48,128]{3,2,1,0:T(8,128)(2,1)S(1)} %get-tuple-element.26), channel_id=1, source_target_pairs={{0,8},{8,0},{1,9},{9,1},{16,24},{24,16},{17,25},{25,17},{2,10},{10... | collective-permute-start | bytes 442376 | tf_op jit(solution)/shard_map/ppermute | solution.py:45
  9.5 6.9 %collective-permute-start.1 = (bf16[4,3,48,128]{3,2,1,0:T(8,128)(2,1)S(1)}, bf16[4,3,48,128]{3,2,1,0:T(8,128)(2,1)S(1)}, u32[]{:S(2)}, u32[]{:S(2)}) collective-permute-start(bf16[4,3,48,128]{3,2,1,0:T(8,128)(2,1)S(1)} %get-tuple-element.27), channel_id=1, source_target_pairs={{8,16},{16,8},{9,17},{17,9},{0,1},{1,0},{24,25},{25,24},{10,18},{1... | collective-permute-start | bytes 442376 | tf_op jit(solution)/shard_map/ppermute | solution.py:46
  9.8 6.5 %collective-permute-start.4 = (bf16[192,128]{1,0:T(8,128)(2,1)S(1)}, bf16[192,128]{1,0:T(8,128)(2,1)S(1)}, u32[]{:S(2)}, u32[]{:S(2)}) collective-permute-start(bf16[192,128]{1,0:T(8,128)(2,1)S(1)} %get-tuple-element.30), channel_id=1, source_target_pairs={{0,2},{2,0},{1,3},{3,1},{4,6},{6,4},{5,7},{7,5},{8,10},{10,8},{9,1... | collective-permute-start | bytes 147464 | tf_op jit(solution)/shard_map/ppermute | solution.py:45
  13.8 2.5 %collective-permute-start.5 = (bf16[192,128]{1,0:T(8,128)(2,1)S(1)}, bf16[192,128]{1,0:T(8,128)(2,1)S(1)}, u32[]{:S(2)}, u32[]{:S(2)}) collective-permute-start(bf16[192,128]{1,0:T(8,128)(2,1)S(1)} %get-tuple-element.31), channel_id=1, source_target_pairs={{2,4},{4,2},{3,5},{5,3},{0,1},{1,0},{6,7},{7,6},{10,12},{12,10},{1... | collective-permute-start | bytes 147464 | tf_op jit(solution)/shard_map/ppermute | solution.py:46
  18.3 1.5 %collective-permute-start.8 = (bf16[32,512]{1,0:T(8,128)(2,1)S(1)}, bf16[32,512]{1,0:T(8,128)(2,1)S(1)}, u32[]{:S(2)}, u32[]{:S(2)}) collective-permute-start(bf16[32,512]{1,0:T(8,128)(2,1)S(1)} %bitcast.4), channel_id=1, source_target_pairs={{0,1},{1,0},{2,3},{3,2},{4,5},{5,4},{6,7},{7,6},{8,9},{9,8},{10,11... | collective-permute-start | bytes 98312 | tf_op jit(solution)/shard_map/ppermute | solution.py:543

commit v7 on v6

--- a/solution.py
+++ b/solution.py
@@ -185,27 +185,46 @@
     return pltpu.roll(taps, 0, 1, stride=1, stride_axis=0)
 
 
-def source_kernel(
-    sa_ref, sb_ref, sidx_ref, taps_ref, bins_ref, weight_ref,
-    near_ref, mid_ref, far_ref, pair_ref, table_ref, sx_ref, wt_ref,
-):
+def put_lanes(parts, width):
+    out, pieces, at = [], [], 0
+    for tiles, first, count in parts:
+        while count:
+            j, lane = divmod(first, LANES)
+            size = min(count, LANES - lane, LANES - at)
+            pieces.append((tiles[j], at, at - lane))
+            first, count, at = first + size, count - size, at + size
+            if at == LANES:
+                out.append(join(pieces))
+                pieces, at = [], 0
+    if pieces:
+        pieces.append((jnp.zeros_like(pieces[0][0]), at, 0))
+        out.append(join(pieces))
+    assert len(out) * LANES == width
+    return jnp.concatenate(out, axis=1).astype(BF)
+
+
+def pair_weights(bins_ref, weight_ref, pair_ref, wt_ref):
     rows, cols = bins_ref.shape
-    freqs = near_ref.shape[0]
-    tiles = cols // LANES
+    wt_ref[...] = jnp.zeros(wt_ref.shape, F32)
+    wt_ref[0:DEPTHS, 0:weight_ref.shape[1]] = weight_ref[...]
+    for t in range(cols // LANES):
+        bins = bins_ref[:, t * LANES:(t + 1) * LANES]
+        for z in range(DEPTHS):
+            row = jnp.broadcast_to(wt_ref[z:z + 1, :], (rows, LANES))
+            pair_ref[z, t] = jnp.take_along_axis(row, bins, axis=1)
+
+
+def tap_rows(taps_ref, table_ref, freqs):
     for f in range(freqs):
         for part in range(2):
             at = (2 * f + part) * LANES
             table_ref[at:at + LANES, :] = jnp.zeros((LANES, table_ref.shape[1]), BF)
             table_ref[at:at + TAPS, :] = taps_ref[part, :, f, :].astype(BF)
-    table = table_ref[...]
+    return table_ref[...]
+
+
+def source_operators(sa_ref, sb_ref, sidx_ref, table, freqs, rows, own_refs, halo_refs, sx_ref):
     entries = table.shape[1]
-    wt_ref[...] = jnp.zeros(wt_ref.shape, F32)
-    wt_ref[0:DEPTHS, 0:weight_ref.shape[1]] = weight_ref[...]
-    for t in range(tiles):
-        bins = bins_ref[:, t * LANES:(t + 1) * LANES]
-        for z in range(DEPTHS):
-            row = jnp.broadcast_to(wt_ref[z:z + 1, :], (rows, LANES))
-            pair_ref[z, t] = jnp.take_along_axis(row, bins, axis=1)
     left, right = index_sides(sa_ref, sb_ref, 2 * freqs * HALO, "src")
     sx_ref[...] = jnp.zeros(sx_ref.shape, F32)
     sx_ref[0:DEPTHS, 0:rows] = sidx_ref[...].astype(F32)
@@ -221,7 +240,8 @@
             skewed = skew(taps[:, part * LANES:(part + 1) * LANES])
             found.append((jnp.where(lane >= out, skewed, 0.0), jnp.where(lane < out, skewed, 0.0)))
         ops.append(found)
-    narrow = lane_of((rows, LANES))
+    own = slice(reach, reach + rows)
+    fields = []
     for f in range(freqs):
         s0 = [[tile.astype(BF) for tile in ops[0][2 * f + part]] for part in range(2)]
         s1 = [ops[1][2 * f + part][0].astype(BF) for part in range(2)]
@@ -234,24 +254,33 @@
         by_im = dot(stack, jnp.concatenate(s0[1], axis=1))
         pr = by_re[:2 * rows] - by_im[2 * rows:]
         pi = by_im[:2 * rows] + by_re[2 * rows:]
-        size = rows + 2 * HALF
-        own = slice(reach, reach + rows)
-        parts = [
-            join([(ops[0][2 * f + part][0][own], 0, -reach), (ops[0][2 * f + part][1][own], LANES - reach, -reach)])
-            for part in range(2)
-        ]
-        parts = [jnp.where(narrow < size, part, 0.0) for part in parts]
-        minus = -parts[1]
-        near_ref[f, :, 0:LANES] = jnp.where(narrow < size, parts[0], roll(minus, size)).astype(BF)
-        near_ref[f, :, LANES:] = jnp.where(narrow < 2 * size - LANES, roll(minus, size), 0.0).astype(BF)
-        mids = [
-            join([(g[rows:, :LANES], 0, -HALF), (g[rows:, LANES:], LANES - HALF, -HALF)]) for g in (pr, pi)
-        ]
-        mid_ref[f, :, 0:LANES] = mids[0].astype(BF)
-        mid_ref[f, :, LANES:] = (-mids[1]).astype(BF)
-        re, im = pr[:rows].astype(BF), pi[:rows].astype(BF)
-        far_ref[f, 0] = jnp.concatenate([re, im], axis=0)
-        far_ref[f, 1] = jnp.concatenate([-im, re], axis=0)
+        cut = [[p[:, :LANES], p[:, LANES:]] for p in (pr, pi)]
+        fields.append((
+            [[tile[own] for tile in ops[0][2 * f + part]] for part in range(2)],
+            [[tile[rows:] for tile in tiles] for tiles in cut],
+            [[tile[:rows] for tile in tiles] for tiles in cut],
+        ))
+
+    def negative(tiles):
+        return [-tile for tile in tiles]
+
+    for z in range(DEPTHS - 1):
+        near = HALF * (z + 1)
+        planes = [fields[f][z][0] for f in range(freqs)] + [negative(fields[f][z][1]) for f in range(freqs)]
+        own_refs[z][...] = put_lanes([(tiles, HALO, rows) for tiles in planes], own_refs[z].shape[1])
+        sides = []
+        for tiles in planes:
+            sides += [(tiles, HALO - near, near), (tiles, HALO + rows, near)]
+        halo_refs[z][...] = put_lanes(sides, halo_refs[z].shape[1])
+    for f in range(freqs):
+        re, im = fields[f][DEPTHS - 1]
+        for half, planes in enumerate(((re, negative(im)), (im, re))):
+            at = slice(half * rows, (half + 1) * rows)
+            own_refs[-1][f, at, :] = put_lanes([(tiles, HALO, rows) for tiles in planes], own_refs[-1].shape[2])
+            sides = []
+            for tiles in planes:
+                sides += [(tiles, 0, HALO), (tiles, HALO + rows, HALO)]
+            halo_refs[-1][f, at, :] = put_lanes(sides, halo_refs[-1].shape[2])
 
 
 def windows(own, left, right, blocks):
@@ -308,12 +337,16 @@
     return (left, HALO + part * MID), (right, -part * MID)
 
 
-def own_kernel(x_ref, ra_ref, rb_ref, ridx_ref, table_ref, w_ref, a_ref, widx_ref):
+def own_kernel(
+    x_ref, ra_ref, rb_ref, ridx_ref, sa_ref, sb_ref, sidx_ref, taps_ref, bins_ref, weight_ref,
+    w_ref, a_ref, pair_ref, own0_ref, own1_ref, own2_ref, halo0_ref, halo1_ref, halo2_ref,
+    widx_ref, table_ref, sx_ref, wt_ref,
+):
     planes, rows, cols = x_ref.shape
     tiles = cols // LANES
     freqs = planes // 2
     blocks = w_ref.shape[1]
-    table = table_ref[...]
+    table = tap_rows(taps_ref, table_ref, freqs)
     entries = table.shape[1]
     left, right = index_sides(ra_ref, rb_ref, freqs * rows, "rec")
     widx_ref[...] = jnp.zeros(widx_ref.shape, F32)
@@ -356,16 +389,33 @@
         a_ref[z, p, b] = value
 
     receiver_steps(first, w_ref, freqs, rows, keep)
+    source_operators(
+        sa_ref, sb_ref, sidx_ref, table, freqs, rows,
+        (own0_ref, own1_ref, own2_ref), (halo0_ref, halo1_ref, halo2_ref), sx_ref,
+    )
+    pair_weights(bins_ref, weight_ref, pair_ref, wt_ref)
+
+
+def stacked(ref, planes, b, first, size):
+    at = slice(first, first + size)
+    return jnp.concatenate([jnp.concatenate([ref[p, b + k, at] for p in planes], axis=0) for k in range(2)], axis=1)
+
+
+def last_step(own, halo, own2_ref, halo2_ref, f, b, out):
+    planes = (f, own.shape[0] // 2 + f)
+    rows = own.shape[2]
+    got = dot(own2_ref[f, :out], stacked(own, planes, b, 0, rows))
+    width = len(planes) * 2 * HALO
+    return got + dot(halo2_ref[f, :out, :width], stacked(halo, planes, b, 0, 2 * HALO))
 
 
 def image_kernel(
-    ma_ref, mb_ref, sa_ref, sb_ref, ra_ref, rb_ref, w_ref, own_ref, near_ref, mid_ref, far_ref, pair_ref,
-    send_ref, keep_ref, deep_ref, a_ref, part_ref,
+    ma_ref, mb_ref, sa_ref, sb_ref, ra_ref, rb_ref, w_ref, own_ref, own0_ref, own1_ref, own2_ref,
+    halo0_ref, halo1_ref, halo2_ref, pair_ref, send_ref, keep_ref, deep_ref, a_ref, part_ref,
 ):
     _, planes, blocks, rows, _ = own_ref.shape
     freqs = planes // 2
     tiles = pair_ref.shape[1]
-    full = rows + 2 * HALO
     first = []
     for p in range(planes):
         part, f = divmod(p, freqs)
@@ -387,39 +437,26 @@
             sides.append((jnp.concatenate([top, low], axis=0), amount))
         first.append(windows(main, *sides, blocks))
 
-    def place(z, p, b):
-        return deep_ref.at[p, b] if z == DEPTHS - 1 else a_ref.at[z, p, b]
+    def halo(z):
+        return deep_ref if z == DEPTHS - 1 else a_ref.at[z]
 
     def keep(z, p, b, value):
-        to = place(z, p, b)
-        to[0:HALO] = value[:HALO]
-        to[HALO:HALO + rows] = own_ref[z, p, b]
-        to[HALO + rows:] = value[HALO:]
+        halo(z)[p, b] = value
 
     receiver_steps(first, w_ref, freqs, 2 * HALO, keep)
-
-    def field(z, p, b, reach):
-        at = slice(HALO - reach, HALO + rows + reach)
-        return jnp.concatenate([place(z, p, b)[at], place(z, p, b + 1)[at]], axis=1)
-
     images = []
-    for z, ref in ((0, near_ref), (1, mid_ref)):
-        reach = HALF * (z + 1)
-        size = rows + 2 * reach
+    for z, lhs, side in ((0, own0_ref, halo0_ref), (1, own1_ref, halo1_ref)):
+        near = HALF * (z + 1)
         out = []
         for b in range(0, blocks, 2):
-            total = None
-            for f in range(freqs):
-                both = jnp.concatenate([field(z, f, b, reach), field(z, freqs + f, b, reach)], axis=0)
-                term = dot(ref[f, :, 0:2 * size], both)
-                total = term if total is None else total + term
+            total = dot(lhs[...], stacked(own_ref.at[z], range(planes), b, 0, rows))
+            total += dot(side[...], stacked(halo(z), range(planes), b, HALO - near, 2 * near))
             out += [total[:, :LANES], total[:, LANES:]]
         images.append([gather(out, t * LANES + HALF * (DEPTHS - 1 - z), LANES) for t in range(tiles)])
     real = [None] * blocks
     for b in range(0, blocks, 2):
         for f in range(freqs):
-            got = dot(far_ref[f, 0][:rows, :full], field(2, f, b, HALO))
-            got += dot(far_ref[f, 1][:rows, :full], field(2, freqs + f, b, HALO))
+            got = last_step(own_ref.at[DEPTHS - 1], deep_ref, own2_ref, halo2_ref, f, b, rows)
             got = got.astype(BF).astype(F32)
             for k in range(2):
                 term = got[:, k * LANES:(k + 1) * LANES]
@@ -439,16 +476,14 @@
         send_ref[j - 1] = part_ref[pl.ds(pl.multiple_of(there * share, 8), share), :].astype(BF)
 
 
-def final_kernel(deep_ref, far_ref, final_ref):
-    planes, blocks, full, _ = deep_ref.shape
-    _, rows, cols = final_ref.shape
+def final_kernel(own_ref, deep_ref, own2_ref, halo2_ref, final_ref):
+    _, planes, blocks, rows, _ = own_ref.shape
+    cols = final_ref.shape[2]
     freqs = planes // 2
     for f in range(freqs):
         out = []
         for b in range(0, blocks, 2):
-            parts = [jnp.concatenate([deep_ref[p, b], deep_ref[p, b + 1]], axis=1) for p in (f, freqs + f)]
-            got = dot(far_ref[f, 0][:, :full], parts[0]) + dot(far_ref[f, 1][:, :full], parts[1])
-            got = got.astype(BF)
+            got = last_step(own_ref.at[DEPTHS - 1], deep_ref, own2_ref, halo2_ref, f, b, 2 * rows).astype(BF)
             out += [got[:, :LANES], got[:, LANES:]]
         for t in range(0, cols, LANES):
             both = gather(out, t)
@@ -480,7 +515,6 @@
     entries = tap_table.shape[1]
     count = lax.axis_size("freq")
     share = rows // count
-    full = rows + 2 * HALO
     blocks = -(-(cols + 2 * (HALO - HALF)) // OUT)
 
     main = ((planes, tiles - 1, HALO, LANES), BF)
@@ -503,46 +537,44 @@
     ea, eb = local_call(edge_kernel, [edge, edge], moved=1 << 16)(sa, sb)
     ea, eb = swaps(ea, eb, "rec")
 
-    near, mid, far, pair, table = local_call(
-        source_kernel,
-        [
-            ((freqs, rows, 2 * LANES), BF),
-            ((freqs, rows, 2 * LANES), BF),
-            ((freqs, 2, 2 * rows, 2 * LANES), BF),
-            ((DEPTHS, tiles, rows, LANES), F32),
-            ((planes * LANES, entries), BF),
-        ],
-        [((8, LANES), F32), ((8, LANES), F32)],
-        flops=1 << 28,
-        moved=2 << 20,
-    )(sa, sb, src_index, tap_table, offset_bin, bin_weight)
-    w, own = local_call(
+    sizes = [-(-planes * n // LANES) * LANES for n in (rows, 2 * HALF, 4 * HALF)]
+    deep = -(-4 * HALO // LANES) * LANES
+    w, own, pair, *lhs = local_call(
         own_kernel,
         [
             ((DEPTHS, blocks, freqs, 2, WROWS, LANES), BF),
             ((DEPTHS, planes, blocks, rows, LANES), BF),
+            ((DEPTHS, tiles, rows, LANES), F32),
+            ((rows, sizes[0]), BF),
+            ((rows, sizes[0]), BF),
+            ((freqs, 2 * rows, 2 * rows), BF),
+            ((rows, sizes[1]), BF),
+            ((rows, sizes[2]), BF),
+            ((freqs, 2 * rows, deep), BF),
         ],
-        [((8, cols), F32)],
+        [((8, cols), F32), ((planes * LANES, entries), BF), ((8, LANES), F32), ((8, LANES), F32)],
         flops=1 << 31,
         moved=5 << 20,
-    )(x, ra, rb, rec_index, table)
+    )(x, ra, rb, rec_index, sa, sb, src_index, tap_table, offset_bin, bin_weight)
     send, keep, deep = local_call(
         image_kernel,
         [
             ((max(count - 1, 1), share, cols), BF),
             ((share, cols), F32),
-            ((planes, blocks, full, LANES), BF),
+            ((planes, blocks, 2 * HALO, LANES), BF),
         ],
-        [((DEPTHS - 1, planes, blocks, full, LANES), BF), ((rows, cols), F32)],
+        [((DEPTHS - 1, planes, blocks, 2 * HALO, LANES), BF), ((rows, cols), F32)],
         flops=1 << 31,
         moved=8 << 20,
         vmem=24,
-    )(ma, mb, sa, sb, ea, eb, w, own, near, mid, far, pair)
+    )(ma, mb, sa, sb, ea, eb, w, own, *lhs, pair)
     total = keep
     for j in range(1, count):
         got = lax.ppermute(send[j - 1], "freq", [(i, partner(i, j, count)) for i in range(count)])
         total = total + got.astype(F32)
-    (final,) = local_call(final_kernel, [((planes, rows, cols), BF)], flops=1 << 28, moved=1 << 20)(deep, far)
+    (final,) = local_call(final_kernel, [((planes, rows, cols), BF)], flops=1 << 28, moved=1 << 20)(
+        own, deep, lhs[2], lhs[5]
+    )
     scale = 1.0 / math.sqrt(freqs * count * DEPTHS)
     return final.reshape(wave.shape), total * scale
 

time: 20.6 us -> 20.4 us (level)
    pallas_call x1 -> x0, Pallas kernels: 0.96 us -> none  [migrate(): local_call(source_kernel, [((freqs, rows, 2 * LANES), BF), ((freqs, rows,...]
    pallas_call x1, Pallas kernels: 2.21 us -> 3.08 us  [migrate(): local_call(own_kernel, [((DEPTHS, blocks, freqs, 2, WROWS, LANES), BF), (...]
where the time goes in v7:
time: 20.4 us; the launch traced here: 20.3 us
  starting transfers between devices  11.5 us (56%)
  Pallas kernels  7.45 us (37%)
  between operations  0.7 us (3%)
  other arithmetic  0.64 us (3%)
    ppermute x4, starting transfers between devices, swaps(): a = lax.ppermute(a, (axis, 'freq'), pairs_of(axis, 0))  10.4 us
    pallas_call x1, Pallas kernels, migrate(): local_call(own_kernel, [((DEPTHS, blocks, freqs, 2, WROWS, LANES), BF), (...  3.08 us
    pallas_call x1, Pallas kernels, migrate(): local_call(image_kernel, [((max(count - 1, 1), share, cols), BF), ((share...  1.93 us
    pallas_call x1, Pallas kernels, migrate(): local_call(final_kernel, [((planes, rows, cols), BF)], flops=1 << 28, mov...  1.14 us
    pallas_call x1, Pallas kernels, migrate(): local_call(load_kernel, [main, main, small, small] + [(a.shape, a.dtype)...  1.11 us
    ppermute x4, starting transfers between devices, swaps(): b = lax.ppermute(b, (axis, 'freq'), pairs_of(axis, 1))  0.68 us
    mul x1, other arithmetic, migrate(): return (final.reshape(wave.shape), total * scale)  0.64 us
  transfers between devices with their start and end apart: 9, of which 0 were waited for; matrix products, arithmetic and copies ran while one was open for 0% of the time, Pallas kernels for 22%

profile of v7, /device:TPU:0, one launch (start us, length us, event | category | flops | bytes accessed | tf_op | source)
XLA Modules:
  0.0 20.3 jit_solution(14126590073127772040)
XLA Ops:
  0.6 1.1 %shard_map.77 = (bf16[4,3,48,128]{3,2,1,0:T(8,128)(2,1)S(1)}, bf16[4,3,48,128]{3,2,1,0:T(8,128)(2,1)S(1)}, bf16[208,128]{1,0:T(8,128)(2,1)S(1)}, bf16[208,128]{1...) custom-call(bf16[4,64,512]{2,1,0:T(8,128)(2,1)} %bitcast.6, ...), custom_call_target="tpu_custom_call" | custom-call | bytes 1048576 | tf_op jit(solution)/shard_map/pallas_call | solution.py:524
  1.7 3.0 %collective-permute-start.2 = (bf16[208,128]{1,0:T(8,128)(2,1)S(1)}, bf16[208,128]{1,0:T(8,128)(2,1)S(1)}, u32[]{:S(2)}, u32[]{:S(2)}) collective-permute-start(bf16[208,128]{1,0:T(8,128)(2,1)S(1)} %get-tuple-element.32), channel_id=1, source_target_pairs={{0,8},{8,0},{1,9},{9,1},{16,24},{24,16},{17,25},{25,17},{2,10},{10... | collective-permute-start | bytes 159752 | tf_op jit(solution)/shard_map/ppermute | solution.py:45
  4.8 0.0 collective-permute-start.3
  4.8 0.1 shard_map.78
  4.9 1.6 %collective-permute-start = (bf16[144,128]{1,0:T(8,128)(2,1)S(1)}, bf16[144,128]{1,0:T(8,128)(2,1)S(1)}, u32[]{:S(2)}, u32[]{:S(2)}) collective-permute-start(bf16[144,128]{1,0:T(8,128)(2,1)S(1)} %get-tuple-element.30), channel_id=1, source_target_pairs={{0,2},{2,0},{1,3},{3,1},{4,6},{6,4},{5,7},{7,5},{8,10},{10,8},{9,1... | collective-permute-start | bytes 110600 | tf_op jit(solution)/shard_map/ppermute | solution.py:45
  6.5 0.2 %collective-permute-start.1 = (bf16[144,128]{1,0:T(8,128)(2,1)S(1)}, bf16[144,128]{1,0:T(8,128)(2,1)S(1)}, u32[]{:S(2)}, u32[]{:S(2)}) collective-permute-start(bf16[144,128]{1,0:T(8,128)(2,1)S(1)} %get-tuple-element.31), channel_id=1, source_target_pairs={{2,4},{4,2},{3,5},{5,3},{0,1},{1,0},{6,7},{7,6},{10,12},{12,10},{1... | collective-permute-start | bytes 110600 | tf_op jit(solution)/shard_map/ppermute | solution.py:46
  6.7 2.8 %collective-permute-start.4 = (bf16[4,3,48,128]{3,2,1,0:T(8,128)(2,1)S(1)}, bf16[4,3,48,128]{3,2,1,0:T(8,128)(2,1)S(1)}, u32[]{:S(2)}, u32[]{:S(2)}) collective-permute-start(bf16[4,3,48,128]{3,2,1,0:T(8,128)(2,1)S(1)} %get-tuple-element.39), channel_id=1, source_target_pairs={{0,8},{8,0},{1,9},{9,1},{16,24},{24,16},{17,25},{25,17},{2,10},{10... | collective-permute-start | bytes 442376 | tf_op jit(solution)/shard_map/ppermute | solution.py:45
  9.5 0.0 collective-permute-done.2.sa_ref
  9.5 0.2 %collective-permute-start.5 = (bf16[4,3,48,128]{3,2,1,0:T(8,128)(2,1)S(1)}, bf16[4,3,48,128]{3,2,1,0:T(8,128)(2,1)S(1)}, u32[]{:S(2)}, u32[]{:S(2)}) collective-permute-start(bf16[4,3,48,128]{3,2,1,0:T(8,128)(2,1)S(1)} %get-tuple-element.40), channel_id=1, source_target_pairs={{8,16},{16,8},{9,17},{17,9},{0,1},{1,0},{24,25},{25,24},{10,18},{1... | collective-permute-start | bytes 442376 | tf_op jit(solution)/shard_map/ppermute | solution.py:46
  9.7 0.0 collective-permute-done.3.sb_ref
  9.7 0.1 shard_map.80
  9.8 3.0 %collective-permute-start.6 = (bf16[192,128]{1,0:T(8,128)(2,1)S(1)}, bf16[192,128]{1,0:T(8,128)(2,1)S(1)}, u32[]{:S(2)}, u32[]{:S(2)}) collective-permute-start(bf16[192,128]{1,0:T(8,128)(2,1)S(1)} %get-tuple-element.41), channel_id=1, source_target_pairs={{0,2},{2,0},{1,3},{3,1},{4,6},{6,4},{5,7},{7,5},{8,10},{10,8},{9,1... | collective-permute-start | bytes 147464 | tf_op jit(solution)/shard_map/ppermute | solution.py:45
  12.8 0.0 collective-permute-done.ra_ref
  12.8 0.2 %collective-permute-start.7 = (bf16[192,128]{1,0:T(8,128)(2,1)S(1)}, bf16[192,128]{1,0:T(8,128)(2,1)S(1)}, u32[]{:S(2)}, u32[]{:S(2)}) collective-permute-start(bf16[192,128]{1,0:T(8,128)(2,1)S(1)} %get-tuple-element.42), channel_id=1, source_target_pairs={{2,4},{4,2},{3,5},{5,3},{0,1},{1,0},{6,7},{7,6},{10,12},{12,10},{1... | collective-permute-start | bytes 147464 | tf_op jit(solution)/shard_map/ppermute | solution.py:46
  13.1 0.0 collective-permute-done.1.rb_ref
  13.1 3.1 %shard_map.79 = (bf16[3,6,2,2,224,128]{5,4,3,2,1,0:T(8,128)(2,1)S(1)}, bf16[3,4,6,64,128]{4,3,2,1,0:T(8,128)(2,1)S(1)}, f32[3,4,64,128]{3,2,1,0:T(8,128)S(1)}, b...) custom-call(bf16[4,64,512]{2,1,0:T(8,128)(2,1)S(1)} %get-tuple-eleme, ...), custom_call_target="tpu_custom_call" | custom-call | flops 2147483648 | bytes 5242880 | tf_op jit(solution)/shard_map/pallas_call | solution.py:542
  16.2 0.0 collective-permute-done.6.ra_ref
  16.2 0.0 collective-permute-done.7.rb_ref
  16.2 0.0 collective-permute-done.4.ma_ref
  16.2 0.0 collective-permute-done.5.mb_ref
  16.2 1.9 %shard_map.81 = (bf16[1,32,512]{2,1,0:T(8,128)(2,1)S(1)}, f32[32,512]{1,0:T(8,128)S(1)}, bf16[4,6,96,128]{3,2,1,0:T(8,128)(2,1)S(1)}) custom-call(bf16[4,3,48,128]{3,2,1,0:T(8,128)(2,1)S(1)} %collective-permute-done.4.ma_ref, bf16[4,3,48,128]{3,2,1,0:T(8,128)(2,1)S(1)} %collective-permute-done.5.mb_ref, bf16[208,128]{1,0:T(8,128)(2,1)S(1)} %collective-permute-done.2.sa_ref, ...), custom_call_target="tpu_custom_call" | custom-call | flops 2147483648 | bytes 8388608 | tf_op jit(solution)/shard_map/pallas_call | solution.py:559
  18.1 0.4 %collective-permute-start.8 = (bf16[32,512]{1,0:T(8,128)(2,1)S(1)}, bf16[32,512]{1,0:T(8,128)(2,1)S(1)}, u32[]{:S(2)}, u32[]{:S(2)}) collective-permute-start(bf16[32,512]{1,0:T(8,128)(2,1)S(1)} %bitcast.4), channel_id=1, source_target_pairs={{0,1},{1,0},{2,3},{3,2},{4,5},{5,4},{6,7},{7,6},{8,9},{9,8},{10,11... | collective-permute-start | bytes 98312 | tf_op jit(solution)/shard_map/ppermute | solution.py:573
  18.5 1.1 %shard_map.82 = bf16[4,64,512]{2,1,0:T(8,128)(2,1)} custom-call(bf16[3,4,6,64,128]{4,3,2,1,0:T(8,128)(2,1)S(1)} %get-tuple-element.38.own_ref, bf16[4,6,96,128]{3,2,1,0:T(8,128)(2,1)S(1)} %get-tuple-element.51.deep_ref, bf16[2,128,128]{2,1,0:T(8,128)(2,1)S(1)} %get-tuple-element.46.own2_ref, bf16[2,128,256]{2,1,0:T(8,128)(2,1)S(1)} %get-tuple-element.49.halo2_ref), custom_call_target="tpu_custom_call" | custom-call | flops 268435456 | bytes 1048576 | tf_op jit(solution)/shard_map/pallas_call | solution.py:575
  19.6 0.0 collective-permute-done.8
  19.6 0.6 %add_multiply_fusion = f32[32,512]{1,0:T(8,128)} fusion(f32[32,512]{1,0:T(8,128)S(1)} %get-tuple-element.52, bf16[32,512]{1,0:T(8,128)(2,1)S(1)} %collective-permute-done.8), kind=kLoop, calls=%fused_computation | loop fusion | flops 49152 | bytes 163840 | tf_op jit(solution)/shard_map/mul | solution.py:579
Async XLA Ops:
  1.7 7.8 %collective-permute-start.2 = (bf16[208,128]{1,0:T(8,128)(2,1)S(1)}, bf16[208,128]{1,0:T(8,128)(2,1)S(1)}, u32[]{:S(2)}, u32[]{:S(2)}) collective-permute-start(bf16[208,128]{1,0:T(8,128)(2,1)S(1)} %get-tuple-element.32), channel_id=1, source_target_pairs={{0,8},{8,0},{1,9},{9,1},{16,24},{24,16},{17,25},{25,17},{2,10},{10... | collective-permute-start | bytes 159752 | tf_op jit(solution)/shard_map/ppermute | solution.py:45
  4.8 5.0 %collective-permute-start.3 = (bf16[208,128]{1,0:T(8,128)(2,1)S(1)}, bf16[208,128]{1,0:T(8,128)(2,1)S(1)}, u32[]{:S(2)}, u32[]{:S(2)}) collective-permute-start(bf16[208,128]{1,0:T(8,128)(2,1)S(1)} %get-tuple-element.33), channel_id=1, source_target_pairs={{8,16},{16,8},{9,17},{17,9},{0,1},{1,0},{24,25},{25,24},{10,18},{1... | collective-permute-start | bytes 159752 | tf_op jit(solution)/shard_map/ppermute | solution.py:46
  4.9 8.0 %collective-permute-start = (bf16[144,128]{1,0:T(8,128)(2,1)S(1)}, bf16[144,128]{1,0:T(8,128)(2,1)S(1)}, u32[]{:S(2)}, u32[]{:S(2)}) collective-permute-start(bf16[144,128]{1,0:T(8,128)(2,1)S(1)} %get-tuple-element.30), channel_id=1, source_target_pairs={{0,2},{2,0},{1,3},{3,1},{4,6},{6,4},{5,7},{7,5},{8,10},{10,8},{9,1... | collective-permute-start | bytes 110600 | tf_op jit(solution)/shard_map/ppermute | solution.py:45
  6.5 6.6 %collective-permute-start.1 = (bf16[144,128]{1,0:T(8,128)(2,1)S(1)}, bf16[144,128]{1,0:T(8,128)(2,1)S(1)}, u32[]{:S(2)}, u32[]{:S(2)}) collective-permute-start(bf16[144,128]{1,0:T(8,128)(2,1)S(1)} %get-tuple-element.31), channel_id=1, source_target_pairs={{2,4},{4,2},{3,5},{5,3},{0,1},{1,0},{6,7},{7,6},{10,12},{12,10},{1... | collective-permute-start | bytes 110600 | tf_op jit(solution)/shard_map/ppermute | solution.py:46
  6.7 9.4 %collective-permute-start.4 = (bf16[4,3,48,128]{3,2,1,0:T(8,128)(2,1)S(1)}, bf16[4,3,48,128]{3,2,1,0:T(8,128)(2,1)S(1)}, u32[]{:S(2)}, u32[]{:S(2)}) collective-permute-start(bf16[4,3,48,128]{3,2,1,0:T(8,128)(2,1)S(1)} %get-tuple-element.39), channel_id=1, source_target_pairs={{0,8},{8,0},{1,9},{9,1},{16,24},{24,16},{17,25},{25,17},{2,10},{10... | collective-permute-start | bytes 442376 | tf_op jit(solution)/shard_map/ppermute | solution.py:45
  9.5 6.7 %collective-permute-start.5 = (bf16[4,3,48,128]{3,2,1,0:T(8,128)(2,1)S(1)}, bf16[4,3,48,128]{3,2,1,0:T(8,128)(2,1)S(1)}, u32[]{:S(2)}, u32[]{:S(2)}) collective-permute-start(bf16[4,3,48,128]{3,2,1,0:T(8,128)(2,1)S(1)} %get-tuple-element.40), channel_id=1, source_target_pairs={{8,16},{16,8},{9,17},{17,9},{0,1},{1,0},{24,25},{25,24},{10,18},{1... | collective-permute-start | bytes 442376 | tf_op jit(solution)/shard_map/ppermute | solution.py:46
  9.8 6.3 %collective-permute-start.6 = (bf16[192,128]{1,0:T(8,128)(2,1)S(1)}, bf16[192,128]{1,0:T(8,128)(2,1)S(1)}, u32[]{:S(2)}, u32[]{:S(2)}) collective-permute-start(bf16[192,128]{1,0:T(8,128)(2,1)S(1)} %get-tuple-element.41), channel_id=1, source_target_pairs={{0,2},{2,0},{1,3},{3,1},{4,6},{6,4},{5,7},{7,5},{8,10},{10,8},{9,1... | collective-permute-start | bytes 147464 | tf_op jit(solution)/shard_map/ppermute | solution.py:45
  12.8 3.3 %collective-permute-start.7 = (bf16[192,128]{1,0:T(8,128)(2,1)S(1)}, bf16[192,128]{1,0:T(8,128)(2,1)S(1)}, u32[]{:S(2)}, u32[]{:S(2)}) collective-permute-start(bf16[192,128]{1,0:T(8,128)(2,1)S(1)} %get-tuple-element.42), channel_id=1, source_target_pairs={{2,4},{4,2},{3,5},{5,3},{0,1},{1,0},{6,7},{7,6},{10,12},{12,10},{1... | collective-permute-start | bytes 147464 | tf_op jit(solution)/shard_map/ppermute | solution.py:46
  18.1 1.5 %collective-permute-start.8 = (bf16[32,512]{1,0:T(8,128)(2,1)S(1)}, bf16[32,512]{1,0:T(8,128)(2,1)S(1)}, u32[]{:S(2)}, u32[]{:S(2)}) collective-permute-start(bf16[32,512]{1,0:T(8,128)(2,1)S(1)} %bitcast.4), channel_id=1, source_target_pairs={{0,1},{1,0},{2,3},{3,2},{4,5},{5,4},{6,7},{7,6},{8,9},{9,8},{10,11... | collective-permute-start | bytes 98312 | tf_op jit(solution)/shard_map/ppermute | solution.py:573

commit v8 on v6

--- a/solution.py
+++ b/solution.py
@@ -93,19 +93,16 @@
 
 
 def load_kernel(*refs):
-    count = 6
-    sources, targets = refs[:count], refs[count + 4:2 * count + 4]
-    ma_ref, mb_ref, sa_ref, sb_ref = refs[count:count + 4]
-    sem = refs[2 * count + 4]
+    count = len(refs) // 2 - 1
+    sources, targets = refs[:count], refs[count + 2:2 * count + 2]
+    sa_ref, sb_ref = refs[count:count + 2]
+    sem = refs[2 * count + 2]
     copies = [pltpu.make_async_copy(s, t, sem.at[i]) for i, (s, t) in enumerate(zip(sources, targets))]
     for copy in copies:
         copy.start()
     x_ref, sidx_ref = targets[:2]
     planes, rows, cols = x_ref.shape
-    even = is_even("src")
-    low = rows - HALO
-    at_a = pl.multiple_of(jnp.where(even, low, 0), 16)
-    at_b = pl.multiple_of(jnp.where(even, 0, low), 16)
+    at_a, at_b = halo_rows(rows)
     lane = lane_of((HALO, LANES))
     base = planes * HALO
     copies[1].wait()
@@ -115,14 +112,20 @@
         small[base:base + DEPTHS, 0:rows] = index
     copies[0].wait()
     for p in range(planes):
-        for at, main, small in ((at_a, ma_ref, sa_ref), (at_b, mb_ref, sb_ref)):
-            tiles = [x_ref[p, pl.ds(at, HALO), t:t + LANES] for t in range(0, cols, LANES)]
-            main[p, 0] = jnp.where(lane < MID, tiles[-1], tiles[0])
-            for t, tile in enumerate(tiles[1:-1]):
-                main[p, t + 1] = tile
-            small[p * HALO:(p + 1) * HALO, :] = jnp.where(lane < MID, tiles[0], tiles[-1])
+        for at, small in ((at_a, sa_ref), (at_b, sb_ref)):
+            ends = [x_ref[p, pl.ds(at, HALO), t:t + LANES] for t in (0, cols - LANES)]
+            small[p * HALO:(p + 1) * HALO, :] = jnp.where(lane < MID, *ends)
     for copy in copies[2:]:
         copy.wait()
+
+
+def halo_rows(rows):
+    even = is_even("src")
+    low = rows - HALO
+    return (
+        pl.multiple_of(jnp.where(even, low, 0), 16),
+        pl.multiple_of(jnp.where(even, 0, low), 16),
+    )
 
 
 def put_edges(ends, at, tail, head):
@@ -135,9 +138,16 @@
     ends[1][place, :] = jnp.where(even, left, right)
 
 
-def near_kernel(x_ref, ridx_ref, ra_ref, rb_ref):
+def pack_kernel(x_ref, ridx_ref, ma_ref, mb_ref, ra_ref, rb_ref):
     planes, rows, cols = x_ref.shape
     freqs = planes // 2
+    lane = lane_of((HALO, LANES))
+    for p in range(planes):
+        for at, main in zip(halo_rows(rows), (ma_ref, mb_ref)):
+            tiles = [x_ref[p, pl.ds(at, HALO), t:t + LANES] for t in range(0, cols, LANES)]
+            main[p, 0] = jnp.where(lane < MID, tiles[-1], tiles[0])
+            for t, tile in enumerate(tiles[1:-1]):
+                main[p, t + 1] = tile
     ends = (ra_ref, rb_ref)
     last = cols - LANES
     for f in range(freqs):
@@ -186,9 +196,15 @@
 
 
 def source_kernel(
-    sa_ref, sb_ref, sidx_ref, taps_ref, bins_ref, weight_ref,
-    near_ref, mid_ref, far_ref, pair_ref, table_ref, sx_ref, wt_ref,
+    sa_ref, sb_ref, sidx_ref, taps_ref, bins_hbm, weight_hbm,
+    near_ref, mid_ref, far_ref, pair_ref, table_ref, sx_ref, wt_ref, bins_ref, weight_ref, sem,
 ):
+    copies = [
+        pltpu.make_async_copy(source, target, sem.at[i])
+        for i, (source, target) in enumerate(((bins_hbm, bins_ref), (weight_hbm, weight_ref)))
+    ]
+    for copy in copies:
+        copy.start()
     rows, cols = bins_ref.shape
     freqs = near_ref.shape[0]
     tiles = cols // LANES
@@ -199,13 +215,6 @@
             table_ref[at:at + TAPS, :] = taps_ref[part, :, f, :].astype(BF)
     table = table_ref[...]
     entries = table.shape[1]
-    wt_ref[...] = jnp.zeros(wt_ref.shape, F32)
-    wt_ref[0:DEPTHS, 0:weight_ref.shape[1]] = weight_ref[...]
-    for t in range(tiles):
-        bins = bins_ref[:, t * LANES:(t + 1) * LANES]
-        for z in range(DEPTHS):
-            row = jnp.broadcast_to(wt_ref[z:z + 1, :], (rows, LANES))
-            pair_ref[z, t] = jnp.take_along_axis(row, bins, axis=1)
     left, right = index_sides(sa_ref, sb_ref, 2 * freqs * HALO, "src")
     sx_ref[...] = jnp.zeros(sx_ref.shape, F32)
     sx_ref[0:DEPTHS, 0:rows] = sidx_ref[...].astype(F32)
@@ -252,6 +261,15 @@
         re, im = pr[:rows].astype(BF), pi[:rows].astype(BF)
         far_ref[f, 0] = jnp.concatenate([re, im], axis=0)
         far_ref[f, 1] = jnp.concatenate([-im, re], axis=0)
+    for copy in copies:
+        copy.wait()
+    wt_ref[...] = jnp.zeros(wt_ref.shape, F32)
+    wt_ref[0:DEPTHS, 0:weight_ref.shape[1]] = weight_ref[...]
+    for t in range(tiles):
+        bins = bins_ref[:, t * LANES:(t + 1) * LANES]
+        for z in range(DEPTHS):
+            row = jnp.broadcast_to(wt_ref[z:z + 1, :], (rows, LANES))
+            pair_ref[z, t] = jnp.take_along_axis(row, bins, axis=1)
 
 
 def windows(own, left, right, blocks):
@@ -485,24 +503,25 @@
 
     main = ((planes, tiles - 1, HALO, LANES), BF)
     small = ((planes * HALO + IDX_ROWS, LANES), BF)
-    inputs = (wave.reshape(planes, rows, cols), src_index, rec_index, jnp.transpose(tap_table, (0, 3, 2, 1)), offset_bin, bin_weight)
+    inputs = (wave.reshape(planes, rows, cols), src_index, rec_index, jnp.transpose(tap_table, (0, 3, 2, 1)))
     inputs = tuple(pltpu.with_memory_space_constraint(a, pltpu.HBM) for a in inputs)
-    ma, mb, sa, sb, x, src_index, rec_index, tap_table, offset_bin, bin_weight = local_call(
+    sa, sb, x, src_index, rec_index, tap_table = local_call(
         load_kernel,
-        [main, main, small, small] + [(a.shape, a.dtype) for a in inputs],
+        [small, small] + [(a.shape, a.dtype) for a in inputs],
         [pltpu.SemaphoreType.DMA((len(inputs),))],
         moved=1 << 20,
         in_specs=[pl.BlockSpec(memory_space=pltpu.HBM)] * len(inputs),
     )(*inputs)
     sa, sb = swaps(sa, sb, "src")
+    near = ((freqs * rows + IDX_ROWS, LANES), BF)
+    ma, mb, ra, rb = local_call(pack_kernel, [main, main, near, near], moved=1 << 18)(x, rec_index)
     ma, mb = swaps(ma, mb, "src")
-    near = ((freqs * rows + IDX_ROWS, LANES), BF)
-    ra, rb = local_call(near_kernel, [near, near], moved=1 << 16)(x, rec_index)
     ra, rb = swaps(ra, rb, "rec")
     edge = ((freqs * 2 * HALO, LANES), BF)
     ea, eb = local_call(edge_kernel, [edge, edge], moved=1 << 16)(sa, sb)
     ea, eb = swaps(ea, eb, "rec")
 
+    late = tuple(pltpu.with_memory_space_constraint(a, pltpu.HBM) for a in (offset_bin, bin_weight))
     near, mid, far, pair, table = local_call(
         source_kernel,
         [
@@ -512,10 +531,14 @@
             ((DEPTHS, tiles, rows, LANES), F32),
             ((planes * LANES, entries), BF),
         ],
-        [((8, LANES), F32), ((8, LANES), F32)],
+        [((8, LANES), F32), ((8, LANES), F32)]
+        + [(a.shape, a.dtype) for a in late]
+        + [pltpu.SemaphoreType.DMA((len(late),))],
         flops=1 << 28,
         moved=2 << 20,
-    )(sa, sb, src_index, tap_table, offset_bin, bin_weight)
+        in_specs=[pl.BlockSpec(memory_space=pltpu.VMEM)] * 4
+        + [pl.BlockSpec(memory_space=pltpu.HBM)] * len(late),
+    )(sa, sb, src_index, tap_table, *late)
     w, own = local_call(
         own_kernel,
         [

time: 20.6 us -> 21.2 us (1.029)
  Pallas kernels: 7.52 us -> 8.19 us
    pallas_call x1, Pallas kernels: 0.96 us -> 1.7 us  [migrate(): local_call(source_kernel, [((freqs, rows, 2 * LANES), BF), ((freqs, rows,...]
  transfers between devices with their start and end apart: 9 -> 9, of which waited for: 0 -> 0; matrix products, arithmetic and copies ran while one was open for 0% -> 0% of each run, Pallas kernels for 22% -> 25%
where the time goes in v8:
time: 21.2 us; the launch traced here: 21.1 us
  starting transfers between devices  11.5 us (54%)
  Pallas kernels  8.19 us (39%)
  between operations  0.71 us (3%)
  other arithmetic  0.64 us (3%)
    ppermute x4, starting transfers between devices, swaps(): a = lax.ppermute(a, (axis, 'freq'), pairs_of(axis, 0))  10.4 us
    pallas_call x1, Pallas kernels, migrate(): local_call(own_kernel, [((DEPTHS, blocks, freqs, 2, WROWS, LANES), BF), (...  2.21 us
    pallas_call x1, Pallas kernels, migrate(): local_call(image_kernel, [((max(count - 1, 1), share, cols), BF), ((share...  1.92 us
    pallas_call x1, Pallas kernels, migrate(): local_call(source_kernel, [((freqs, rows, 2 * LANES), BF), ((freqs, rows,...  1.7 us
    pallas_call x1, Pallas kernels, migrate(): local_call(final_kernel, [((planes, rows, cols), BF)], flops=1 << 28, mov...  1.13 us
    pallas_call x1, Pallas kernels, migrate(): local_call(load_kernel, [small, small] + [(a.shape, a.dtype) for a in inp...  1.03 us
    ppermute x4, starting transfers between devices, swaps(): b = lax.ppermute(b, (axis, 'freq'), pairs_of(axis, 1))  0.74 us
    mul x1, other arithmetic, migrate(): return (final.reshape(wave.shape), total * scale)  0.64 us
  transfers between devices with their start and end apart: 9, of which 0 were waited for; matrix products, arithmetic and copies ran while one was open for 0% of the time, Pallas kernels for 25%

profile of v8, /device:TPU:0, one launch (start us, length us, event | category | flops | bytes accessed | tf_op | source)
XLA Modules:
  0.0 21.1 jit_solution(558262699669127857)
XLA Ops:
  0.6 1.0 %shard_map.77 = (bf16[208,128]{1,0:T(8,128)(2,1)S(1)}, bf16[208,128]{1,0:T(8,128)(2,1)S(1)}, bf16[4,64,512]{2,1,0:T(8,128)(2,1)S(1)}, s32[3,64]{1,0:T(4,128)S(1)...) custom-call(bf16[4,64,512]{2,1,0:T(8,128)(2,1)} %bitcast.5, s32[3,64]{1,0:T(4,128)} %refs_1_.1, s32[3,512]{1,0:T(4,128)} %refs_2_.1, ...), custom_call_target="tpu_custom_call" | custom-call | bytes 1048576 | tf_op jit(solution)/shard_map/pallas_call | solution.py:508
  1.7 3.0 %collective-permute-start.2 = (bf16[208,128]{1,0:T(8,128)(2,1)S(1)}, bf16[208,128]{1,0:T(8,128)(2,1)S(1)}, u32[]{:S(2)}, u32[]{:S(2)}) collective-permute-start(bf16[208,128]{1,0:T(8,128)(2,1)S(1)} %get-tuple-element.28), channel_id=1, source_target_pairs={{0,8},{8,0},{1,9},{9,1},{16,24},{24,16},{17,25},{25,17},{2,10},{10... | collective-permute-start | bytes 159752 | tf_op jit(solution)/shard_map/ppermute | solution.py:45
  4.7 0.0 collective-permute-start.3
  4.7 0.1 shard_map.78
  4.8 1.6 %collective-permute-start.6 = (bf16[144,128]{1,0:T(8,128)(2,1)S(1)}, bf16[144,128]{1,0:T(8,128)(2,1)S(1)}, u32[]{:S(2)}, u32[]{:S(2)}) collective-permute-start(bf16[144,128]{1,0:T(8,128)(2,1)S(1)} %get-tuple-element.32), channel_id=1, source_target_pairs={{0,2},{2,0},{1,3},{3,1},{4,6},{6,4},{5,7},{7,5},{8,10},{10,8},{9,1... | collective-permute-start | bytes 110600 | tf_op jit(solution)/shard_map/ppermute | solution.py:45
  6.4 0.2 %collective-permute-start.7 = (bf16[144,128]{1,0:T(8,128)(2,1)S(1)}, bf16[144,128]{1,0:T(8,128)(2,1)S(1)}, u32[]{:S(2)}, u32[]{:S(2)}) collective-permute-start(bf16[144,128]{1,0:T(8,128)(2,1)S(1)} %get-tuple-element.33), channel_id=1, source_target_pairs={{2,4},{4,2},{3,5},{5,3},{0,1},{1,0},{6,7},{7,6},{10,12},{12,10},{1... | collective-permute-start | bytes 110600 | tf_op jit(solution)/shard_map/ppermute | solution.py:46
  6.7 2.8 %collective-permute-start = (bf16[4,3,48,128]{3,2,1,0:T(8,128)(2,1)S(1)}, bf16[4,3,48,128]{3,2,1,0:T(8,128)(2,1)S(1)}, u32[]{:S(2)}, u32[]{:S(2)}) collective-permute-start(bf16[4,3,48,128]{3,2,1,0:T(8,128)(2,1)S(1)} %get-tuple-element.26), channel_id=1, source_target_pairs={{0,8},{8,0},{1,9},{9,1},{16,24},{24,16},{17,25},{25,17},{2,10},{10... | collective-permute-start | bytes 442376 | tf_op jit(solution)/shard_map/ppermute | solution.py:45
  9.4 0.0 collective-permute-done.2.sa_ref
  9.4 0.2 %collective-permute-start.1 = (bf16[4,3,48,128]{3,2,1,0:T(8,128)(2,1)S(1)}, bf16[4,3,48,128]{3,2,1,0:T(8,128)(2,1)S(1)}, u32[]{:S(2)}, u32[]{:S(2)}) collective-permute-start(bf16[4,3,48,128]{3,2,1,0:T(8,128)(2,1)S(1)} %get-tuple-element.27), channel_id=1, source_target_pairs={{8,16},{16,8},{9,17},{17,9},{0,1},{1,0},{24,25},{25,24},{10,18},{1... | collective-permute-start | bytes 442376 | tf_op jit(solution)/shard_map/ppermute | solution.py:46
  9.7 0.0 collective-permute-done.3.sb_ref
  9.7 0.1 shard_map.79
  9.8 3.0 %collective-permute-start.4 = (bf16[192,128]{1,0:T(8,128)(2,1)S(1)}, bf16[192,128]{1,0:T(8,128)(2,1)S(1)}, u32[]{:S(2)}, u32[]{:S(2)}) collective-permute-start(bf16[192,128]{1,0:T(8,128)(2,1)S(1)} %get-tuple-element.30), channel_id=1, source_target_pairs={{0,2},{2,0},{1,3},{3,1},{4,6},{6,4},{5,7},{7,5},{8,10},{10,8},{9,1... | collective-permute-start | bytes 147464 | tf_op jit(solution)/shard_map/ppermute | solution.py:45
  12.8 1.7 %shard_map.80 = (bf16[2,64,256]{2,1,0:T(8,128)(2,1)S(1)}, bf16[2,64,256]{2,1,0:T(8,128)(2,1)S(1)}, bf16[2,2,128,256]{3,2,1,0:T(8,128)(2,1)S(1)}, f32[3,4,64,128]{3,2,1,0:T(8,128)S(1)}, bf16[512,64]{1,0:T(8,128)(2,1)S(1)}) custom-call(bf16[208,128]{1,0:T(8,128)(2,1)S(1)} %collective-permute-done.2.sa_ref, bf16[208,128]{1,0:T(8,128)(2,1)S(1)} %collective-permute-done.3.sb_ref, ...), custom_call_target="tpu_custom_call" | custom-call | flops 268435456 | bytes 2097152 | tf_op jit(solution)/shard_map/pallas_call | solution.py:525
  14.5 0.0 collective-permute-done.6.ra_ref
  14.5 0.3 %collective-permute-start.5 = (bf16[192,128]{1,0:T(8,128)(2,1)S(1)}, bf16[192,128]{1,0:T(8,128)(2,1)S(1)}, u32[]{:S(2)}, u32[]{:S(2)}) collective-permute-start(bf16[192,128]{1,0:T(8,128)(2,1)S(1)} %get-tuple-element.31), channel_id=1, source_target_pairs={{2,4},{4,2},{3,5},{5,3},{0,1},{1,0},{6,7},{7,6},{10,12},{12,10},{1... | collective-permute-start | bytes 147464 | tf_op jit(solution)/shard_map/ppermute | solution.py:46
  14.8 0.0 collective-permute-done.7.rb_ref
  14.8 2.2 %shard_map.81 = (bf16[3,6,2,2,224,128]{5,4,3,2,1,0:T(8,128)(2,1)S(1)}, bf16[3,4,6,64,128]{4,3,2,1,0:T(8,128)(2,1)S(1)}) custom-call(bf16[4,64,512]{2,1,0:T(8,128)(2,1)S(1)} %get-tuple-element.24.x_ref, bf16[144,128]{1,0:T(8,128)(2,1)S(1)} %collective-permute-done.6.ra_ref, bf16[144,128]{1,0:T(8,128)(2,1)S(1)} %collective-permute-done.7.rb_ref, ...), custom_call_target="tpu_custom_call" | custom-call | flops 2147483648 | bytes 5242880 | tf_op jit(solution)/shard_map/pallas_call | solution.py:542
  17.0 0.0 collective-permute-done.4.ra_ref
  17.0 0.0 collective-permute-done.5.rb_ref
  17.0 0.0 collective-permute-done.ma_ref
  17.0 0.0 collective-permute-done.1.mb_ref
  17.0 1.9 %shard_map.82 = (bf16[1,32,512]{2,1,0:T(8,128)(2,1)S(1)}, f32[32,512]{1,0:T(8,128)S(1)}, bf16[4,6,160,128]{3,2,1,0:T(8,128)(2,1)S(1)}) custom-call(bf16[4,3,48,128]{3,2,1,0:T(8,128)(2,1)S(1)} %collective-permute-done.ma_ref, bf16[4,3,48,128]{3,2,1,0:T(8,128)(2,1)S(1)} %collective-permute-done.1.mb_ref, bf16[208,128]{1,0:T(8,128)(2,1)S(1)} %collective-permute-done.2.sa_ref, ...), custom_call_target="tpu_custom_call" | custom-call | flops 2147483648 | bytes 8388608 | tf_op jit(solution)/shard_map/pallas_call | solution.py:552
  19.0 0.4 %collective-permute-start.8 = (bf16[32,512]{1,0:T(8,128)(2,1)S(1)}, bf16[32,512]{1,0:T(8,128)(2,1)S(1)}, u32[]{:S(2)}, u32[]{:S(2)}) collective-permute-start(bf16[32,512]{1,0:T(8,128)(2,1)S(1)} %bitcast.4), channel_id=1, source_target_pairs={{0,1},{1,0},{2,3},{3,2},{4,5},{5,4},{6,7},{7,6},{8,9},{9,8},{10,11... | collective-permute-start | bytes 98312 | tf_op jit(solution)/shard_map/ppermute | solution.py:566
  19.3 1.1 %shard_map.83 = bf16[4,64,512]{2,1,0:T(8,128)(2,1)} custom-call(bf16[4,6,160,128]{3,2,1,0:T(8,128)(2,1)S(1)} %get-tuple-element.43.deep_ref, bf16[2,2,128,256]{3,2,1,0:T(8,128)(2,1)S(1)} %get-tuple-element.41.far_ref), custom_call_target="tpu_custom_call" | custom-call | flops 268435456 | bytes 1048576 | tf_op jit(solution)/shard_map/pallas_call | solution.py:568
  20.4 0.0 collective-permute-done.8
  20.4 0.6 %add_multiply_fusion = f32[32,512]{1,0:T(8,128)} fusion(f32[32,512]{1,0:T(8,128)S(1)} %get-tuple-element.44, bf16[32,512]{1,0:T(8,128)(2,1)S(1)} %collective-permute-done.8), kind=kLoop, calls=%fused_computation | loop fusion | flops 49152 | bytes 163840 | tf_op jit(solution)/shard_map/mul | solution.py:570
Async XLA Ops:
  1.7 7.8 %collective-permute-start.2 = (bf16[208,128]{1,0:T(8,128)(2,1)S(1)}, bf16[208,128]{1,0:T(8,128)(2,1)S(1)}, u32[]{:S(2)}, u32[]{:S(2)}) collective-permute-start(bf16[208,128]{1,0:T(8,128)(2,1)S(1)} %get-tuple-element.28), channel_id=1, source_target_pairs={{0,8},{8,0},{1,9},{9,1},{16,24},{24,16},{17,25},{25,17},{2,10},{10... | collective-permute-start | bytes 159752 | tf_op jit(solution)/shard_map/ppermute | solution.py:45
  4.7 5.0 %collective-permute-start.3 = (bf16[208,128]{1,0:T(8,128)(2,1)S(1)}, bf16[208,128]{1,0:T(8,128)(2,1)S(1)}, u32[]{:S(2)}, u32[]{:S(2)}) collective-permute-start(bf16[208,128]{1,0:T(8,128)(2,1)S(1)} %get-tuple-element.29), channel_id=1, source_target_pairs={{8,16},{16,8},{9,17},{17,9},{0,1},{1,0},{24,25},{25,24},{10,18},{1... | collective-permute-start | bytes 159752 | tf_op jit(solution)/shard_map/ppermute | solution.py:46
  4.8 9.7 %collective-permute-start.6 = (bf16[144,128]{1,0:T(8,128)(2,1)S(1)}, bf16[144,128]{1,0:T(8,128)(2,1)S(1)}, u32[]{:S(2)}, u32[]{:S(2)}) collective-permute-start(bf16[144,128]{1,0:T(8,128)(2,1)S(1)} %get-tuple-element.32), channel_id=1, source_target_pairs={{0,2},{2,0},{1,3},{3,1},{4,6},{6,4},{5,7},{7,5},{8,10},{10,8},{9,1... | collective-permute-start | bytes 110600 | tf_op jit(solution)/shard_map/ppermute | solution.py:45
  6.4 8.3 %collective-permute-start.7 = (bf16[144,128]{1,0:T(8,128)(2,1)S(1)}, bf16[144,128]{1,0:T(8,128)(2,1)S(1)}, u32[]{:S(2)}, u32[]{:S(2)}) collective-permute-start(bf16[144,128]{1,0:T(8,128)(2,1)S(1)} %get-tuple-element.33), channel_id=1, source_target_pairs={{2,4},{4,2},{3,5},{5,3},{0,1},{1,0},{6,7},{7,6},{10,12},{12,10},{1... | collective-permute-start | bytes 110600 | tf_op jit(solution)/shard_map/ppermute | solution.py:46
  6.7 10.3 %collective-permute-start = (bf16[4,3,48,128]{3,2,1,0:T(8,128)(2,1)S(1)}, bf16[4,3,48,128]{3,2,1,0:T(8,128)(2,1)S(1)}, u32[]{:S(2)}, u32[]{:S(2)}) collective-permute-start(bf16[4,3,48,128]{3,2,1,0:T(8,128)(2,1)S(1)} %get-tuple-element.26), channel_id=1, source_target_pairs={{0,8},{8,0},{1,9},{9,1},{16,24},{24,16},{17,25},{25,17},{2,10},{10... | collective-permute-start | bytes 442376 | tf_op jit(solution)/shard_map/ppermute | solution.py:45
  9.4 7.6 %collective-permute-start.1 = (bf16[4,3,48,128]{3,2,1,0:T(8,128)(2,1)S(1)}, bf16[4,3,48,128]{3,2,1,0:T(8,128)(2,1)S(1)}, u32[]{:S(2)}, u32[]{:S(2)}) collective-permute-start(bf16[4,3,48,128]{3,2,1,0:T(8,128)(2,1)S(1)} %get-tuple-element.27), channel_id=1, source_target_pairs={{8,16},{16,8},{9,17},{17,9},{0,1},{1,0},{24,25},{25,24},{10,18},{1... | collective-permute-start | bytes 442376 | tf_op jit(solution)/shard_map/ppermute | solution.py:46
  9.8 7.2 %collective-permute-start.4 = (bf16[192,128]{1,0:T(8,128)(2,1)S(1)}, bf16[192,128]{1,0:T(8,128)(2,1)S(1)}, u32[]{:S(2)}, u32[]{:S(2)}) collective-permute-start(bf16[192,128]{1,0:T(8,128)(2,1)S(1)} %get-tuple-element.30), channel_id=1, source_target_pairs={{0,2},{2,0},{1,3},{3,1},{4,6},{6,4},{5,7},{7,5},{8,10},{10,8},{9,1... | collective-permute-start | bytes 147464 | tf_op jit(solution)/shard_map/ppermute | solution.py:45
  14.5 2.5 %collective-permute-start.5 = (bf16[192,128]{1,0:T(8,128)(2,1)S(1)}, bf16[192,128]{1,0:T(8,128)(2,1)S(1)}, u32[]{:S(2)}, u32[]{:S(2)}) collective-permute-start(bf16[192,128]{1,0:T(8,128)(2,1)S(1)} %get-tuple-element.31), channel_id=1, source_target_pairs={{2,4},{4,2},{3,5},{5,3},{0,1},{1,0},{6,7},{7,6},{10,12},{12,10},{1... | collective-permute-start | bytes 147464 | tf_op jit(solution)/shard_map/ppermute | solution.py:46
  19.0 1.5 %collective-permute-start.8 = (bf16[32,512]{1,0:T(8,128)(2,1)S(1)}, bf16[32,512]{1,0:T(8,128)(2,1)S(1)}, u32[]{:S(2)}, u32[]{:S(2)}) collective-permute-start(bf16[32,512]{1,0:T(8,128)(2,1)S(1)} %bitcast.4), channel_id=1, source_target_pairs={{0,1},{1,0},{2,3},{3,2},{4,5},{5,4},{6,7},{7,6},{8,9},{9,8},{10,11... | collective-permute-start | bytes 98312 | tf_op jit(solution)/shard_map/ppermute | solution.py:566

commit v9 on v6

--- a/solution.py
+++ b/solution.py
@@ -93,10 +93,10 @@
 
 
 def load_kernel(*refs):
-    count = 6
-    sources, targets = refs[:count], refs[count + 4:2 * count + 4]
-    ma_ref, mb_ref, sa_ref, sb_ref = refs[count:count + 4]
-    sem = refs[2 * count + 4]
+    count, made = 6, 6
+    sources, targets = refs[:count], refs[count + made:2 * count + made]
+    ma_ref, mb_ref, sa_ref, sb_ref, ra_ref, rb_ref = refs[count:count + made]
+    sem = refs[2 * count + made]
     copies = [pltpu.make_async_copy(s, t, sem.at[i]) for i, (s, t) in enumerate(zip(sources, targets))]
     for copy in copies:
         copy.start()
@@ -121,7 +121,9 @@
             for t, tile in enumerate(tiles[1:-1]):
                 main[p, t + 1] = tile
             small[p * HALO:(p + 1) * HALO, :] = jnp.where(lane < MID, tiles[0], tiles[-1])
-    for copy in copies[2:]:
+    copies[2].wait()
+    pack_edges(x_ref, targets[2], ra_ref, rb_ref)
+    for copy in copies[3:]:
         copy.wait()
 
 
@@ -135,7 +137,7 @@
     ends[1][place, :] = jnp.where(even, left, right)
 
 
-def near_kernel(x_ref, ridx_ref, ra_ref, rb_ref):
+def pack_edges(x_ref, ridx_ref, ra_ref, rb_ref):
     planes, rows, cols = x_ref.shape
     freqs = planes // 2
     ends = (ra_ref, rb_ref)
@@ -487,17 +489,16 @@
     small = ((planes * HALO + IDX_ROWS, LANES), BF)
     inputs = (wave.reshape(planes, rows, cols), src_index, rec_index, jnp.transpose(tap_table, (0, 3, 2, 1)), offset_bin, bin_weight)
     inputs = tuple(pltpu.with_memory_space_constraint(a, pltpu.HBM) for a in inputs)
-    ma, mb, sa, sb, x, src_index, rec_index, tap_table, offset_bin, bin_weight = local_call(
+    near = ((freqs * rows + IDX_ROWS, LANES), BF)
+    ma, mb, sa, sb, ra, rb, x, src_index, rec_index, tap_table, offset_bin, bin_weight = local_call(
         load_kernel,
-        [main, main, small, small] + [(a.shape, a.dtype) for a in inputs],
+        [main, main, small, small, near, near] + [(a.shape, a.dtype) for a in inputs],
         [pltpu.SemaphoreType.DMA((len(inputs),))],
         moved=1 << 20,
         in_specs=[pl.BlockSpec(memory_space=pltpu.HBM)] * len(inputs),
     )(*inputs)
     sa, sb = swaps(sa, sb, "src")
     ma, mb = swaps(ma, mb, "src")
-    near = ((freqs * rows + IDX_ROWS, LANES), BF)
-    ra, rb = local_call(near_kernel, [near, near], moved=1 << 16)(x, rec_index)
     ra, rb = swaps(ra, rb, "rec")
     edge = ((freqs * 2 * HALO, LANES), BF)
     ea, eb = local_call(edge_kernel, [edge, edge], moved=1 << 16)(sa, sb)

time: 20.6 us -> 20.5 us (level)
    pallas_call x2 -> x1, Pallas kernels: 1.19 us -> 1.17 us  [migrate(): local_call(load_kernel, [main, main, small, small, near, near] + [(a.shap...]
where the time goes in v9:
time: 20.5 us; the launch traced here: 20.3 us
  starting transfers between devices  11.5 us (56%)
  Pallas kernels  7.51 us (37%)
  between operations  0.7 us (3%)
  other arithmetic  0.64 us (3%)
    ppermute x4, starting transfers between devices, swaps(): a = lax.ppermute(a, (axis, 'freq'), pairs_of(axis, 0))  10.4 us
    pallas_call x1, Pallas kernels, migrate(): local_call(own_kernel, [((DEPTHS, blocks, freqs, 2, WROWS, LANES), BF), (...  2.22 us
    pallas_call x1, Pallas kernels, migrate(): local_call(image_kernel, [((max(count - 1, 1), share, cols), BF), ((share...  1.92 us
    pallas_call x1, Pallas kernels, migrate(): local_call(load_kernel, [main, main, small, small, near, near] + [(a.shap...  1.17 us
    pallas_call x1, Pallas kernels, migrate(): local_call(final_kernel, [((planes, rows, cols), BF)], flops=1 << 28, mov...  1.13 us
    pallas_call x1, Pallas kernels, migrate(): local_call(source_kernel, [((freqs, rows, 2 * LANES), BF), ((freqs, rows,...  0.96 us
    ppermute x4, starting transfers between devices, swaps(): b = lax.ppermute(b, (axis, 'freq'), pairs_of(axis, 1))  0.74 us
    mul x1, other arithmetic, migrate(): return (final.reshape(wave.shape), total * scale)  0.64 us
  transfers between devices with their start and end apart: 9, of which 0 were waited for; matrix products, arithmetic and copies ran while one was open for 0% of the time, Pallas kernels for 22%

profile of v9, /device:TPU:0, one launch (start us, length us, event | category | flops | bytes accessed | tf_op | source)
XLA Modules:
  0.0 20.3 jit_solution(7021466227130260645)
XLA Ops:
  0.6 1.2 %shard_map.77 = (bf16[4,3,48,128]{3,2,1,0:T(8,128)(2,1)S(1)}, bf16[4,3,48,128]{3,2,1,0:T(8,128)(2,1)S(1)}, bf16[208,128]{1,0:T(8,128)(2,1)S(1)}, bf16[208,128]{1...) custom-call(bf16[4,64,512]{2,1,0:T(8,128)(2,1)} %bitcast.5, ...), custom_call_target="tpu_custom_call" | custom-call | bytes 1048576 | tf_op jit(solution)/shard_map/pallas_call | solution.py:493
  1.8 3.0 %collective-permute-start.2 = (bf16[208,128]{1,0:T(8,128)(2,1)S(1)}, bf16[208,128]{1,0:T(8,128)(2,1)S(1)}, u32[]{:S(2)}, u32[]{:S(2)}) collective-permute-start(bf16[208,128]{1,0:T(8,128)(2,1)S(1)} %get-tuple-element.28), channel_id=1, source_target_pairs={{0,8},{8,0},{1,9},{9,1},{16,24},{24,16},{17,25},{25,17},{2,10},{10... | collective-permute-start | bytes 159752 | tf_op jit(solution)/shard_map/ppermute | solution.py:45
  4.8 0.0 collective-permute-start.3
  4.8 1.6 %collective-permute-start.6 = (bf16[144,128]{1,0:T(8,128)(2,1)S(1)}, bf16[144,128]{1,0:T(8,128)(2,1)S(1)}, u32[]{:S(2)}, u32[]{:S(2)}) collective-permute-start(bf16[144,128]{1,0:T(8,128)(2,1)S(1)} %get-tuple-element.33), channel_id=1, source_target_pairs={{0,2},{2,0},{1,3},{3,1},{4,6},{6,4},{5,7},{7,5},{8,10},{10,8},{9,1... | collective-permute-start | bytes 110600 | tf_op jit(solution)/shard_map/ppermute | solution.py:45
  6.4 0.2 %collective-permute-start.7 = (bf16[144,128]{1,0:T(8,128)(2,1)S(1)}, bf16[144,128]{1,0:T(8,128)(2,1)S(1)}, u32[]{:S(2)}, u32[]{:S(2)}) collective-permute-start(bf16[144,128]{1,0:T(8,128)(2,1)S(1)} %get-tuple-element.34), channel_id=1, source_target_pairs={{2,4},{4,2},{3,5},{5,3},{0,1},{1,0},{6,7},{7,6},{10,12},{12,10},{1... | collective-permute-start | bytes 110600 | tf_op jit(solution)/shard_map/ppermute | solution.py:46
  6.7 2.8 %collective-permute-start = (bf16[4,3,48,128]{3,2,1,0:T(8,128)(2,1)S(1)}, bf16[4,3,48,128]{3,2,1,0:T(8,128)(2,1)S(1)}, u32[]{:S(2)}, u32[]{:S(2)}) collective-permute-start(bf16[4,3,48,128]{3,2,1,0:T(8,128)(2,1)S(1)} %get-tuple-element.26), channel_id=1, source_target_pairs={{0,8},{8,0},{1,9},{9,1},{16,24},{24,16},{17,25},{25,17},{2,10},{10... | collective-permute-start | bytes 442376 | tf_op jit(solution)/shard_map/ppermute | solution.py:45
  9.4 0.0 collective-permute-done.2.sa_ref
  9.4 0.2 %collective-permute-start.1 = (bf16[4,3,48,128]{3,2,1,0:T(8,128)(2,1)S(1)}, bf16[4,3,48,128]{3,2,1,0:T(8,128)(2,1)S(1)}, u32[]{:S(2)}, u32[]{:S(2)}) collective-permute-start(bf16[4,3,48,128]{3,2,1,0:T(8,128)(2,1)S(1)} %get-tuple-element.27), channel_id=1, source_target_pairs={{8,16},{16,8},{9,17},{17,9},{0,1},{1,0},{24,25},{25,24},{10,18},{1... | collective-permute-start | bytes 442376 | tf_op jit(solution)/shard_map/ppermute | solution.py:46
  9.6 0.0 collective-permute-done.3.sb_ref
  9.6 0.1 shard_map.78
  9.8 3.0 %collective-permute-start.4 = (bf16[192,128]{1,0:T(8,128)(2,1)S(1)}, bf16[192,128]{1,0:T(8,128)(2,1)S(1)}, u32[]{:S(2)}, u32[]{:S(2)}) collective-permute-start(bf16[192,128]{1,0:T(8,128)(2,1)S(1)} %get-tuple-element.30), channel_id=1, source_target_pairs={{0,2},{2,0},{1,3},{3,1},{4,6},{6,4},{5,7},{7,5},{8,10},{10,8},{9,1... | collective-permute-start | bytes 147464 | tf_op jit(solution)/shard_map/ppermute | solution.py:45
  12.8 1.0 %shard_map.79 = (bf16[2,64,256]{2,1,0:T(8,128)(2,1)S(1)}, bf16[2,64,256]{2,1,0:T(8,128)(2,1)S(1)}, bf16[2,2,128,256]{3,2,1,0:T(8,128)(2,1)S(1)}, f32[3,4,64,128]{3,2,1,0:T(8,128)S(1)}, bf16[512,64]{1,0:T(8,128)(2,1)S(1)}) custom-call(bf16[208,128]{1,0:T(8,128)(2,1)S(1)} %collective-permute-done.2.sa_ref, bf16[208,128]{1,0:T(8,128)(2,1)S(1)} %collective-permute-done.3.sb_ref, ...), custom_call_target="tpu_custom_call" | custom-call | flops 268435456 | bytes 2097152 | tf_op jit(solution)/shard_map/pallas_call | solution.py:507
  13.7 0.0 collective-permute-done.6.ra_ref
  13.7 0.3 %collective-permute-start.5 = (bf16[192,128]{1,0:T(8,128)(2,1)S(1)}, bf16[192,128]{1,0:T(8,128)(2,1)S(1)}, u32[]{:S(2)}, u32[]{:S(2)}) collective-permute-start(bf16[192,128]{1,0:T(8,128)(2,1)S(1)} %get-tuple-element.31), channel_id=1, source_target_pairs={{2,4},{4,2},{3,5},{5,3},{0,1},{1,0},{6,7},{7,6},{10,12},{12,10},{1... | collective-permute-start | bytes 147464 | tf_op jit(solution)/shard_map/ppermute | solution.py:46
  14.0 0.0 collective-permute-done.7.rb_ref
  14.0 2.2 %shard_map.80 = (bf16[3,6,2,2,224,128]{5,4,3,2,1,0:T(8,128)(2,1)S(1)}, bf16[3,4,6,64,128]{4,3,2,1,0:T(8,128)(2,1)S(1)}) custom-call(bf16[4,64,512]{2,1,0:T(8,128)(2,1)S(1)} %get-tuple-element.32.x_ref, bf16[144,128]{1,0:T(8,128)(2,1)S(1)} %collective-permute-done.6.ra_ref, bf16[144,128]{1,0:T(8,128)(2,1)S(1)} %collective-permute-done.7.rb_ref, ...), custom_call_target="tpu_custom_call" | custom-call | flops 2147483648 | bytes 5242880 | tf_op jit(solution)/shard_map/pallas_call | solution.py:520
  16.2 0.0 collective-permute-done.4.ra_ref
  16.2 0.0 collective-permute-done.5.rb_ref
  16.3 0.0 collective-permute-done.ma_ref
  16.3 0.0 collective-permute-done.1.mb_ref
  16.3 1.9 %shard_map.81 = (bf16[1,32,512]{2,1,0:T(8,128)(2,1)S(1)}, f32[32,512]{1,0:T(8,128)S(1)}, bf16[4,6,160,128]{3,2,1,0:T(8,128)(2,1)S(1)}) custom-call(bf16[4,3,48,128]{3,2,1,0:T(8,128)(2,1)S(1)} %collective-permute-done.ma_ref, bf16[4,3,48,128]{3,2,1,0:T(8,128)(2,1)S(1)} %collective-permute-done.1.mb_ref, bf16[208,128]{1,0:T(8,128)(2,1)S(1)} %collective-permute-done.2.sa_ref, ...), custom_call_target="tpu_custom_call" | custom-call | flops 2147483648 | bytes 8388608 | tf_op jit(solution)/shard_map/pallas_call | solution.py:530
  18.2 0.4 %collective-permute-start.8 = (bf16[32,512]{1,0:T(8,128)(2,1)S(1)}, bf16[32,512]{1,0:T(8,128)(2,1)S(1)}, u32[]{:S(2)}, u32[]{:S(2)}) collective-permute-start(bf16[32,512]{1,0:T(8,128)(2,1)S(1)} %bitcast.4), channel_id=1, source_target_pairs={{0,1},{1,0},{2,3},{3,2},{4,5},{5,4},{6,7},{7,6},{8,9},{9,8},{10,11... | collective-permute-start | bytes 98312 | tf_op jit(solution)/shard_map/ppermute | solution.py:544
  18.6 1.1 %shard_map.82 = bf16[4,64,512]{2,1,0:T(8,128)(2,1)} custom-call(bf16[4,6,160,128]{3,2,1,0:T(8,128)(2,1)S(1)} %get-tuple-element.47.deep_ref, bf16[2,2,128,256]{3,2,1,0:T(8,128)(2,1)S(1)} %get-tuple-element.45.far_ref), custom_call_target="tpu_custom_call" | custom-call | flops 268435456 | bytes 1048576 | tf_op jit(solution)/shard_map/pallas_call | solution.py:546
  19.7 0.0 collective-permute-done.8
  19.7 0.6 %add_multiply_fusion = f32[32,512]{1,0:T(8,128)} fusion(f32[32,512]{1,0:T(8,128)S(1)} %get-tuple-element.48, bf16[32,512]{1,0:T(8,128)(2,1)S(1)} %collective-permute-done.8), kind=kLoop, calls=%fused_computation | loop fusion | flops 49152 | bytes 163840 | tf_op jit(solution)/shard_map/mul | solution.py:548
Async XLA Ops:
  1.8 7.6 %collective-permute-start.2 = (bf16[208,128]{1,0:T(8,128)(2,1)S(1)}, bf16[208,128]{1,0:T(8,128)(2,1)S(1)}, u32[]{:S(2)}, u32[]{:S(2)}) collective-permute-start(bf16[208,128]{1,0:T(8,128)(2,1)S(1)} %get-tuple-element.28), channel_id=1, source_target_pairs={{0,8},{8,0},{1,9},{9,1},{16,24},{24,16},{17,25},{25,17},{2,10},{10... | collective-permute-start | bytes 159752 | tf_op jit(solution)/shard_map/ppermute | solution.py:45
  4.8 4.8 %collective-permute-start.3 = (bf16[208,128]{1,0:T(8,128)(2,1)S(1)}, bf16[208,128]{1,0:T(8,128)(2,1)S(1)}, u32[]{:S(2)}, u32[]{:S(2)}) collective-permute-start(bf16[208,128]{1,0:T(8,128)(2,1)S(1)} %get-tuple-element.29), channel_id=1, source_target_pairs={{8,16},{16,8},{9,17},{17,9},{0,1},{1,0},{24,25},{25,24},{10,18},{1... | collective-permute-start | bytes 159752 | tf_op jit(solution)/shard_map/ppermute | solution.py:46
  4.8 8.9 %collective-permute-start.6 = (bf16[144,128]{1,0:T(8,128)(2,1)S(1)}, bf16[144,128]{1,0:T(8,128)(2,1)S(1)}, u32[]{:S(2)}, u32[]{:S(2)}) collective-permute-start(bf16[144,128]{1,0:T(8,128)(2,1)S(1)} %get-tuple-element.33), channel_id=1, source_target_pairs={{0,2},{2,0},{1,3},{3,1},{4,6},{6,4},{5,7},{7,5},{8,10},{10,8},{9,1... | collective-permute-start | bytes 110600 | tf_op jit(solution)/shard_map/ppermute | solution.py:45
  6.4 7.6 %collective-permute-start.7 = (bf16[144,128]{1,0:T(8,128)(2,1)S(1)}, bf16[144,128]{1,0:T(8,128)(2,1)S(1)}, u32[]{:S(2)}, u32[]{:S(2)}) collective-permute-start(bf16[144,128]{1,0:T(8,128)(2,1)S(1)} %get-tuple-element.34), channel_id=1, source_target_pairs={{2,4},{4,2},{3,5},{5,3},{0,1},{1,0},{6,7},{7,6},{10,12},{12,10},{1... | collective-permute-start | bytes 110600 | tf_op jit(solution)/shard_map/ppermute | solution.py:46
  6.7 9.6 %collective-permute-start = (bf16[4,3,48,128]{3,2,1,0:T(8,128)(2,1)S(1)}, bf16[4,3,48,128]{3,2,1,0:T(8,128)(2,1)S(1)}, u32[]{:S(2)}, u32[]{:S(2)}) collective-permute-start(bf16[4,3,48,128]{3,2,1,0:T(8,128)(2,1)S(1)} %get-tuple-element.26), channel_id=1, source_target_pairs={{0,8},{8,0},{1,9},{9,1},{16,24},{24,16},{17,25},{25,17},{2,10},{10... | collective-permute-start | bytes 442376 | tf_op jit(solution)/shard_map/ppermute | solution.py:45
  9.4 6.9 %collective-permute-start.1 = (bf16[4,3,48,128]{3,2,1,0:T(8,128)(2,1)S(1)}, bf16[4,3,48,128]{3,2,1,0:T(8,128)(2,1)S(1)}, u32[]{:S(2)}, u32[]{:S(2)}) collective-permute-start(bf16[4,3,48,128]{3,2,1,0:T(8,128)(2,1)S(1)} %get-tuple-element.27), channel_id=1, source_target_pairs={{8,16},{16,8},{9,17},{17,9},{0,1},{1,0},{24,25},{25,24},{10,18},{1... | collective-permute-start | bytes 442376 | tf_op jit(solution)/shard_map/ppermute | solution.py:46
  9.8 6.5 %collective-permute-start.4 = (bf16[192,128]{1,0:T(8,128)(2,1)S(1)}, bf16[192,128]{1,0:T(8,128)(2,1)S(1)}, u32[]{:S(2)}, u32[]{:S(2)}) collective-permute-start(bf16[192,128]{1,0:T(8,128)(2,1)S(1)} %get-tuple-element.30), channel_id=1, source_target_pairs={{0,2},{2,0},{1,3},{3,1},{4,6},{6,4},{5,7},{7,5},{8,10},{10,8},{9,1... | collective-permute-start | bytes 147464 | tf_op jit(solution)/shard_map/ppermute | solution.py:45
  13.7 2.5 %collective-permute-start.5 = (bf16[192,128]{1,0:T(8,128)(2,1)S(1)}, bf16[192,128]{1,0:T(8,128)(2,1)S(1)}, u32[]{:S(2)}, u32[]{:S(2)}) collective-permute-start(bf16[192,128]{1,0:T(8,128)(2,1)S(1)} %get-tuple-element.31), channel_id=1, source_target_pairs={{2,4},{4,2},{3,5},{5,3},{0,1},{1,0},{6,7},{7,6},{10,12},{12,10},{1... | collective-permute-start | bytes 147464 | tf_op jit(solution)/shard_map/ppermute | solution.py:46
  18.2 1.5 %collective-permute-start.8 = (bf16[32,512]{1,0:T(8,128)(2,1)S(1)}, bf16[32,512]{1,0:T(8,128)(2,1)S(1)}, u32[]{:S(2)}, u32[]{:S(2)}) collective-permute-start(bf16[32,512]{1,0:T(8,128)(2,1)S(1)} %bitcast.4), channel_id=1, source_target_pairs={{0,1},{1,0},{2,3},{3,2},{4,5},{5,4},{6,7},{7,6},{8,9},{9,8},{10,11... | collective-permute-start | bytes 98312 | tf_op jit(solution)/shard_map/ppermute | solution.py:544

commit v10 on v6

--- a/solution.py
+++ b/solution.py
@@ -181,8 +181,11 @@
     return dot(hot[0] if len(hot) == 1 else jnp.concatenate(hot, axis=1), table, TT)
 
 
-def skew(taps):
-    return pltpu.roll(taps, 0, 1, stride=1, stride_axis=0)
+def skew(taps, f, part):
+    tile = taps[:, f * LANES:(f + 1) * LANES]
+    low = lane_of(tile.shape) < MID
+    tile = jnp.where(low, 0.0, tile) if part else jnp.where(low, tile, 0.0)
+    return pltpu.roll(tile, part * MID, 1, stride=1, stride_axis=0)
 
 
 def source_kernel(
@@ -194,8 +197,8 @@
     tiles = cols // LANES
     for f in range(freqs):
         for part in range(2):
-            at = (2 * f + part) * LANES
-            table_ref[at:at + LANES, :] = jnp.zeros((LANES, table_ref.shape[1]), BF)
+            at = f * LANES + part * MID
+            table_ref[at:at + MID, :] = jnp.zeros((MID, table_ref.shape[1]), BF)
             table_ref[at:at + TAPS, :] = taps_ref[part, :, f, :].astype(BF)
     table = table_ref[...]
     entries = table.shape[1]
@@ -218,7 +221,7 @@
         taps = taps_of([roll(index, -z * HALF)[z:z + 1]], table, entries)
         found = []
         for part in range(2 * freqs):
-            skewed = skew(taps[:, part * LANES:(part + 1) * LANES])
+            skewed = skew(taps, part // 2, part % 2)
             found.append((jnp.where(lane >= out, skewed, 0.0), jnp.where(lane < out, skewed, 0.0)))
         ops.append(found)
     narrow = lane_of((rows, LANES))
@@ -336,16 +339,17 @@
             index.append(join(pieces)[z:z + 1])
         taps = taps_of(index, table, entries)
         for b in range(blocks):
-            at = slice(b * OUT, (b + 1) * OUT)
+            valid = min(OUT, cols + 2 * before - b * OUT)
+            at = slice(b * OUT, b * OUT + valid)
             for f in range(freqs):
-                re, im = (
-                    skew(taps[at, part * LANES:(part + 1) * LANES]) for part in (2 * f, 2 * f + 1)
-                )
+                re, im = (skew(taps[at], f, part) for part in range(2))
                 minus, re, im = (-im).astype(BF), re.astype(BF), im.astype(BF)
                 for half, (top, low) in enumerate(((re, im), (minus, re))):
-                    w_ref[z, b, f, half, 0:OUT, :] = top
-                    w_ref[z, b, f, half, OUT:LANES, :] = jnp.zeros((LANES - OUT, LANES), BF)
-                    w_ref[z, b, f, half, LANES:, :] = low
+                    w_ref[z, b, f, half, 0:valid, :] = top
+                    w_ref[z, b, f, half, valid:LANES, :] = jnp.zeros((LANES - valid, LANES), BF)
+                    w_ref[z, b, f, half, LANES:LANES + valid, :] = low
+                    if valid < OUT:
+                        w_ref[z, b, f, half, LANES + valid:, :] = jnp.zeros((OUT - valid, LANES), BF)
     first = []
     for p in range(planes):
         part, f = divmod(p, freqs)
@@ -510,7 +514,7 @@
             ((freqs, rows, 2 * LANES), BF),
             ((freqs, 2, 2 * rows, 2 * LANES), BF),
             ((DEPTHS, tiles, rows, LANES), F32),
-            ((planes * LANES, entries), BF),
+            ((freqs * LANES, entries), BF),
         ],
         [((8, LANES), F32), ((8, LANES), F32)],
         flops=1 << 28,

time: 20.6 us -> 20.3 us (0.985)
  Pallas kernels: 7.52 us -> 7.29 us
    pallas_call x1, Pallas kernels: 2.21 us -> 1.95 us  [migrate(): local_call(own_kernel, [((DEPTHS, blocks, freqs, 2, WROWS, LANES), BF), (...]
  transfers between devices with their start and end apart: 9 -> 9, of which waited for: 0 -> 0; matrix products, arithmetic and copies ran while one was open for 0% -> 0% of each run, Pallas kernels for 22% -> 21%
where the time goes in v10:
time: 20.3 us; the launch traced here: 20.2 us
  starting transfers between devices  11.5 us (57%)
  Pallas kernels  7.29 us (36%)
  between operations  0.72 us (4%)
  other arithmetic  0.64 us (3%)
    ppermute x4, starting transfers between devices, swaps(): a = lax.ppermute(a, (axis, 'freq'), pairs_of(axis, 0))  10.4 us
    pallas_call x1, Pallas kernels, migrate(): local_call(own_kernel, [((DEPTHS, blocks, freqs, 2, WROWS, LANES), BF), (...  1.95 us
    pallas_call x1, Pallas kernels, migrate(): local_call(image_kernel, [((max(count - 1, 1), share, cols), BF), ((share...  1.92 us
    pallas_call x1, Pallas kernels, migrate(): local_call(final_kernel, [((planes, rows, cols), BF)], flops=1 << 28, mov...  1.13 us
    pallas_call x1, Pallas kernels, migrate(): local_call(load_kernel, [main, main, small, small] + [(a.shape, a.dtype)...  1.11 us
    pallas_call x1, Pallas kernels, migrate(): local_call(source_kernel, [((freqs, rows, 2 * LANES), BF), ((freqs, rows,...  0.99 us
    ppermute x4, starting transfers between devices, swaps(): b = lax.ppermute(b, (axis, 'freq'), pairs_of(axis, 1))  0.75 us
    mul x1, other arithmetic, migrate(): return (final.reshape(wave.shape), total * scale)  0.64 us
  transfers between devices with their start and end apart: 9, of which 0 were waited for; matrix products, arithmetic and copies ran while one was open for 0% of the time, Pallas kernels for 21%

profile of v10, /device:TPU:0, one launch (start us, length us, event | category | flops | bytes accessed | tf_op | source)
XLA Modules:
  0.0 20.2 jit_solution(9133206017723628085)
XLA Ops:
  0.6 1.1 %shard_map.77 = (bf16[4,3,48,128]{3,2,1,0:T(8,128)(2,1)S(1)}, bf16[4,3,48,128]{3,2,1,0:T(8,128)(2,1)S(1)}, bf16[208,128]{1,0:T(8,128)(2,1)S(1)}, bf16[208,128]{1...) custom-call(bf16[4,64,512]{2,1,0:T(8,128)(2,1)} %bitcast.5, ...), custom_call_target="tpu_custom_call" | custom-call | bytes 1048576 | tf_op jit(solution)/shard_map/pallas_call | solution.py:494
  1.7 3.0 %collective-permute-start.2 = (bf16[208,128]{1,0:T(8,128)(2,1)S(1)}, bf16[208,128]{1,0:T(8,128)(2,1)S(1)}, u32[]{:S(2)}, u32[]{:S(2)}) collective-permute-start(bf16[208,128]{1,0:T(8,128)(2,1)S(1)} %get-tuple-element.28), channel_id=1, source_target_pairs={{0,8},{8,0},{1,9},{9,1},{16,24},{24,16},{17,25},{25,17},{2,10},{10... | collective-permute-start | bytes 159752 | tf_op jit(solution)/shard_map/ppermute | solution.py:45
  4.8 0.0 collective-permute-start.3
  4.8 0.1 shard_map.79
  4.9 1.6 %collective-permute-start.6 = (bf16[144,128]{1,0:T(8,128)(2,1)S(1)}, bf16[144,128]{1,0:T(8,128)(2,1)S(1)}, u32[]{:S(2)}, u32[]{:S(2)}) collective-permute-start(bf16[144,128]{1,0:T(8,128)(2,1)S(1)} %get-tuple-element.34), channel_id=1, source_target_pairs={{0,2},{2,0},{1,3},{3,1},{4,6},{6,4},{5,7},{7,5},{8,10},{10,8},{9,1... | collective-permute-start | bytes 110600 | tf_op jit(solution)/shard_map/ppermute | solution.py:45
  6.5 0.2 %collective-permute-start.7 = (bf16[144,128]{1,0:T(8,128)(2,1)S(1)}, bf16[144,128]{1,0:T(8,128)(2,1)S(1)}, u32[]{:S(2)}, u32[]{:S(2)}) collective-permute-start(bf16[144,128]{1,0:T(8,128)(2,1)S(1)} %get-tuple-element.35), channel_id=1, source_target_pairs={{2,4},{4,2},{3,5},{5,3},{0,1},{1,0},{6,7},{7,6},{10,12},{12,10},{1... | collective-permute-start | bytes 110600 | tf_op jit(solution)/shard_map/ppermute | solution.py:46
  6.7 2.8 %collective-permute-start = (bf16[4,3,48,128]{3,2,1,0:T(8,128)(2,1)S(1)}, bf16[4,3,48,128]{3,2,1,0:T(8,128)(2,1)S(1)}, u32[]{:S(2)}, u32[]{:S(2)}) collective-permute-start(bf16[4,3,48,128]{3,2,1,0:T(8,128)(2,1)S(1)} %get-tuple-element.26), channel_id=1, source_target_pairs={{0,8},{8,0},{1,9},{9,1},{16,24},{24,16},{17,25},{25,17},{2,10},{10... | collective-permute-start | bytes 442376 | tf_op jit(solution)/shard_map/ppermute | solution.py:45
  9.5 0.0 collective-permute-done.2.sa_ref
  9.5 0.2 %collective-permute-start.1 = (bf16[4,3,48,128]{3,2,1,0:T(8,128)(2,1)S(1)}, bf16[4,3,48,128]{3,2,1,0:T(8,128)(2,1)S(1)}, u32[]{:S(2)}, u32[]{:S(2)}) collective-permute-start(bf16[4,3,48,128]{3,2,1,0:T(8,128)(2,1)S(1)} %get-tuple-element.27), channel_id=1, source_target_pairs={{8,16},{16,8},{9,17},{17,9},{0,1},{1,0},{24,25},{25,24},{10,18},{1... | collective-permute-start | bytes 442376 | tf_op jit(solution)/shard_map/ppermute | solution.py:46
  9.7 0.0 collective-permute-done.3.sb_ref
  9.7 0.1 shard_map.78
  9.8 3.0 %collective-permute-start.4 = (bf16[192,128]{1,0:T(8,128)(2,1)S(1)}, bf16[192,128]{1,0:T(8,128)(2,1)S(1)}, u32[]{:S(2)}, u32[]{:S(2)}) collective-permute-start(bf16[192,128]{1,0:T(8,128)(2,1)S(1)} %get-tuple-element.30), channel_id=1, source_target_pairs={{0,2},{2,0},{1,3},{3,1},{4,6},{6,4},{5,7},{7,5},{8,10},{10,8},{9,1... | collective-permute-start | bytes 147464 | tf_op jit(solution)/shard_map/ppermute | solution.py:45
  12.8 1.0 %shard_map.80 = (bf16[2,64,256]{2,1,0:T(8,128)(2,1)S(1)}, bf16[2,64,256]{2,1,0:T(8,128)(2,1)S(1)}, bf16[2,2,128,256]{3,2,1,0:T(8,128)(2,1)S(1)}, f32[3,4,64,128]{3,2,1,0:T(8,128)S(1)}, bf16[256,64]{1,0:T(8,128)(2,1)S(1)}) custom-call(bf16[208,128]{1,0:T(8,128)(2,1)S(1)} %collective-permute-done.2.sa_ref, bf16[208,128]{1,0:T(8,128)(2,1)S(1)} %collective-permute-done.3.sb_ref, ...), custom_call_target="tpu_custom_call" | custom-call | flops 268435456 | bytes 2097152 | tf_op jit(solution)/shard_map/pallas_call | solution.py:510
  13.8 0.0 collective-permute-done.6.ra_ref
  13.9 0.3 %collective-permute-start.5 = (bf16[192,128]{1,0:T(8,128)(2,1)S(1)}, bf16[192,128]{1,0:T(8,128)(2,1)S(1)}, u32[]{:S(2)}, u32[]{:S(2)}) collective-permute-start(bf16[192,128]{1,0:T(8,128)(2,1)S(1)} %get-tuple-element.31), channel_id=1, source_target_pairs={{2,4},{4,2},{3,5},{5,3},{0,1},{1,0},{6,7},{7,6},{10,12},{12,10},{1... | collective-permute-start | bytes 147464 | tf_op jit(solution)/shard_map/ppermute | solution.py:46
  14.1 0.0 collective-permute-done.7.rb_ref
  14.1 1.9 %shard_map.81 = (bf16[3,6,2,2,224,128]{5,4,3,2,1,0:T(8,128)(2,1)S(1)}, bf16[3,4,6,64,128]{4,3,2,1,0:T(8,128)(2,1)S(1)}) custom-call(bf16[4,64,512]{2,1,0:T(8,128)(2,1)S(1)} %get-tuple-element.32.x_ref, bf16[144,128]{1,0:T(8,128)(2,1)S(1)} %collective-permute-done.6.ra_ref, bf16[144,128]{1,0:T(8,128)(2,1)S(1)} %collective-permute-done.7.rb_ref, ...), custom_call_target="tpu_custom_call" | custom-call | flops 2147483648 | bytes 5242880 | tf_op jit(solution)/shard_map/pallas_call | solution.py:523
  16.1 0.0 collective-permute-done.4.ra_ref
  16.1 0.0 collective-permute-done.5.rb_ref
  16.1 0.0 collective-permute-done.ma_ref
  16.1 0.0 collective-permute-done.1.mb_ref
  16.1 1.9 %shard_map.82 = (bf16[1,32,512]{2,1,0:T(8,128)(2,1)S(1)}, f32[32,512]{1,0:T(8,128)S(1)}, bf16[4,6,160,128]{3,2,1,0:T(8,128)(2,1)S(1)}) custom-call(bf16[4,3,48,128]{3,2,1,0:T(8,128)(2,1)S(1)} %collective-permute-done.ma_ref, bf16[4,3,48,128]{3,2,1,0:T(8,128)(2,1)S(1)} %collective-permute-done.1.mb_ref, bf16[208,128]{1,0:T(8,128)(2,1)S(1)} %collective-permute-done.2.sa_ref, ...), custom_call_target="tpu_custom_call" | custom-call | flops 2147483648 | bytes 8388608 | tf_op jit(solution)/shard_map/pallas_call | solution.py:533
  18.1 0.4 %collective-permute-start.8 = (bf16[32,512]{1,0:T(8,128)(2,1)S(1)}, bf16[32,512]{1,0:T(8,128)(2,1)S(1)}, u32[]{:S(2)}, u32[]{:S(2)}) collective-permute-start(bf16[32,512]{1,0:T(8,128)(2,1)S(1)} %bitcast.4), channel_id=1, source_target_pairs={{0,1},{1,0},{2,3},{3,2},{4,5},{5,4},{6,7},{7,6},{8,9},{9,8},{10,11... | collective-permute-start | bytes 98312 | tf_op jit(solution)/shard_map/ppermute | solution.py:547
  18.4 1.1 %shard_map.83 = bf16[4,64,512]{2,1,0:T(8,128)(2,1)} custom-call(bf16[4,6,160,128]{3,2,1,0:T(8,128)(2,1)S(1)} %get-tuple-element.47.deep_ref, bf16[2,2,128,256]{3,2,1,0:T(8,128)(2,1)S(1)} %get-tuple-element.45.far_ref), custom_call_target="tpu_custom_call" | custom-call | flops 268435456 | bytes 1048576 | tf_op jit(solution)/shard_map/pallas_call | solution.py:549
  19.6 0.0 collective-permute-done.8
  19.6 0.6 %add_multiply_fusion = f32[32,512]{1,0:T(8,128)} fusion(f32[32,512]{1,0:T(8,128)S(1)} %get-tuple-element.48, bf16[32,512]{1,0:T(8,128)(2,1)S(1)} %collective-permute-done.8), kind=kLoop, calls=%fused_computation | loop fusion | flops 49152 | bytes 163840 | tf_op jit(solution)/shard_map/mul | solution.py:551
Async XLA Ops:
  1.7 7.8 %collective-permute-start.2 = (bf16[208,128]{1,0:T(8,128)(2,1)S(1)}, bf16[208,128]{1,0:T(8,128)(2,1)S(1)}, u32[]{:S(2)}, u32[]{:S(2)}) collective-permute-start(bf16[208,128]{1,0:T(8,128)(2,1)S(1)} %get-tuple-element.28), channel_id=1, source_target_pairs={{0,8},{8,0},{1,9},{9,1},{16,24},{24,16},{17,25},{25,17},{2,10},{10... | collective-permute-start | bytes 159752 | tf_op jit(solution)/shard_map/ppermute | solution.py:45
  4.8 5.0 %collective-permute-start.3 = (bf16[208,128]{1,0:T(8,128)(2,1)S(1)}, bf16[208,128]{1,0:T(8,128)(2,1)S(1)}, u32[]{:S(2)}, u32[]{:S(2)}) collective-permute-start(bf16[208,128]{1,0:T(8,128)(2,1)S(1)} %get-tuple-element.29), channel_id=1, source_target_pairs={{8,16},{16,8},{9,17},{17,9},{0,1},{1,0},{24,25},{25,24},{10,18},{1... | collective-permute-start | bytes 159752 | tf_op jit(solution)/shard_map/ppermute | solution.py:46
  4.9 9.0 %collective-permute-start.6 = (bf16[144,128]{1,0:T(8,128)(2,1)S(1)}, bf16[144,128]{1,0:T(8,128)(2,1)S(1)}, u32[]{:S(2)}, u32[]{:S(2)}) collective-permute-start(bf16[144,128]{1,0:T(8,128)(2,1)S(1)} %get-tuple-element.34), channel_id=1, source_target_pairs={{0,2},{2,0},{1,3},{3,1},{4,6},{6,4},{5,7},{7,5},{8,10},{10,8},{9,1... | collective-permute-start | bytes 110600 | tf_op jit(solution)/shard_map/ppermute | solution.py:45
  6.5 7.6 %collective-permute-start.7 = (bf16[144,128]{1,0:T(8,128)(2,1)S(1)}, bf16[144,128]{1,0:T(8,128)(2,1)S(1)}, u32[]{:S(2)}, u32[]{:S(2)}) collective-permute-start(bf16[144,128]{1,0:T(8,128)(2,1)S(1)} %get-tuple-element.35), channel_id=1, source_target_pairs={{2,4},{4,2},{3,5},{5,3},{0,1},{1,0},{6,7},{7,6},{10,12},{12,10},{1... | collective-permute-start | bytes 110600 | tf_op jit(solution)/shard_map/ppermute | solution.py:46
  6.7 9.4 %collective-permute-start = (bf16[4,3,48,128]{3,2,1,0:T(8,128)(2,1)S(1)}, bf16[4,3,48,128]{3,2,1,0:T(8,128)(2,1)S(1)}, u32[]{:S(2)}, u32[]{:S(2)}) collective-permute-start(bf16[4,3,48,128]{3,2,1,0:T(8,128)(2,1)S(1)} %get-tuple-element.26), channel_id=1, source_target_pairs={{0,8},{8,0},{1,9},{9,1},{16,24},{24,16},{17,25},{25,17},{2,10},{10... | collective-permute-start | bytes 442376 | tf_op jit(solution)/shard_map/ppermute | solution.py:45
  9.5 6.6 %collective-permute-start.1 = (bf16[4,3,48,128]{3,2,1,0:T(8,128)(2,1)S(1)}, bf16[4,3,48,128]{3,2,1,0:T(8,128)(2,1)S(1)}, u32[]{:S(2)}, u32[]{:S(2)}) collective-permute-start(bf16[4,3,48,128]{3,2,1,0:T(8,128)(2,1)S(1)} %get-tuple-element.27), channel_id=1, source_target_pairs={{8,16},{16,8},{9,17},{17,9},{0,1},{1,0},{24,25},{25,24},{10,18},{1... | collective-permute-start | bytes 442376 | tf_op jit(solution)/shard_map/ppermute | solution.py:46
  9.8 6.3 %collective-permute-start.4 = (bf16[192,128]{1,0:T(8,128)(2,1)S(1)}, bf16[192,128]{1,0:T(8,128)(2,1)S(1)}, u32[]{:S(2)}, u32[]{:S(2)}) collective-permute-start(bf16[192,128]{1,0:T(8,128)(2,1)S(1)} %get-tuple-element.30), channel_id=1, source_target_pairs={{0,2},{2,0},{1,3},{3,1},{4,6},{6,4},{5,7},{7,5},{8,10},{10,8},{9,1... | collective-permute-start | bytes 147464 | tf_op jit(solution)/shard_map/ppermute | solution.py:45
  13.9 2.3 %collective-permute-start.5 = (bf16[192,128]{1,0:T(8,128)(2,1)S(1)}, bf16[192,128]{1,0:T(8,128)(2,1)S(1)}, u32[]{:S(2)}, u32[]{:S(2)}) collective-permute-start(bf16[192,128]{1,0:T(8,128)(2,1)S(1)} %get-tuple-element.31), channel_id=1, source_target_pairs={{2,4},{4,2},{3,5},{5,3},{0,1},{1,0},{6,7},{7,6},{10,12},{12,10},{1... | collective-permute-start | bytes 147464 | tf_op jit(solution)/shard_map/ppermute | solution.py:46
  18.1 1.5 %collective-permute-start.8 = (bf16[32,512]{1,0:T(8,128)(2,1)S(1)}, bf16[32,512]{1,0:T(8,128)(2,1)S(1)}, u32[]{:S(2)}, u32[]{:S(2)}) collective-permute-start(bf16[32,512]{1,0:T(8,128)(2,1)S(1)} %bitcast.4), channel_id=1, source_target_pairs={{0,1},{1,0},{2,3},{3,2},{4,5},{5,4},{6,7},{7,6},{8,9},{9,8},{10,11... | collective-permute-start | bytes 98312 | tf_op jit(solution)/shard_map/ppermute | solution.py:547
